TPU v7x, 128 devices: a whole 4x4x4 slice. The times are simulated.
128 devices in a mesh: level: 8 (over z, y_hi), leaf: 8 (over x, core), rhs: 2 (over y_lo).
Axes of the slice: x: 4, y: 4 (y_hi: 2, y_lo: 2; y = y_hi * 2 + y_lo), z: 4, core: 2. Of those that a mesh axis runs over, the one named last changes fastest.
Arguments:
- charges: float32 [64, 262144], P(None, ('level', 'leaf', 'rhs')), may hold values from -6 to 6
- cluster_order: int32 [262144], P(('level', 'leaf')), may hold values from 0 to 4095, as said below
- near_tiles: float32 [2048, 4, 128, 128], P(('level', 'leaf', 'rhs')), may hold values from -0.25 to 0.25
- near_index: int32 [2048, 4], P(('level', 'leaf', 'rhs')), may hold values from 0 to 31, as said below
- near_count: int32 [2048], P(('level', 'leaf', 'rhs')), may hold values from 1 to 4, as said below
- proj_basis: float32 [4, 262144, 256], P(None, ('level', 'leaf', 'rhs'))
- corr_basis: float32 [4, 256, 262144], P(None, None, ('level', 'leaf', 'rhs')), may hold values from -0.1875 to 0.1875
- coupling: float32 [64, 4, 2, 256, 256], P(('level', 'leaf'))
Outputs:
- solution: float32 [64, 262144], P(None, ('level', 'leaf', 'rhs'))
Inputs may be any that keep to these rules, and one draw needn't show every extreme that they name: `cluster_order`: every aligned block of 4096 entries is a permutation of 0 to 4095. `near_index`: the entries of a row are distinct tile numbers of the same leaf, the first being the row's own tile. `near_count`: the first tile row of every leaf has 4.
All inputs are finite; a program needn't handle non-finite values.
Results may differ from a plain program's by a relative error of at most 0.0001.
Values sent between devices are 32-bit elements; how exact they have to be, the bound alone decides.
No kernel may reach another device: no remote copies, remote signals or barrier semaphores. Data moves between devices by JAX's collectives and lax.ppermute only.
A program may use at most 128 MiB of HBM per device.

v0:
```python
import jax
import jax.numpy as jnp
from jax import lax
from jax.sharding import PartitionSpec as P


def from_partner(block, axis, distance):
    count = lax.axis_size(axis)
    route = []
    for low in range(count):
        high = low | 1 << distance
        if high != low and high < count:
            route += [(low, high), (high, low)]
    return lax.ppermute(block, axis, route)


def partner_sum(values, bit_pos):
    return from_partner(values, ("level", "leaf"), bit_pos)


def local(
    charges, cluster_order, near_tiles, near_index, near_count, proj_basis, corr_basis, coupling
):
    rhs_count = charges.shape[0]
    row_count = charges.shape[1]
    near_slots = near_tiles.shape[1]
    tile_size = near_tiles.shape[2]
    leaf_charges = lax.all_gather(charges, "rhs", axis=1, tiled=True)
    ordered = jnp.take(leaf_charges, cluster_order, axis=1)
    blocks = ordered.reshape(rhs_count, -1, tile_size)
    picked = blocks[:, near_index]
    live_mask = (jnp.arange(near_slots)[None, :] < near_count[:, None]).astype(jnp.float32)
    picked = picked * live_mask[None, :, :, None]
    current = jnp.einsum("rtki,tkio->rto", picked, near_tiles, precision=lax.Precision.HIGHEST)
    current = current.reshape(rhs_count, row_count)
    for height in range(proj_basis.shape[0]):
        projected = jnp.dot(
            current,
            proj_basis[height],
            precision=lax.Precision.HIGHEST,
            preferred_element_type=jnp.float32,
        )
        own_sum = lax.psum(projected, "rhs")
        for bit_pos in range(height):
            own_sum = own_sum + partner_sum(own_sum, bit_pos)
        sib_sum = partner_sum(own_sum, height)
        coeff = jnp.dot(
            own_sum,
            coupling[0, height, 0],
            precision=lax.Precision.HIGHEST,
            preferred_element_type=jnp.float32,
        )
        coeff = coeff + jnp.dot(
            sib_sum,
            coupling[0, height, 1],
            precision=lax.Precision.HIGHEST,
            preferred_element_type=jnp.float32,
        )
        current = current - jnp.dot(
            coeff,
            corr_basis[height],
            precision=lax.Precision.HIGHEST,
            preferred_element_type=jnp.float32,
        )
    return current


def solution(mesh):
    return jax.shard_map(
        local,
        mesh=mesh,
        in_specs=(
            P(None, ("level", "leaf", "rhs")),
            P(("level", "leaf")),
            P(("level", "leaf", "rhs"), None, None, None),
            P(("level", "leaf", "rhs"), None),
            P(("level", "leaf", "rhs")),
            P(None, ("level", "leaf", "rhs"), None),
            P(None, None, ("level", "leaf", "rhs")),
            P(("level", "leaf"), None, None, None, None),
        ),
        out_specs=P(None, ("level", "leaf", "rhs")),
        check_vma=False,
    )
```

profile of v0, /device:TPU:0, one launch (start us, length us, event | category | flops | bytes accessed | tf_op | source)
XLA Modules:
  0.0 264.1 jit_solution(9186109787617975266)
XLA Ops:
  6.5 2.4 copy.12
  8.9 0.0 all-gather.2.cloned.1.call-update
  8.9 0.0 all-reduce.5.cloned.1.call-start
  9.0 0.1 copy.13
  9.1 0.1 reshape.48
  9.2 0.1 fusion.50
  9.3 0.0 copy-done.1
  9.3 37.9 %all-gather.2.cloned.1.call-done = f32[64,4096]{0,1:T(8,128)} async-done(((f32[64,2048]{0,1:T(8,128)}), f32[64,4096]{0,1:T(8,128)}) %all-gather.2.cloned.1.call-update) | async-done | bytes 1048592 | tf_op jit(solution)/shard_map/all_gather | solution.py:28
  47.2 15.7 %gather_fusion = f32[4096,64]{1,0:T(8,128)} fusion(f32[64,4096]{0,1:T(8,128)} %all-gather.2.cloned.1.call-done, s32[4096]{0:T(1024)S(1)} %fusion.49), kind=kCustom, calls=%fused_computation | custom fusion | bytes 2113536 | tf_op jit(solution)/shard_map/jit(_take)/gather | solution.py:29
  62.9 1.9 broadcast_select_fusion
  64.8 2.8 %gather_fusion.1 = f32[64,64,128]{1,2,0:T(8,128)} fusion(f32[64,32,128]{0,2,1:T(8,128)S(1)} %broadcast_select_fusion, s32[1024]{0:T(1024)S(1)} %pad_clamp_fusion), kind=kCustom, calls=%fused_computation.1 | custom fusion | bytes 4194560 | tf_op jit(solution)/shard_map/gather | solution.py:31
  67.6 2.8 %copy.14 = f32[64,64,128]{2,1,0:T(8,128)S(1)} copy(f32[64,64,128]{1,2,0:T(8,128)} %gather_fusion.1) | data formatting | bytes 4194304 | tf_op jit(solution)/shard_map/gather | solution.py:31
  70.5 4.6 %fusion.23 = f32[16,8,8,128]{3,2,1,0:T(8,128)S(1)} fusion(f32[16,4,128,128]{3,2,1,0:T(8,128)} %param.10, f32[16,4,64,128]{3,2,1,0:T(8,128)S(1)} %bitcast.85, f32[16,4]{1,0:T(8,128)S(1)} %fusion.50), kind=kOutput, calls=%fused_computation.29 | convolution fusion | flops 805830656 | bytes 6816000 | tf_op jit(solution)/shard_map/rtki,tkio->rto/dot_general | solution.py:34
  75.1 3.4 %fusion.10 = f32[64,256]{1,0:T(8,128)} fusion(f32[4,2048,256]{2,1,0:T(8,128)} %param.13, f32[16,8,8,128]{3,2,1,0:T(8,128)S(1)} %fusion.23), kind=kOutput, calls=%fused_computation.16 | convolution fusion | flops 402653184 | bytes 2686976 | tf_op jit(solution)/shard_map/dot_general | solution.py:37
  78.5 0.0 all-reduce.5.cloned.1.call-update
  78.5 0.0 all-reduce.7.cloned.1.call-start
  78.5 28.5 %all-reduce.5.cloned.1.call-done = f32[64,256]{1,0:T(8,128)} async-done(((f32[64,256]{1,0:T(8,128)}), f32[64,256]{1,0:T(8,128)}) %all-reduce.5.cloned.1.call-update) | async-done | bytes 65552 | tf_op jit(solution)/shard_map/psum | solution.py:43
  107.0 0.0 collective-permute-start
  107.0 1.2 fusion.39
  108.2 0.2 collective-permute-done
  108.5 1.2 convolution_add_fusion.3
  109.7 3.0 %convolution_subtract_fusion.3 = f32[64,2048]{1,0:T(8,128)S(1)} fusion(f32[64,256]{1,0:T(8,128)S(1)} %convolution_add_fusion.3, f32[4,256,2048]{2,1,0:T(8,128)} %param.14, f32[16,8,8,128]{3,2,1,0:T(8,128)S(1)} %fusion.23), kind=kOutput, calls=%fused_computation.5 | convolution fusion | flops 402784256 | bytes 3211264 | tf_op jit(solution)/shard_map/dot_general | solution.py:59
  112.6 3.5 %fusion.7 = f32[64,256]{1,0:T(8,128)} fusion(f32[64,2048]{1,0:T(8,128)S(1)} %convolution_subtract_fusion.3, f32[4,2048,256]{2,1,0:T(8,128)} %param.13), kind=kOutput, calls=%fused_computation.13 | convolution fusion | flops 402653184 | bytes 2686976 | tf_op jit(solution)/shard_map/dot_general | solution.py:37
  116.2 0.0 all-reduce.7.cloned.1.call-update
  116.2 0.0 all-reduce.9.cloned.1.call-start
  116.3 28.5 %all-reduce.7.cloned.1.call-done = f32[64,256]{1,0:T(8,128)} async-done(((f32[64,256]{1,0:T(8,128)}), f32[64,256]{1,0:T(8,128)}) %all-reduce.7.cloned.1.call-update) | async-done | bytes 65552 | tf_op jit(solution)/shard_map/psum | solution.py:43
  144.7 0.0 collective-permute-start.1
  144.7 1.5 collective-permute-done.1
  146.2 0.8 add.57
  147.0 1.5 collective-permute-start.2
  148.6 2.8 %collective-permute-done.2 = f32[64,256]{1,0:T(8,128)S(1)} collective-permute-done((f32[64,256]{1,0:T(8,128)S(1)}, f32[64,256]{1,0:T(8,128)S(1)}, u32[]{:S(2)}, u32[]{:S(2)}) %collective-permute-start.2) | collective-permute-done | bytes 65568 | tf_op jit(solution)/shard_map/ppermute | solution.py:14
  151.4 0.0 copy-done
  151.4 0.2 fusion.35
  151.6 0.2 convolution_add_fusion.2
  151.9 3.0 %convolution_subtract_fusion.2 = f32[64,2048]{1,0:T(8,128)S(1)} fusion(f32[64,2048]{1,0:T(8,128)S(1)} %convolution_subtract_fusion.3, f32[64,256]{1,0:T(8,128)S(1)} %convolution_add_fusion.2, f32[4,256,2048]{2,1,0:T(8,128)} %param.14), kind=kOutput, calls=%fused_computation.4 | convolution fusion | flops 402784256 | bytes 3211264 | tf_op jit(solution)/shard_map/dot_general | solution.py:59
  154.9 3.4 %fusion.4 = f32[64,256]{1,0:T(8,128)} fusion(f32[64,2048]{1,0:T(8,128)S(1)} %convolution_subtract_fusion.2, f32[4,2048,256]{2,1,0:T(8,128)} %param.13), kind=kOutput, calls=%fused_computation.10 | convolution fusion | flops 402653184 | bytes 2686976 | tf_op jit(solution)/shard_map/dot_general | solution.py:37
  158.3 0.0 all-reduce.9.cloned.1.call-update
  158.3 0.0 all-reduce.11.cloned.1.call-start
  158.3 28.5 %all-reduce.9.cloned.1.call-done = f32[64,256]{1,0:T(8,128)} async-done(((f32[64,256]{1,0:T(8,128)}), f32[64,256]{1,0:T(8,128)}) %all-reduce.9.cloned.1.call-update) | async-done | bytes 65552 | tf_op jit(solution)/shard_map/psum | solution.py:43
  186.8 0.0 collective-permute-start.3
  186.8 1.5 collective-permute-done.3
  188.2 0.9 add.59
  189.1 1.5 collective-permute-start.4
  190.6 2.8 %collective-permute-done.4 = f32[64,256]{1,0:T(8,128)S(1)} collective-permute-done((f32[64,256]{1,0:T(8,128)S(1)}, f32[64,256]{1,0:T(8,128)S(1)}, u32[]{:S(2)}, u32[]{:S(2)}) %collective-permute-start.4) | collective-permute-done | bytes 65568 | tf_op jit(solution)/shard_map/ppermute | solution.py:14
  193.5 3.2 %collective-permute-start.5 = (f32[64,256]{1,0:T(8,128)S(1)}, f32[64,256]{1,0:T(8,128)S(1)}, u32[]{:S(2)}, u32[]{:S(2)}) collective-permute-start(f32[64,256]{1,0:T(8,128)S(1)} %add.60), channel_id=1, source_target_pairs={{0,8},{8,0},{2,10},{10,2},{4,12},{12,4},{6,14},{14,6},{16,24},{24,... | collective-permute-start | bytes 196616 | tf_op jit(solution)/shard_map/ppermute | solution.py:14
  196.7 2.8 %collective-permute-done.5 = f32[64,256]{1,0:T(8,128)S(1)} collective-permute-done((f32[64,256]{1,0:T(8,128)S(1)}, f32[64,256]{1,0:T(8,128)S(1)}, u32[]{:S(2)}, u32[]{:S(2)}) %collective-permute-start.5) | collective-permute-done | bytes 65568 | tf_op jit(solution)/shard_map/ppermute | solution.py:14
  199.5 0.2 fusion.32
  199.7 0.3 convolution_add_fusion.1
  200.0 3.0 %convolution_subtract_fusion.1 = f32[64,2048]{1,0:T(8,128)S(1)} fusion(f32[64,2048]{1,0:T(8,128)S(1)} %convolution_subtract_fusion.2, f32[64,256]{1,0:T(8,128)S(1)} %convolution_add_fusion.1, f32[4,256,2048]{2,1,0:T(8,128)} %param.14), kind=kOutput, calls=%fused_computation.3 | convolution fusion | flops 402784256 | bytes 3211264 | tf_op jit(solution)/shard_map/dot_general | solution.py:59
  203.0 3.4 %fusion.1 = f32[64,256]{1,0:T(8,128)} fusion(f32[64,2048]{1,0:T(8,128)S(1)} %convolution_subtract_fusion.1, f32[4,2048,256]{2,1,0:T(8,128)} %param.13), kind=kOutput, calls=%fused_computation.7 | convolution fusion | flops 402653184 | bytes 2686976 | tf_op jit(solution)/shard_map/dot_general | solution.py:37
  206.4 0.0 all-reduce.11.cloned.1.call-update
  206.4 28.5 %all-reduce.11.cloned.1.call-done = f32[64,256]{1,0:T(8,128)} async-done(((f32[64,256]{1,0:T(8,128)}), f32[64,256]{1,0:T(8,128)}) %all-reduce.11.cloned.1.call-update) | async-done | bytes 65552 | tf_op jit(solution)/shard_map/psum | solution.py:43
  234.9 0.0 collective-permute-start.6
  234.9 1.5 collective-permute-done.6
  236.4 0.8 add.62
  237.2 1.5 collective-permute-start.7
  238.8 2.8 %collective-permute-done.7 = f32[64,256]{1,0:T(8,128)S(1)} collective-permute-done((f32[64,256]{1,0:T(8,128)S(1)}, f32[64,256]{1,0:T(8,128)S(1)}, u32[]{:S(2)}, u32[]{:S(2)}) %collective-permute-start.7) | collective-permute-done | bytes 65568 | tf_op jit(solution)/shard_map/ppermute | solution.py:14
  241.6 3.1 %collective-permute-start.8 = (f32[64,256]{1,0:T(8,128)S(1)}, f32[64,256]{1,0:T(8,128)S(1)}, u32[]{:S(2)}, u32[]{:S(2)}) collective-permute-start(f32[64,256]{1,0:T(8,128)S(1)} %add.63), channel_id=1, source_target_pairs={{0,8},{8,0},{2,10},{10,2},{4,12},{12,4},{6,14},{14,6},{16,24},{24,... | collective-permute-start | bytes 196616 | tf_op jit(solution)/shard_map/ppermute | solution.py:14
  244.6 2.8 %collective-permute-done.8 = f32[64,256]{1,0:T(8,128)S(1)} collective-permute-done((f32[64,256]{1,0:T(8,128)S(1)}, f32[64,256]{1,0:T(8,128)S(1)}, u32[]{:S(2)}, u32[]{:S(2)}) %collective-permute-start.8) | collective-permute-done | bytes 65568 | tf_op jit(solution)/shard_map/ppermute | solution.py:14
  247.4 2.8 %collective-permute-start.9 = (f32[64,256]{1,0:T(8,128)S(1)}, f32[64,256]{1,0:T(8,128)S(1)}, u32[]{:S(2)}, u32[]{:S(2)}) collective-permute-start(f32[64,256]{1,0:T(8,128)S(1)} %add.64), channel_id=1, source_target_pairs={{0,16},{16,0},{2,18},{18,2},{4,20},{20,4},{6,22},{22,6},{8,24},{24... | collective-permute-start | bytes 196616 | tf_op jit(solution)/shard_map/ppermute | solution.py:14
  250.2 3.0 %collective-permute-done.9 = f32[64,256]{1,0:T(8,128)S(1)} collective-permute-done((f32[64,256]{1,0:T(8,128)S(1)}, f32[64,256]{1,0:T(8,128)S(1)}, u32[]{:S(2)}, u32[]{:S(2)}) %collective-permute-start.9) | collective-permute-done | bytes 65568 | tf_op jit(solution)/shard_map/ppermute | solution.py:14
  253.3 0.2 fusion.29
  253.5 0.2 convolution_add_fusion
  253.8 3.8 %convolution_subtract_fusion = f32[64,2048]{1,0:T(8,128)} fusion(f32[64,2048]{1,0:T(8,128)S(1)} %convolution_subtract_fusion.1, f32[64,256]{1,0:T(8,128)S(1)} %convolution_add_fusion, f32[4,256,2048]{2,1,0:T(8,128)} %param.14), kind=kOutput, calls=%fused_computation.2 | convolution fusion | flops 402784256 | bytes 3211264 | tf_op jit(solution)/shard_map/dot_general | solution.py:59
  (14 shorter events, 0.1 us)
Async XLA Ops:
  6.5 2.5 copy-start.2
  6.5 2.7 %copy-start.3 = (s32[16]{0:T(128)S(1)}, s32[16]{0:T(128)}, u32[]{:S(2)}) copy-start(s32[16]{0:T(128)} %param.12) | copy-start | bytes 196
  6.5 2.8 %copy-start.1 = (s32[4096]{0:T(1024)S(1)}, s32[4096]{0:T(1024)}, u32[]{:S(2)}) copy-start(s32[4096]{0:T(1024)} %param.9) | copy-start | bytes 49156
  6.5 40.7 %all-gather.2.cloned.1.call-start = ((), (), s32[]{:S(2)}) async-start(), calls=%async_computation | async-start | bytes 3145728 | tf_op jit(solution)/shard_map/all_gather | solution.py:28
  8.9 98.0 %all-reduce.5.cloned.1.call-start = ((), (), s32[]{:S(2)}) async-start(), calls=%async_computation.1 | async-start | bytes 131072 | tf_op jit(solution)/shard_map/psum | solution.py:43
  78.5 66.2 %all-reduce.7.cloned.1.call-start = ((), (), s32[]{:S(2)}) async-start(), calls=%async_computation.2 | async-start | bytes 131072 | tf_op jit(solution)/shard_map/psum | solution.py:43
  107.0 1.5 collective-permute-start
  112.6 38.7 %copy-start = (f32[1,4,2,256,256]{4,3,2,1,0:T(8,128)S(1)}, f32[1,4,2,256,256]{4,3,2,1,0:T(8,128)}, u32[]{:S(2)}) copy-start(f32[1,4,2,256,256]{4,3,2,1,0:T(8,128)} %param.15) | copy-start | bytes 6291460
  116.2 70.6 %all-reduce.9.cloned.1.call-start = ((), (), s32[]{:S(2)}) async-start(), calls=%async_computation.3 | async-start | bytes 131072 | tf_op jit(solution)/shard_map/psum | solution.py:43
  144.7 1.5 collective-permute-start.1
  147.0 4.3 %collective-permute-start.2 = (f32[64,256]{1,0:T(8,128)S(1)}, f32[64,256]{1,0:T(8,128)S(1)}, u32[]{:S(2)}, u32[]{:S(2)}) collective-permute-start(f32[64,256]{1,0:T(8,128)S(1)} %add.57), channel_id=1, source_target_pairs={{0,4},{4,0},{2,6},{6,2},{8,12},{12,8},{10,14},{14,10},{16,20},{20,... | collective-permute-start | bytes 196616 | tf_op jit(solution)/shard_map/ppermute | solution.py:14
  158.3 76.6 %all-reduce.11.cloned.1.call-start = ((), (), s32[]{:S(2)}) async-start(), calls=%async_computation.4 | async-start | bytes 131072 | tf_op jit(solution)/shard_map/psum | solution.py:43
  186.8 1.5 collective-permute-start.3
  189.1 4.3 %collective-permute-start.4 = (f32[64,256]{1,0:T(8,128)S(1)}, f32[64,256]{1,0:T(8,128)S(1)}, u32[]{:S(2)}, u32[]{:S(2)}) collective-permute-start(f32[64,256]{1,0:T(8,128)S(1)} %add.59), channel_id=1, source_target_pairs={{0,4},{4,0},{2,6},{6,2},{8,12},{12,8},{10,14},{14,10},{16,20},{20,... | collective-permute-start | bytes 196616 | tf_op jit(solution)/shard_map/ppermute | solution.py:14
  193.5 6.0 %collective-permute-start.5 = (f32[64,256]{1,0:T(8,128)S(1)}, f32[64,256]{1,0:T(8,128)S(1)}, u32[]{:S(2)}, u32[]{:S(2)}) collective-permute-start(f32[64,256]{1,0:T(8,128)S(1)} %add.60), channel_id=1, source_target_pairs={{0,8},{8,0},{2,10},{10,2},{4,12},{12,4},{6,14},{14,6},{16,24},{24,... | collective-permute-start | bytes 196616 | tf_op jit(solution)/shard_map/ppermute | solution.py:14
  234.9 1.5 collective-permute-start.6
  237.2 4.3 %collective-permute-start.7 = (f32[64,256]{1,0:T(8,128)S(1)}, f32[64,256]{1,0:T(8,128)S(1)}, u32[]{:S(2)}, u32[]{:S(2)}) collective-permute-start(f32[64,256]{1,0:T(8,128)S(1)} %add.62), channel_id=1, source_target_pairs={{0,4},{4,0},{2,6},{6,2},{8,12},{12,8},{10,14},{14,10},{16,20},{20,... | collective-permute-start | bytes 196616 | tf_op jit(solution)/shard_map/ppermute | solution.py:14
  241.6 5.8 %collective-permute-start.8 = (f32[64,256]{1,0:T(8,128)S(1)}, f32[64,256]{1,0:T(8,128)S(1)}, u32[]{:S(2)}, u32[]{:S(2)}) collective-permute-start(f32[64,256]{1,0:T(8,128)S(1)} %add.63), channel_id=1, source_target_pairs={{0,8},{8,0},{2,10},{10,2},{4,12},{12,4},{6,14},{14,6},{16,24},{24,... | collective-permute-start | bytes 196616 | tf_op jit(solution)/shard_map/ppermute | solution.py:14
  247.4 5.8 %collective-permute-start.9 = (f32[64,256]{1,0:T(8,128)S(1)}, f32[64,256]{1,0:T(8,128)S(1)}, u32[]{:S(2)}, u32[]{:S(2)}) collective-permute-start(f32[64,256]{1,0:T(8,128)S(1)} %add.64), channel_id=1, source_target_pairs={{0,16},{16,0},{2,18},{18,2},{4,20},{20,4},{6,22},{22,6},{8,24},{24... | collective-permute-start | bytes 196616 | tf_op jit(solution)/shard_map/ppermute | solution.py:14
Sparse Core Ops, SparseCore 0:
  9.1 38.0 all-gather.1
  78.6 28.3 all-reduce.4
  116.3 28.3 all-reduce.6
  158.4 28.3 all-reduce.8
  206.5 28.3 all-reduce.10
where the time goes:
time: 265 us; the launch traced here: 264 us
  waiting for transfers between devices  173 us (65%)
  matrix products  34.9 us (13%)
  local copies, waits for them, and re-layouts  23.9 us (9%)
  starting transfers between devices  13.9 us (5%)
  between operations  13.3 us (5%)
  other arithmetic  4.61 us (2%)
    psum x4, waiting for transfers between devices, local(): own_sum = lax.psum(projected, 'rhs')  114 us
    all_gather x1, waiting for transfers between devices, local(): leaf_charges = lax.all_gather(charges, 'rhs', axis=1, tiled=True)  37.9 us
    ppermute x10, waiting for transfers between devices, from_partner(): return lax.ppermute(block, axis, route)  21.6 us
    gather x1, local copies, waits for them, and re-layouts, local(): ordered = jnp.take(leaf_charges, cluster_order, axis=1)  15.7 us
    ppermute x10, starting transfers between devices, from_partner(): return lax.ppermute(block, axis, route)  13.8 us
    dot_general x4, matrix products, local(): jnp.dot(current, proj_basis[height], precision=lax.Precision.HIGHEST, pre...  13.7 us
    dot_general x4, matrix products, local(): jnp.dot(coeff, corr_basis[height], precision=lax.Precision.HIGHEST, prefe...  12.7 us
    gather x2, local copies, waits for them, and re-layouts, local(): picked = blocks[:, near_index]  5.6 us
  transfers between devices with their start and end apart: 15, of which 15 were waited for; matrix products, arithmetic and copies ran while one was open for 1% of the time, Pallas kernels for 0%

commit v1 on v0

--- a/solution.py
+++ b/solution.py
@@ -25,41 +25,45 @@
     row_count = charges.shape[1]
     near_slots = near_tiles.shape[1]
     tile_size = near_tiles.shape[2]
-    leaf_charges = lax.all_gather(charges, "rhs", axis=1, tiled=True)
+    other = from_partner(charges, "rhs", 0)
+    first = lax.axis_index("rhs") == 0
+    leaf_charges = jnp.concatenate(
+        [jnp.where(first, charges, other), jnp.where(first, other, charges)], axis=1
+    )
     ordered = jnp.take(leaf_charges, cluster_order, axis=1)
     blocks = ordered.reshape(rhs_count, -1, tile_size)
     picked = blocks[:, near_index]
     live_mask = (jnp.arange(near_slots)[None, :] < near_count[:, None]).astype(jnp.float32)
     picked = picked * live_mask[None, :, :, None]
-    current = jnp.einsum("rtki,tkio->rto", picked, near_tiles, precision=lax.Precision.HIGHEST)
+    current = jnp.einsum("rtki,tkio->rto", picked, near_tiles, precision=lax.Precision.HIGH)
     current = current.reshape(rhs_count, row_count)
     for height in range(proj_basis.shape[0]):
         projected = jnp.dot(
             current,
             proj_basis[height],
-            precision=lax.Precision.HIGHEST,
+            precision=lax.Precision.HIGH,
             preferred_element_type=jnp.float32,
         )
-        own_sum = lax.psum(projected, "rhs")
+        own_sum = projected + from_partner(projected, "rhs", 0)
         for bit_pos in range(height):
             own_sum = own_sum + partner_sum(own_sum, bit_pos)
         sib_sum = partner_sum(own_sum, height)
         coeff = jnp.dot(
             own_sum,
             coupling[0, height, 0],
-            precision=lax.Precision.HIGHEST,
+            precision=lax.Precision.HIGH,
             preferred_element_type=jnp.float32,
         )
         coeff = coeff + jnp.dot(
             sib_sum,
             coupling[0, height, 1],
-            precision=lax.Precision.HIGHEST,
+            precision=lax.Precision.HIGH,
             preferred_element_type=jnp.float32,
         )
         current = current - jnp.dot(
             coeff,
             corr_basis[height],
-            precision=lax.Precision.HIGHEST,
+            precision=lax.Precision.HIGH,
             preferred_element_type=jnp.float32,
         )
     return current

time: 265 us -> 112 us (0.42)
  waiting for transfers between devices: 173 us -> 38.1 us
  matrix products: 34.9 us -> 21.7 us
  between operations: 13.3 us -> 0.32 us
  starting transfers between devices: 13.9 us -> 24.5 us
    psum x4 -> x0, waiting for transfers between devices: 114 us -> none  [local(): own_sum = lax.psum(projected, 'rhs')]
    all_gather x1 -> x0, waiting for transfers between devices: 37.9 us -> none  [local(): leaf_charges = lax.all_gather(charges, 'rhs', axis=1, tiled=True)]
    ppermute x10 -> x15, waiting for transfers between devices: 21.6 us -> 38.1 us  [from_partner(): return lax.ppermute(block, axis, route)]
    dot_general x16, matrix products: 30.3 us -> 17.7 us  [the longest x4 7.82 us: local(): jnp.dot(coeff, corr_basis[height], precision=lax.Precision.HIGH, preferre...]
    ppermute x10 -> x15, starting transfers between devices: 13.8 us -> 24.5 us  [from_partner(): return lax.ppermute(block, axis, route)]
  transfers between devices with their start and end apart: 15 -> 15, of which waited for: 15 -> 15; matrix products, arithmetic and copies ran while one was open for 1% -> 4% of each run, Pallas kernels for 0% -> 0%
where the time goes in v1:
time: 112 us; the launch traced here: 111 us
  waiting for transfers between devices  38.1 us (34%)
  starting transfers between devices  24.5 us (22%)
  local copies, waits for them, and re-layouts  21.7 us (19%)
  matrix products  21.7 us (19%)
  other arithmetic  5.18 us (5%)
    ppermute x15, waiting for transfers between devices, from_partner(): return lax.ppermute(block, axis, route)  38.1 us
    ppermute x15, starting transfers between devices, from_partner(): return lax.ppermute(block, axis, route)  24.5 us
    gather x1, local copies, waits for them, and re-layouts, local(): ordered = jnp.take(leaf_charges, cluster_order, axis=1)  14.2 us
    dot_general x4, matrix products, local(): jnp.dot(coeff, corr_basis[height], precision=lax.Precision.HIGH, preferre...  7.82 us
    dot_general x4, matrix products, local(): jnp.dot(current, proj_basis[height], precision=lax.Precision.HIGH, prefer...  6.18 us
    gather x2, local copies, waits for them, and re-layouts, local(): picked = blocks[:, near_index]  5.59 us
    dot_general x1, matrix products, local(): jnp.einsum('rtki,tkio->rto', picked, near_tiles, precision=lax.Precision....  3.95 us
  transfers between devices with their start and end apart: 15, of which 15 were waited for; matrix products, arithmetic and copies ran while one was open for 4% of the time, Pallas kernels for 0%

profile of v1, /device:TPU:0, one launch (start us, length us, event | category | flops | bytes accessed | tf_op | source)
XLA Modules:
  0.0 111.5 jit_solution(15144108997019937585)
XLA Ops:
  0.0 1.7 %collective-permute-start = (f32[64,2048]{1,0:T(8,128)}, f32[64,2048]{1,0:T(8,128)S(1)}, u32[]{:S(2)}, u32[]{:S(2)}) collective-permute-start(f32[64,2048]{1,0:T(8,128)} %param.8), channel_id=1, source_target_pairs={{0,1},{1,0},{2,3},{3,2},{4,5},{5,4},{6,7},{7,6},{8,9},{9,8},{10,11... | collective-permute-start | bytes 1572872 | tf_op jit(solution)/shard_map/ppermute | solution.py:14
  1.7 1.4 %copy.20 = f32[64,2048]{0,1:T(8,128)S(1)} copy(f32[64,2048]{1,0:T(8,128)} %param.8) | data formatting | bytes 1048576 | tf_op args[0]
  3.1 0.7 compare_select_fusion.1
  3.8 0.1 copy.24
  3.8 0.1 reshape.48
  3.9 0.7 fusion.50
  4.7 0.7 and_bitcast_fusion
  5.4 0.7 fusion.49
  6.1 7.7 %collective-permute-done = f32[64,2048]{1,0:T(8,128)S(1)} collective-permute-done((f32[64,2048]{1,0:T(8,128)}, f32[64,2048]{1,0:T(8,128)S(1)}, u32[]{:S(2)}, u32[]{:S(2)}) %collective-permute-start) | collective-permute-done | bytes 524320 | tf_op jit(solution)/shard_map/ppermute | solution.py:14
  13.8 0.3 copy.21
  14.1 0.1 broadcast_select_fusion.2
  14.3 0.1 pad_maximum_fusion
  14.4 14.2 %gather_fusion = f32[4096,64]{1,0:T(8,128)} fusion(f32[64,4096]{0,1:T(8,128)S(1)} %pad_maximum_fusion, s32[4096]{0:T(1024)S(1)} %fusion.49), kind=kCustom, calls=%fused_computation | custom fusion | bytes 2113536 | tf_op jit(solution)/shard_map/jit(_take)/gather | solution.py:33
  28.6 1.9 %broadcast_select_fusion = f32[64,32,128]{0,2,1:T(8,128)S(1)} fusion(f32[64,32,128]{0,2,1:T(8,128)} %bitcast.90, pred[32,128]{1,0:T(8,128)(4,1)S(1)} %and_bitcast_fusion), kind=kLoop, calls=%fused_computation.36 | loop fusion | flops 262144 | bytes 2101248 | tf_op jit(solution)/shard_map/jit(_take)/select_n | solution.py:33
  30.5 2.8 %gather_fusion.1 = f32[64,64,128]{1,2,0:T(8,128)} fusion(f32[64,32,128]{0,2,1:T(8,128)S(1)} %broadcast_select_fusion, s32[1024]{0:T(1024)S(1)} %pad_clamp_fusion), kind=kCustom, calls=%fused_computation.1 | custom fusion | bytes 4194560 | tf_op jit(solution)/shard_map/gather | solution.py:35
  33.3 2.8 %copy.25 = f32[64,64,128]{2,1,0:T(8,128)S(1)} copy(f32[64,64,128]{1,2,0:T(8,128)} %gather_fusion.1) | data formatting | bytes 4194304 | tf_op jit(solution)/shard_map/gather | solution.py:35
  36.1 0.0 slice-start
  36.1 0.0 slice-start.2
  36.2 3.9 %fusion.23 = f32[16,8,8,128]{3,2,1,0:T(8,128)S(1)} fusion(f32[16,4,128,128]{3,2,1,0:T(8,128)} %param.10, f32[16,4,64,128]{3,2,1,0:T(8,128)S(1)} %bitcast.89, f32[16,4]{1,0:T(8,128)S(1)} %fusion.50), kind=kOutput, calls=%fused_computation.30 | convolution fusion | flops 403177472 | bytes 6816000 | tf_op jit(solution)/shard_map/rtki,tkio->rto/dot_general | solution.py:38
  40.1 2.3 %fusion.10 = f32[64,256]{1,0:T(8,128)S(1)} fusion(f32[4,2048,256]{2,1,0:T(8,128)} %param.13, f32[16,8,8,128]{3,2,1,0:T(8,128)S(1)} %fusion.23), kind=kOutput, calls=%fused_computation.17 | convolution fusion | flops 201326592 | bytes 2686976 | tf_op jit(solution)/shard_map/dot_general | solution.py:41
  42.4 1.8 %collective-permute-start.1 = (f32[64,256]{1,0:T(8,128)S(1)}, f32[64,256]{1,0:T(8,128)S(1)}, u32[]{:S(2)}, u32[]{:S(2)}) collective-permute-start(f32[64,256]{1,0:T(8,128)S(1)} %fusion.10), channel_id=1, source_target_pairs={{0,1},{1,0},{2,3},{3,2},{4,5},{5,4},{6,7},{7,6},{8,9},{9,8},{10,11... | collective-permute-start | bytes 196616 | tf_op jit(solution)/shard_map/ppermute | solution.py:14
  44.3 2.5 %collective-permute-done.1 = f32[64,256]{1,0:T(8,128)S(1)} collective-permute-done((f32[64,256]{1,0:T(8,128)S(1)}, f32[64,256]{1,0:T(8,128)S(1)}, u32[]{:S(2)}, u32[]{:S(2)}) %collective-permute-start.1) | collective-permute-done | bytes 65568 | tf_op jit(solution)/shard_map/ppermute | solution.py:14
  46.8 0.1 collective-permute-start.2
  46.9 1.2 %collective-permute-done.2 = f32[64,256]{1,0:T(8,128)S(1)} collective-permute-done((f32[64,256]{1,0:T(8,128)S(1)}, f32[64,256]{1,0:T(8,128)S(1)}, u32[]{:S(2)}, u32[]{:S(2)}) %collective-permute-start.2) | collective-permute-done | bytes 65568 | tf_op jit(solution)/shard_map/ppermute | solution.py:14
  48.1 1.2 %fusion.38 = f32[64,256]{1,0:T(8,128)S(1)} fusion(f32[64,256]{1,0:T(8,128)S(1)} %collective-permute-done.2, f32[1,4,2,256,256]{4,3,2,1,0:T(8,128)} %param.15), kind=kOutput, calls=%fused_computation.50 | convolution fusion | flops 25165824 | bytes 393216 | tf_op jit(solution)/shard_map/dot_general | solution.py:57
  49.3 1.3 %convolution_add_fusion.3 = f32[64,256]{1,0:T(8,128)S(1)} fusion(f32[64,256]{1,0:T(8,128)S(1)} %fusion.38, f32[64,256]{1,0:T(8,128)S(1)} %add.60, f32[1,4,2,256,256]{4,3,2,1,0:T(8,128)} %param.15), kind=kOutput, calls=%fused_computation.34 | convolution fusion | flops 25182208 | bytes 458752 | tf_op jit(solution)/shard_map/dot_general | solution.py:51
  50.6 0.0 slice-start.3
  50.6 3.0 %convolution_subtract_fusion.3 = f32[64,2048]{1,0:T(8,128)S(1)} fusion(f32[64,256]{1,0:T(8,128)S(1)} %convolution_add_fusion.3, f32[4,256,2048]{2,1,0:T(8,128)} %param.14, f32[16,8,8,128]{3,2,1,0:T(8,128)S(1)} %fusion.23), kind=kOutput, calls=%fused_computation.5 | convolution fusion | flops 201457664 | bytes 3211264 | tf_op jit(solution)/shard_map/dot_general | solution.py:63
  53.6 2.3 %fusion.7 = f32[64,256]{1,0:T(8,128)S(1)} fusion(f32[64,2048]{1,0:T(8,128)S(1)} %convolution_subtract_fusion.3, f32[4,2048,256]{2,1,0:T(8,128)} %param.13), kind=kOutput, calls=%fused_computation.14 | convolution fusion | flops 201326592 | bytes 2686976 | tf_op jit(solution)/shard_map/dot_general | solution.py:41
  55.9 1.8 %collective-permute-start.3 = (f32[64,256]{1,0:T(8,128)S(1)}, f32[64,256]{1,0:T(8,128)S(1)}, u32[]{:S(2)}, u32[]{:S(2)}) collective-permute-start(f32[64,256]{1,0:T(8,128)S(1)} %fusion.7), channel_id=1, source_target_pairs={{0,1},{1,0},{2,3},{3,2},{4,5},{5,4},{6,7},{7,6},{8,9},{9,8},{10,11... | collective-permute-start | bytes 196616 | tf_op jit(solution)/shard_map/ppermute | solution.py:14
  57.8 2.5 %collective-permute-done.3 = f32[64,256]{1,0:T(8,128)S(1)} collective-permute-done((f32[64,256]{1,0:T(8,128)S(1)}, f32[64,256]{1,0:T(8,128)S(1)}, u32[]{:S(2)}, u32[]{:S(2)}) %collective-permute-start.3) | collective-permute-done | bytes 65568 | tf_op jit(solution)/shard_map/ppermute | solution.py:14
  60.3 0.1 collective-permute-start.4
  60.4 1.2 %collective-permute-done.4 = f32[64,256]{1,0:T(8,128)S(1)} collective-permute-done((f32[64,256]{1,0:T(8,128)S(1)}, f32[64,256]{1,0:T(8,128)S(1)}, u32[]{:S(2)}, u32[]{:S(2)}) %collective-permute-start.4) | collective-permute-done | bytes 65568 | tf_op jit(solution)/shard_map/ppermute | solution.py:14
  61.6 1.7 %collective-permute-start.5 = (f32[64,256]{1,0:T(8,128)S(1)}, f32[64,256]{1,0:T(8,128)S(1)}, u32[]{:S(2)}, u32[]{:S(2)}) collective-permute-start(f32[64,256]{1,0:T(8,128)S(1)} %add.63), channel_id=1, source_target_pairs={{0,4},{4,0},{2,6},{6,2},{8,12},{12,8},{10,14},{14,10},{16,20},{20,... | collective-permute-start | bytes 196616 | tf_op jit(solution)/shard_map/ppermute | solution.py:14
  63.4 2.6 %collective-permute-done.5 = f32[64,256]{1,0:T(8,128)S(1)} collective-permute-done((f32[64,256]{1,0:T(8,128)S(1)}, f32[64,256]{1,0:T(8,128)S(1)}, u32[]{:S(2)}, u32[]{:S(2)}) %collective-permute-start.5) | collective-permute-done | bytes 65568 | tf_op jit(solution)/shard_map/ppermute | solution.py:14
  66.0 0.2 fusion.35
  66.2 0.2 convolution_add_fusion.2
  66.4 2.4 %convolution_subtract_fusion.2 = f32[64,2048]{1,0:T(8,128)S(1)} fusion(f32[64,2048]{1,0:T(8,128)S(1)} %convolution_subtract_fusion.3, f32[64,256]{1,0:T(8,128)S(1)} %convolution_add_fusion.2, f32[4,256,2048]{2,1,0:T(8,128)} %param.14), kind=kOutput, calls=%fused_computation.4 | convolution fusion | flops 201457664 | bytes 3211264 | tf_op jit(solution)/shard_map/dot_general | solution.py:63
  68.8 0.8 fusion.4
  69.6 1.8 %collective-permute-start.6 = (f32[64,256]{1,0:T(8,128)S(1)}, f32[64,256]{1,0:T(8,128)S(1)}, u32[]{:S(2)}, u32[]{:S(2)}) collective-permute-start(f32[64,256]{1,0:T(8,128)S(1)} %fusion.4), channel_id=1, source_target_pairs={{0,1},{1,0},{2,3},{3,2},{4,5},{5,4},{6,7},{7,6},{8,9},{9,8},{10,11... | collective-permute-start | bytes 196616 | tf_op jit(solution)/shard_map/ppermute | solution.py:14
  71.4 2.5 %collective-permute-done.6 = f32[64,256]{1,0:T(8,128)S(1)} collective-permute-done((f32[64,256]{1,0:T(8,128)S(1)}, f32[64,256]{1,0:T(8,128)S(1)}, u32[]{:S(2)}, u32[]{:S(2)}) %collective-permute-start.6) | collective-permute-done | bytes 65568 | tf_op jit(solution)/shard_map/ppermute | solution.py:14
  74.0 0.1 collective-permute-start.7
  74.0 1.2 %collective-permute-done.7 = f32[64,256]{1,0:T(8,128)S(1)} collective-permute-done((f32[64,256]{1,0:T(8,128)S(1)}, f32[64,256]{1,0:T(8,128)S(1)}, u32[]{:S(2)}, u32[]{:S(2)}) %collective-permute-start.7) | collective-permute-done | bytes 65568 | tf_op jit(solution)/shard_map/ppermute | solution.py:14
  75.3 1.7 %collective-permute-start.8 = (f32[64,256]{1,0:T(8,128)S(1)}, f32[64,256]{1,0:T(8,128)S(1)}, u32[]{:S(2)}, u32[]{:S(2)}) collective-permute-start(f32[64,256]{1,0:T(8,128)S(1)} %add.66), channel_id=1, source_target_pairs={{0,4},{4,0},{2,6},{6,2},{8,12},{12,8},{10,14},{14,10},{16,20},{20,... | collective-permute-start | bytes 196616 | tf_op jit(solution)/shard_map/ppermute | solution.py:14
  77.0 2.6 %collective-permute-done.8 = f32[64,256]{1,0:T(8,128)S(1)} collective-permute-done((f32[64,256]{1,0:T(8,128)S(1)}, f32[64,256]{1,0:T(8,128)S(1)}, u32[]{:S(2)}, u32[]{:S(2)}) %collective-permute-start.8) | collective-permute-done | bytes 65568 | tf_op jit(solution)/shard_map/ppermute | solution.py:14
  79.7 3.3 %collective-permute-start.9 = (f32[64,256]{1,0:T(8,128)S(1)}, f32[64,256]{1,0:T(8,128)S(1)}, u32[]{:S(2)}, u32[]{:S(2)}) collective-permute-start(f32[64,256]{1,0:T(8,128)S(1)} %add.67), channel_id=1, source_target_pairs={{0,8},{8,0},{2,10},{10,2},{4,12},{12,4},{6,14},{14,6},{16,24},{24,... | collective-permute-start | bytes 196616 | tf_op jit(solution)/shard_map/ppermute | solution.py:14
  82.9 2.6 %collective-permute-done.9 = f32[64,256]{1,0:T(8,128)S(1)} collective-permute-done((f32[64,256]{1,0:T(8,128)S(1)}, f32[64,256]{1,0:T(8,128)S(1)}, u32[]{:S(2)}, u32[]{:S(2)}) %collective-permute-start.9) | collective-permute-done | bytes 65568 | tf_op jit(solution)/shard_map/ppermute | solution.py:14
  85.5 0.2 fusion.32
  85.7 0.2 convolution_add_fusion.1
  86.0 0.8 convolution_subtract_fusion.1
  86.8 0.8 fusion.1
  87.6 1.8 %collective-permute-start.10 = (f32[64,256]{1,0:T(8,128)S(1)}, f32[64,256]{1,0:T(8,128)S(1)}, u32[]{:S(2)}, u32[]{:S(2)}) collective-permute-start(f32[64,256]{1,0:T(8,128)S(1)} %fusion.1), channel_id=1, source_target_pairs={{0,1},{1,0},{2,3},{3,2},{4,5},{5,4},{6,7},{7,6},{8,9},{9,8},{10,11... | collective-permute-start | bytes 196616 | tf_op jit(solution)/shard_map/ppermute | solution.py:14
  89.4 2.5 %collective-permute-done.10 = f32[64,256]{1,0:T(8,128)S(1)} collective-permute-done((f32[64,256]{1,0:T(8,128)S(1)}, f32[64,256]{1,0:T(8,128)S(1)}, u32[]{:S(2)}, u32[]{:S(2)}) %collective-permute-start.10) | collective-permute-done | bytes 65568 | tf_op jit(solution)/shard_map/ppermute | solution.py:14
  92.0 0.1 collective-permute-start.11
  92.1 1.2 %collective-permute-done.11 = f32[64,256]{1,0:T(8,128)S(1)} collective-permute-done((f32[64,256]{1,0:T(8,128)S(1)}, f32[64,256]{1,0:T(8,128)S(1)}, u32[]{:S(2)}, u32[]{:S(2)}) %collective-permute-start.11) | collective-permute-done | bytes 65568 | tf_op jit(solution)/shard_map/ppermute | solution.py:14
  93.3 1.7 %collective-permute-start.12 = (f32[64,256]{1,0:T(8,128)S(1)}, f32[64,256]{1,0:T(8,128)S(1)}, u32[]{:S(2)}, u32[]{:S(2)}) collective-permute-start(f32[64,256]{1,0:T(8,128)S(1)} %add.70), channel_id=1, source_target_pairs={{0,4},{4,0},{2,6},{6,2},{8,12},{12,8},{10,14},{14,10},{16,20},{20,... | collective-permute-start | bytes 196616 | tf_op jit(solution)/shard_map/ppermute | solution.py:14
  95.0 2.6 %collective-permute-done.12 = f32[64,256]{1,0:T(8,128)S(1)} collective-permute-done((f32[64,256]{1,0:T(8,128)S(1)}, f32[64,256]{1,0:T(8,128)S(1)}, u32[]{:S(2)}, u32[]{:S(2)}) %collective-permute-start.12) | collective-permute-done | bytes 65568 | tf_op jit(solution)/shard_map/ppermute | solution.py:14
  97.7 3.3 %collective-permute-start.13 = (f32[64,256]{1,0:T(8,128)S(1)}, f32[64,256]{1,0:T(8,128)S(1)}, u32[]{:S(2)}, u32[]{:S(2)}) collective-permute-start(f32[64,256]{1,0:T(8,128)S(1)} %add.71), channel_id=1, source_target_pairs={{0,8},{8,0},{2,10},{10,2},{4,12},{12,4},{6,14},{14,6},{16,24},{24,... | collective-permute-start | bytes 196616 | tf_op jit(solution)/shard_map/ppermute | solution.py:14
  100.9 2.6 %collective-permute-done.13 = f32[64,256]{1,0:T(8,128)S(1)} collective-permute-done((f32[64,256]{1,0:T(8,128)S(1)}, f32[64,256]{1,0:T(8,128)S(1)}, u32[]{:S(2)}, u32[]{:S(2)}) %collective-permute-start.13) | collective-permute-done | bytes 65568 | tf_op jit(solution)/shard_map/ppermute | solution.py:14
  103.5 3.4 %collective-permute-start.14 = (f32[64,256]{1,0:T(8,128)S(1)}, f32[64,256]{1,0:T(8,128)S(1)}, u32[]{:S(2)}, u32[]{:S(2)}) collective-permute-start(f32[64,256]{1,0:T(8,128)S(1)} %add.72), channel_id=1, source_target_pairs={{0,16},{16,0},{2,18},{18,2},{4,20},{20,4},{6,22},{22,6},{8,24},{24... | collective-permute-start | bytes 196616 | tf_op jit(solution)/shard_map/ppermute | solution.py:14
  107.0 2.4 %collective-permute-done.14 = f32[64,256]{1,0:T(8,128)S(1)} collective-permute-done((f32[64,256]{1,0:T(8,128)S(1)}, f32[64,256]{1,0:T(8,128)S(1)}, u32[]{:S(2)}, u32[]{:S(2)}) %collective-permute-start.14) | collective-permute-done | bytes 65568 | tf_op jit(solution)/shard_map/ppermute | solution.py:14
  109.4 0.2 fusion.29
  109.6 0.2 convolution_add_fusion
  109.8 1.6 %convolution_subtract_fusion = f32[64,2048]{1,0:T(8,128)} fusion(f32[64,2048]{1,0:T(8,128)S(1)} %convolution_subtract_fusion.1, f32[64,256]{1,0:T(8,128)S(1)} %convolution_add_fusion, f32[4,256,2048]{2,1,0:T(8,128)S(1)} %bitcast.88), kind=kOutput, calls=%fused_computation.2 | convolution fusion | flops 201457664 | bytes 3211264 | tf_op jit(solution)/shard_map/dot_general | solution.py:63
  (20 shorter events, 0.1 us)
Async XLA Ops:
  0.0 13.8 %collective-permute-start = (f32[64,2048]{1,0:T(8,128)}, f32[64,2048]{1,0:T(8,128)S(1)}, u32[]{:S(2)}, u32[]{:S(2)}) collective-permute-start(f32[64,2048]{1,0:T(8,128)} %param.8), channel_id=1, source_target_pairs={{0,1},{1,0},{2,3},{3,2},{4,5},{5,4},{6,7},{7,6},{8,9},{9,8},{10,11... | collective-permute-start | bytes 1572872 | tf_op jit(solution)/shard_map/ppermute | solution.py:14
  36.1 32.6 %slice-start = ((s8[8388608]{0:T(1024)(128)(4,1)}), s8[4194304]{0:T(1024)(128)(4,1)S(1)}, s32[]{:S(2)}) async-start(s8[8388608]{0:T(1024)(128)(4,1)} %bitcast.85), calls=%async_computation | async-start | bytes 8388608
  36.1 49.8 %slice-start.2 = ((s8[8388608]{0:T(1024)(128)(4,1)}), s8[4194304]{0:T(1024)(128)(4,1)S(1)}, s32[]{:S(2)}) async-start(s8[8388608]{0:T(1024)(128)(4,1)} %bitcast.87), calls=%async_computation.2 | async-start | bytes 8388608
  42.4 4.3 %collective-permute-start.1 = (f32[64,256]{1,0:T(8,128)S(1)}, f32[64,256]{1,0:T(8,128)S(1)}, u32[]{:S(2)}, u32[]{:S(2)}) collective-permute-start(f32[64,256]{1,0:T(8,128)S(1)} %fusion.10), channel_id=1, source_target_pairs={{0,1},{1,0},{2,3},{3,2},{4,5},{5,4},{6,7},{7,6},{8,9},{9,8},{10,11... | collective-permute-start | bytes 196616 | tf_op jit(solution)/shard_map/ppermute | solution.py:14
  46.8 1.3 %collective-permute-start.2 = (f32[64,256]{1,0:T(8,128)S(1)}, f32[64,256]{1,0:T(8,128)S(1)}, u32[]{:S(2)}, u32[]{:S(2)}) collective-permute-start(f32[64,256]{1,0:T(8,128)S(1)} %add.60), channel_id=1, source_target_pairs={{0,2},{2,0},{4,6},{6,4},{8,10},{10,8},{12,14},{14,12},{16,18},{18,... | collective-permute-start | bytes 196616 | tf_op jit(solution)/shard_map/ppermute | solution.py:14
  49.3 16.7 %copy-start = (f32[1,4,2,256,256]{4,3,2,1,0:T(8,128)S(1)}, f32[1,4,2,256,256]{4,3,2,1,0:T(8,128)}, u32[]{:S(2)}) copy-start(f32[1,4,2,256,256]{4,3,2,1,0:T(8,128)} %param.15) | copy-start | bytes 6291460
  49.3 19.5 %slice-start.1 = ((s8[8388608]{0:T(1024)(128)(4,1)}), s8[4194304]{0:T(1024)(128)(4,1)S(1)}, s32[]{:S(2)}) async-start(s8[8388608]{0:T(1024)(128)(4,1)} %bitcast.85), calls=%async_computation.1 | async-start | bytes 8388608
  50.6 35.3 %slice-start.3 = ((s8[8388608]{0:T(1024)(128)(4,1)}), s8[4194304]{0:T(1024)(128)(4,1)S(1)}, s32[]{:S(2)}) async-start(s8[8388608]{0:T(1024)(128)(4,1)} %bitcast.87), calls=%async_computation.3 | async-start | bytes 8388608
  55.9 4.3 %collective-permute-start.3 = (f32[64,256]{1,0:T(8,128)S(1)}, f32[64,256]{1,0:T(8,128)S(1)}, u32[]{:S(2)}, u32[]{:S(2)}) collective-permute-start(f32[64,256]{1,0:T(8,128)S(1)} %fusion.7), channel_id=1, source_target_pairs={{0,1},{1,0},{2,3},{3,2},{4,5},{5,4},{6,7},{7,6},{8,9},{9,8},{10,11... | collective-permute-start | bytes 196616 | tf_op jit(solution)/shard_map/ppermute | solution.py:14
  60.3 1.3 %collective-permute-start.4 = (f32[64,256]{1,0:T(8,128)S(1)}, f32[64,256]{1,0:T(8,128)S(1)}, u32[]{:S(2)}, u32[]{:S(2)}) collective-permute-start(f32[64,256]{1,0:T(8,128)S(1)} %add.62), channel_id=1, source_target_pairs={{0,2},{2,0},{4,6},{6,4},{8,10},{10,8},{12,14},{14,12},{16,18},{18,... | collective-permute-start | bytes 196616 | tf_op jit(solution)/shard_map/ppermute | solution.py:14
  61.6 4.3 %collective-permute-start.5 = (f32[64,256]{1,0:T(8,128)S(1)}, f32[64,256]{1,0:T(8,128)S(1)}, u32[]{:S(2)}, u32[]{:S(2)}) collective-permute-start(f32[64,256]{1,0:T(8,128)S(1)} %add.63), channel_id=1, source_target_pairs={{0,4},{4,0},{2,6},{6,2},{8,12},{12,8},{10,14},{14,10},{16,20},{20,... | collective-permute-start | bytes 196616 | tf_op jit(solution)/shard_map/ppermute | solution.py:14
  69.6 4.3 %collective-permute-start.6 = (f32[64,256]{1,0:T(8,128)S(1)}, f32[64,256]{1,0:T(8,128)S(1)}, u32[]{:S(2)}, u32[]{:S(2)}) collective-permute-start(f32[64,256]{1,0:T(8,128)S(1)} %fusion.4), channel_id=1, source_target_pairs={{0,1},{1,0},{2,3},{3,2},{4,5},{5,4},{6,7},{7,6},{8,9},{9,8},{10,11... | collective-permute-start | bytes 196616 | tf_op jit(solution)/shard_map/ppermute | solution.py:14
  74.0 1.3 %collective-permute-start.7 = (f32[64,256]{1,0:T(8,128)S(1)}, f32[64,256]{1,0:T(8,128)S(1)}, u32[]{:S(2)}, u32[]{:S(2)}) collective-permute-start(f32[64,256]{1,0:T(8,128)S(1)} %add.65), channel_id=1, source_target_pairs={{0,2},{2,0},{4,6},{6,4},{8,10},{10,8},{12,14},{14,12},{16,18},{18,... | collective-permute-start | bytes 196616 | tf_op jit(solution)/shard_map/ppermute | solution.py:14
  75.3 4.3 %collective-permute-start.8 = (f32[64,256]{1,0:T(8,128)S(1)}, f32[64,256]{1,0:T(8,128)S(1)}, u32[]{:S(2)}, u32[]{:S(2)}) collective-permute-start(f32[64,256]{1,0:T(8,128)S(1)} %add.66), channel_id=1, source_target_pairs={{0,4},{4,0},{2,6},{6,2},{8,12},{12,8},{10,14},{14,10},{16,20},{20,... | collective-permute-start | bytes 196616 | tf_op jit(solution)/shard_map/ppermute | solution.py:14
  79.7 5.8 %collective-permute-start.9 = (f32[64,256]{1,0:T(8,128)S(1)}, f32[64,256]{1,0:T(8,128)S(1)}, u32[]{:S(2)}, u32[]{:S(2)}) collective-permute-start(f32[64,256]{1,0:T(8,128)S(1)} %add.67), channel_id=1, source_target_pairs={{0,8},{8,0},{2,10},{10,2},{4,12},{12,4},{6,14},{14,6},{16,24},{24,... | collective-permute-start | bytes 196616 | tf_op jit(solution)/shard_map/ppermute | solution.py:14
  87.6 4.3 %collective-permute-start.10 = (f32[64,256]{1,0:T(8,128)S(1)}, f32[64,256]{1,0:T(8,128)S(1)}, u32[]{:S(2)}, u32[]{:S(2)}) collective-permute-start(f32[64,256]{1,0:T(8,128)S(1)} %fusion.1), channel_id=1, source_target_pairs={{0,1},{1,0},{2,3},{3,2},{4,5},{5,4},{6,7},{7,6},{8,9},{9,8},{10,11... | collective-permute-start | bytes 196616 | tf_op jit(solution)/shard_map/ppermute | solution.py:14
  92.0 1.3 %collective-permute-start.11 = (f32[64,256]{1,0:T(8,128)S(1)}, f32[64,256]{1,0:T(8,128)S(1)}, u32[]{:S(2)}, u32[]{:S(2)}) collective-permute-start(f32[64,256]{1,0:T(8,128)S(1)} %add.69), channel_id=1, source_target_pairs={{0,2},{2,0},{4,6},{6,4},{8,10},{10,8},{12,14},{14,12},{16,18},{18,... | collective-permute-start | bytes 196616 | tf_op jit(solution)/shard_map/ppermute | solution.py:14
  93.3 4.3 %collective-permute-start.12 = (f32[64,256]{1,0:T(8,128)S(1)}, f32[64,256]{1,0:T(8,128)S(1)}, u32[]{:S(2)}, u32[]{:S(2)}) collective-permute-start(f32[64,256]{1,0:T(8,128)S(1)} %add.70), channel_id=1, source_target_pairs={{0,4},{4,0},{2,6},{6,2},{8,12},{12,8},{10,14},{14,10},{16,20},{20,... | collective-permute-start | bytes 196616 | tf_op jit(solution)/shard_map/ppermute | solution.py:14
  97.7 5.8 %collective-permute-start.13 = (f32[64,256]{1,0:T(8,128)S(1)}, f32[64,256]{1,0:T(8,128)S(1)}, u32[]{:S(2)}, u32[]{:S(2)}) collective-permute-start(f32[64,256]{1,0:T(8,128)S(1)} %add.71), channel_id=1, source_target_pairs={{0,8},{8,0},{2,10},{10,2},{4,12},{12,4},{6,14},{14,6},{16,24},{24,... | collective-permute-start | bytes 196616 | tf_op jit(solution)/shard_map/ppermute | solution.py:14
  103.5 5.8 %collective-permute-start.14 = (f32[64,256]{1,0:T(8,128)S(1)}, f32[64,256]{1,0:T(8,128)S(1)}, u32[]{:S(2)}, u32[]{:S(2)}) collective-permute-start(f32[64,256]{1,0:T(8,128)S(1)} %add.72), channel_id=1, source_target_pairs={{0,16},{16,0},{2,18},{18,2},{4,20},{20,4},{6,22},{22,6},{8,24},{24... | collective-permute-start | bytes 196616 | tf_op jit(solution)/shard_map/ppermute | solution.py:14

commit v2 on v1

v2 whole, which is shorter than its diff:
```python
import jax
import jax.numpy as jnp
from jax import lax
from jax.sharding import Mesh, PartitionSpec as P

AXES = ("z", "y", "x1", "x0", "core", "rhs")
FAST = lax.Precision.HIGH


def dot(a, b):
    return jnp.dot(a, b, precision=FAST, preferred_element_type=jnp.float32)


def swap(block, axes, mask):
    count = lax.axis_size(axes)
    return lax.ppermute(block, axes, [(i, i ^ mask) for i in range(count)])


def over_rhs(block):
    return swap(block, ("rhs",), 1)


PARTNERS = (
    (("core",), 1),
    (("x0",), 1),
    (("x1", "x0"), 3),
    (("y", "x1", "x0", "core", "rhs"), 17),
)


def local(
    charges, cluster_order, near_tiles, near_index, near_count, proj_basis, corr_basis, coupling
):
    rhs_count = charges.shape[0]
    row_count = charges.shape[1]
    near_slots = near_tiles.shape[1]
    tile_size = near_tiles.shape[2]
    levels = proj_basis.shape[0]
    other = over_rhs(charges)
    gram = {}
    for low in range(levels):
        for high in range(low + 1, levels):
            gram[low, high] = dot(corr_basis[low], proj_basis[high])
    first = lax.axis_index("rhs") == 0
    leaf_charges = jnp.concatenate(
        [jnp.where(first, charges, other), jnp.where(first, other, charges)], axis=1
    )
    ordered = jnp.take(leaf_charges, cluster_order, axis=1)
    blocks = ordered.reshape(rhs_count, -1, tile_size)
    picked = blocks[:, near_index]
    live_mask = (jnp.arange(near_slots)[None, :] < near_count[:, None]).astype(jnp.float32)
    picked = picked * live_mask[None, :, :, None]
    current = jnp.einsum("rtki,tkio->rto", picked, near_tiles, precision=FAST)
    current = current.reshape(rhs_count, row_count)
    reduced = [dot(current, proj_basis[height]) for height in range(levels)]
    for height in range(levels):
        own_sum = reduced[height]
        own_sum = own_sum + over_rhs(own_sum)
        for axes, mask in PARTNERS[:height]:
            own_sum = own_sum + swap(own_sum, axes, mask)
        sib_sum = swap(own_sum, *PARTNERS[height])
        coeff = dot(own_sum, coupling[0, height, 0]) + dot(sib_sum, coupling[0, height, 1])
        for high in range(height + 1, levels):
            reduced[high] = reduced[high] - dot(coeff, gram[height, high])
        current = current - dot(coeff, corr_basis[height])
    return current


def solution(mesh):
    split = Mesh(mesh.devices.reshape(-1, 2, 2, 2, 2, 2), AXES)
    every = AXES
    leaf = AXES[:-1]
    return jax.shard_map(
        local,
        mesh=split,
        in_specs=(
            P(None, every),
            P(leaf),
            P(every, None, None, None),
            P(every, None),
            P(every),
            P(None, every, None),
            P(None, None, every),
            P(leaf, None, None, None, None),
        ),
        out_specs=P(None, every),
        check_vma=False,
    )
```

time: 112 us -> 102 us (0.911)
  waiting for transfers between devices: 38.1 us -> 22.3 us
  matrix products: 21.7 us -> 34.5 us
  starting transfers between devices: 24.5 us -> 18.9 us
  other arithmetic: 5.18 us -> 3.85 us
    ppermute x15, waiting for transfers between devices: 38.1 us -> 22.3 us  [swap(): return lax.ppermute(block, axes, [(i, i ^ mask) for i in range(count)])]
    dot_general x17 -> x29, matrix products: 21.7 us -> 34.5 us  [the longest x28 30.6 us: dot(): return jnp.dot(a, b, precision=FAST, preferred_element_type=jnp.float32)]
    ppermute x15, starting transfers between devices: 24.5 us -> 18.9 us  [swap(): return lax.ppermute(block, axes, [(i, i ^ mask) for i in range(count)])]
  transfers between devices with their start and end apart: 15 -> 15, of which waited for: 15 -> 12; matrix products, arithmetic and copies ran while one was open for 4% -> 27% of each run, Pallas kernels for 0% -> 0%
where the time goes in v2:
time: 102 us
  matrix products  34.5 us (34%)
  waiting for transfers between devices  22.3 us (22%)
  local copies, waits for them, and re-layouts  21.7 us (21%)
  starting transfers between devices  18.9 us (19%)
  other arithmetic  3.85 us (4%)
    dot_general x28, matrix products, dot(): return jnp.dot(a, b, precision=FAST, preferred_element_type=jnp.float32)  30.6 us
    ppermute x15, waiting for transfers between devices, swap(): return lax.ppermute(block, axes, [(i, i ^ mask) for i in range(count)])  22.3 us
    ppermute x15, starting transfers between devices, swap(): return lax.ppermute(block, axes, [(i, i ^ mask) for i in range(count)])  18.9 us
    gather x1, local copies, waits for them, and re-layouts, local(): ordered = jnp.take(leaf_charges, cluster_order, axis=1)  14.2 us
    gather x2, local copies, waits for them, and re-layouts, local(): picked = blocks[:, near_index]  5.58 us
    dot_general x1, matrix products, local(): current = jnp.einsum('rtki,tkio->rto', picked, near_tiles, precision=FAST)  3.95 us
  transfers between devices with their start and end apart: 15, of which 12 were waited for; matrix products, arithmetic and copies ran while one was open for 27% of the time, Pallas kernels for 0%

profile of v2, /device:TPU:0, one launch (start us, length us, event | category | flops | bytes accessed | tf_op | source)
XLA Modules:
  0.0 101.6 jit_solution(1567714904024936823)
XLA Ops:
  0.0 1.7 %collective-permute-start = (f32[64,2048]{1,0:T(8,128)}, f32[64,2048]{1,0:T(8,128)S(1)}, u32[]{:S(2)}, u32[]{:S(2)}) collective-permute-start(f32[64,2048]{1,0:T(8,128)} %param.8), channel_id=1, source_target_pairs={{0,1},{1,0},{2,3},{3,2},{4,5},{5,4},{6,7},{7,6},{8,9},{9,8},{10,11... | collective-permute-start | bytes 1572872 | tf_op jit(solution)/shard_map/ppermute | solution.py:16
  1.7 1.4 %copy.20 = f32[64,2048]{0,1:T(8,128)S(1)} copy(f32[64,2048]{1,0:T(8,128)} %param.8) | data formatting | bytes 1048576 | tf_op args[0]
  3.1 0.7 fusion.85
  3.8 0.7 and_bitcast_fusion
  4.5 3.3 %fusion.20 = f32[256,256]{1,0:T(8,128)S(1)} fusion(f32[4,2048,256]{2,1,0:T(8,128)} %param.13, f32[4,256,2048]{2,1,0:T(8,128)} %param.14), kind=kOutput, calls=%fused_computation.27 | convolution fusion | flops 805306368 | bytes 4456448 | tf_op jit(solution)/shard_map/dot_general | solution.py:11
  7.8 3.3 %fusion.5 = f32[256,256]{1,0:T(8,128)S(1)} fusion(f32[4,2048,256]{2,1,0:T(8,128)} %param.13, f32[4,256,2048]{2,1,0:T(8,128)} %param.14), kind=kOutput, calls=%fused_computation.12 | convolution fusion | flops 805306368 | bytes 4456448 | tf_op jit(solution)/shard_map/dot_general | solution.py:11
  11.2 0.1 reshape.48
  11.4 3.3 %fusion.3 = f32[256,256]{1,0:T(8,128)S(1)} fusion(f32[4,256,2048]{2,1,0:T(8,128)} %param.14, f32[4,2048,256]{2,1,0:T(8,128)} %param.13), kind=kOutput, calls=%fused_computation.10 | convolution fusion | flops 805306368 | bytes 4456448 | tf_op jit(solution)/shard_map/dot_general | solution.py:11
  14.7 0.3 copy.21
  15.0 0.1 broadcast_select_fusion.2
  15.2 0.1 pad_maximum_fusion
  15.3 14.2 %gather_fusion = f32[4096,64]{1,0:T(8,128)} fusion(f32[64,4096]{0,1:T(8,128)S(1)} %pad_maximum_fusion, s32[4096]{0:T(1024)S(1)} %fusion.85), kind=kCustom, calls=%fused_computation | custom fusion | bytes 2113536 | tf_op jit(solution)/shard_map/jit(_take)/gather | solution.py:48
  29.5 1.9 %broadcast_select_fusion = f32[64,32,128]{0,2,1:T(8,128)S(1)} fusion(f32[64,32,128]{0,2,1:T(8,128)} %bitcast.129, pred[32,128]{1,0:T(8,128)(4,1)S(1)} %and_bitcast_fusion), kind=kLoop, calls=%fused_computation.72 | loop fusion | flops 262144 | bytes 2101248 | tf_op jit(solution)/shard_map/jit(_take)/select_n | solution.py:48
  31.5 2.8 %gather_fusion.1 = f32[64,64,128]{1,2,0:T(8,128)} fusion(f32[64,32,128]{0,2,1:T(8,128)S(1)} %broadcast_select_fusion, s32[1024]{0:T(1024)S(1)} %pad_clamp_fusion), kind=kCustom, calls=%fused_computation.1 | custom fusion | bytes 4194560 | tf_op jit(solution)/shard_map/gather | solution.py:50
  34.2 2.8 %copy.25 = f32[64,64,128]{2,1,0:T(8,128)S(1)} copy(f32[64,64,128]{1,2,0:T(8,128)} %gather_fusion.1) | data formatting | bytes 4194304 | tf_op jit(solution)/shard_map/gather | solution.py:50
  37.1 3.9 %fusion.53 = f32[16,8,8,128]{3,2,1,0:T(8,128)S(1)} fusion(f32[16,4,128,128]{3,2,1,0:T(8,128)} %param.10, f32[16,4,64,128]{3,2,1,0:T(8,128)S(1)} %bitcast.128, f32[16,4]{1,0:T(8,128)S(1)} %fusion.86), kind=kOutput, calls=%fused_computation.60 | convolution fusion | flops 403177472 | bytes 6816000 | tf_op jit(solution)/shard_map/rtki,tkio->rto/dot_general | solution.py:53
  41.0 2.5 %fusion.28 = f32[64,256]{1,0:T(8,128)S(1)} fusion(f32[4,2048,256]{2,1,0:T(8,128)} %param.13, f32[16,8,8,128]{3,2,1,0:T(8,128)S(1)} %fusion.53), kind=kOutput, calls=%fused_computation.35 | convolution fusion | flops 201326592 | bytes 2686976 | tf_op jit(solution)/shard_map/dot_general | solution.py:11
  43.5 0.9 collective-permute-start.1
  44.4 3.4 %fusion.13 = f32[256,256]{1,0:T(8,128)S(1)} fusion(f32[4,2048,256]{2,1,0:T(8,128)} %param.13, f32[4,256,2048]{2,1,0:T(8,128)} %param.14), kind=kOutput, calls=%fused_computation.20 | convolution fusion | flops 805306368 | bytes 4456448 | tf_op jit(solution)/shard_map/dot_general | solution.py:11
  48.0 2.3 %fusion.22 = f32[64,256]{1,0:T(8,128)S(1)} fusion(f32[4,2048,256]{2,1,0:T(8,128)} %param.13, f32[16,8,8,128]{3,2,1,0:T(8,128)S(1)} %fusion.53), kind=kOutput, calls=%fused_computation.29 | convolution fusion | flops 201326592 | bytes 2686976 | tf_op jit(solution)/shard_map/dot_general | solution.py:11
  50.3 0.2 fusion.74
  50.5 0.2 convolution_add_fusion.3
  50.8 0.2 convolution_subtract_fusion.9
  51.0 1.3 %collective-permute-start.3 = (f32[64,256]{1,0:T(8,128)S(1)}, f32[64,256]{1,0:T(8,128)S(1)}, u32[]{:S(2)}, u32[]{:S(2)}) collective-permute-start(f32[64,256]{1,0:T(8,128)S(1)} %convolution_subtract_fusion.9), channel_id=1, source_target_pairs={{0,1},{1,0},{2,3},{3,2},{4,5},{5,4},{6,7},{7,6},{8,9},{9,8},{10,11... | collective-permute-start | bytes 196616 | tf_op jit(solution)/shard_map/ppermute | solution.py:16
  52.3 2.7 %fusion.11 = f32[256,256]{1,0:T(8,128)S(1)} fusion(f32[4,2048,256]{2,1,0:T(8,128)S(1)} %bitcast.125, f32[4,256,2048]{2,1,0:T(8,128)} %param.14), kind=kOutput, calls=%fused_computation.18 | convolution fusion | flops 805306368 | bytes 4456448 | tf_op jit(solution)/shard_map/dot_general | solution.py:11
  55.0 0.5 collective-permute-done.3
  55.6 0.3 collective-permute-start.4
  55.8 0.8 fusion.15
  56.6 0.5 collective-permute-done.4
  57.1 1.6 %collective-permute-start.5 = (f32[64,256]{1,0:T(8,128)S(1)}, f32[64,256]{1,0:T(8,128)S(1)}, u32[]{:S(2)}, u32[]{:S(2)}) collective-permute-start(f32[64,256]{1,0:T(8,128)S(1)} %add.63), channel_id=1, source_target_pairs={{0,4},{4,0},{1,5},{5,1},{2,6},{6,2},{3,7},{7,3},{8,12},{12,8},{9,1... | collective-permute-start | bytes 196616 | tf_op jit(solution)/shard_map/ppermute | solution.py:16
  58.7 0.2 convolution_subtract_fusion.8
  58.9 2.5 %collective-permute-done.5 = f32[64,256]{1,0:T(8,128)S(1)} collective-permute-done((f32[64,256]{1,0:T(8,128)S(1)}, f32[64,256]{1,0:T(8,128)S(1)}, u32[]{:S(2)}, u32[]{:S(2)}) %collective-permute-start.5) | collective-permute-done | bytes 65568 | tf_op jit(solution)/shard_map/ppermute | solution.py:16
  61.4 0.2 fusion.71
  61.7 0.2 convolution_add_fusion.2
  61.9 0.2 convolution_subtract_fusion.7
  62.1 1.3 %collective-permute-start.6 = (f32[64,256]{1,0:T(8,128)S(1)}, f32[64,256]{1,0:T(8,128)S(1)}, u32[]{:S(2)}, u32[]{:S(2)}) collective-permute-start(f32[64,256]{1,0:T(8,128)S(1)} %convolution_subtract_fusion.7), channel_id=1, source_target_pairs={{0,1},{1,0},{2,3},{3,2},{4,5},{5,4},{6,7},{7,6},{8,9},{9,8},{10,11... | collective-permute-start | bytes 196616 | tf_op jit(solution)/shard_map/ppermute | solution.py:16
  63.4 1.1 %fusion.1 = f32[256,256]{1,0:T(8,128)S(1)} fusion(f32[4,256,2048]{2,1,0:T(8,128)S(1)} %bitcast.127, f32[4,2048,256]{2,1,0:T(8,128)S(1)} %bitcast.125), kind=kOutput, calls=%fused_computation.8 | convolution fusion | flops 805306368 | bytes 4456448 | tf_op jit(solution)/shard_map/dot_general | solution.py:11
  64.5 1.9 %collective-permute-done.6 = f32[64,256]{1,0:T(8,128)S(1)} collective-permute-done((f32[64,256]{1,0:T(8,128)S(1)}, f32[64,256]{1,0:T(8,128)S(1)}, u32[]{:S(2)}, u32[]{:S(2)}) %collective-permute-start.6) | collective-permute-done | bytes 65568 | tf_op jit(solution)/shard_map/ppermute | solution.py:16
  66.5 0.8 fusion.7
  67.3 0.5 collective-permute-done.7
  67.8 1.6 %collective-permute-start.8 = (f32[64,256]{1,0:T(8,128)S(1)}, f32[64,256]{1,0:T(8,128)S(1)}, u32[]{:S(2)}, u32[]{:S(2)}) collective-permute-start(f32[64,256]{1,0:T(8,128)S(1)} %add.66), channel_id=1, source_target_pairs={{0,4},{4,0},{1,5},{5,1},{2,6},{6,2},{3,7},{7,3},{8,12},{12,8},{9,1... | collective-permute-start | bytes 196616 | tf_op jit(solution)/shard_map/ppermute | solution.py:16
  69.4 0.2 convolution_subtract_fusion.6
  69.6 2.6 %collective-permute-done.8 = f32[64,256]{1,0:T(8,128)S(1)} collective-permute-done((f32[64,256]{1,0:T(8,128)S(1)}, f32[64,256]{1,0:T(8,128)S(1)}, u32[]{:S(2)}, u32[]{:S(2)}) %collective-permute-start.8) | collective-permute-done | bytes 65568 | tf_op jit(solution)/shard_map/ppermute | solution.py:16
  72.2 2.8 %collective-permute-start.9 = (f32[64,256]{1,0:T(8,128)S(1)}, f32[64,256]{1,0:T(8,128)S(1)}, u32[]{:S(2)}, u32[]{:S(2)}) collective-permute-start(f32[64,256]{1,0:T(8,128)S(1)} %add.67), channel_id=1, source_target_pairs={{0,12},{4,8},{8,4},{12,0},{1,13},{5,9},{9,5},{13,1},{2,14},{6,10},... | collective-permute-start | bytes 196616 | tf_op jit(solution)/shard_map/ppermute | solution.py:16
  75.0 0.2 convolution_subtract_fusion.5
  75.2 2.5 %collective-permute-done.9 = f32[64,256]{1,0:T(8,128)S(1)} collective-permute-done((f32[64,256]{1,0:T(8,128)S(1)}, f32[64,256]{1,0:T(8,128)S(1)}, u32[]{:S(2)}, u32[]{:S(2)}) %collective-permute-start.9) | collective-permute-done | bytes 65568 | tf_op jit(solution)/shard_map/ppermute | solution.py:16
  77.7 0.2 fusion.68
  77.9 0.2 convolution_add_fusion.1
  78.2 0.2 convolution_subtract_fusion.4
  78.4 1.3 %collective-permute-start.10 = (f32[64,256]{1,0:T(8,128)S(1)}, f32[64,256]{1,0:T(8,128)S(1)}, u32[]{:S(2)}, u32[]{:S(2)}) collective-permute-start(f32[64,256]{1,0:T(8,128)S(1)} %convolution_subtract_fusion.4), channel_id=1, source_target_pairs={{0,1},{1,0},{2,3},{3,2},{4,5},{5,4},{6,7},{7,6},{8,9},{9,8},{10,11... | collective-permute-start | bytes 196616 | tf_op jit(solution)/shard_map/ppermute | solution.py:16
  79.7 3.1 %collective-permute-done.10 = f32[64,256]{1,0:T(8,128)S(1)} collective-permute-done((f32[64,256]{1,0:T(8,128)S(1)}, f32[64,256]{1,0:T(8,128)S(1)}, u32[]{:S(2)}, u32[]{:S(2)}) %collective-permute-start.10) | collective-permute-done | bytes 65568 | tf_op jit(solution)/shard_map/ppermute | solution.py:16
  82.8 1.2 %collective-permute-done.11 = f32[64,256]{1,0:T(8,128)S(1)} collective-permute-done((f32[64,256]{1,0:T(8,128)S(1)}, f32[64,256]{1,0:T(8,128)S(1)}, u32[]{:S(2)}, u32[]{:S(2)}) %collective-permute-start.11) | collective-permute-done | bytes 65568 | tf_op jit(solution)/shard_map/ppermute | solution.py:16
  84.1 0.4 collective-permute-start.12
  84.4 0.8 convolution_subtract_fusion.3
  85.3 3.1 %collective-permute-done.12 = f32[64,256]{1,0:T(8,128)S(1)} collective-permute-done((f32[64,256]{1,0:T(8,128)S(1)}, f32[64,256]{1,0:T(8,128)S(1)}, u32[]{:S(2)}, u32[]{:S(2)}) %collective-permute-start.12) | collective-permute-done | bytes 65568 | tf_op jit(solution)/shard_map/ppermute | solution.py:16
  88.4 2.8 %collective-permute-start.13 = (f32[64,256]{1,0:T(8,128)S(1)}, f32[64,256]{1,0:T(8,128)S(1)}, u32[]{:S(2)}, u32[]{:S(2)}) collective-permute-start(f32[64,256]{1,0:T(8,128)S(1)} %add.71), channel_id=1, source_target_pairs={{0,12},{4,8},{8,4},{12,0},{1,13},{5,9},{9,5},{13,1},{2,14},{6,10},... | collective-permute-start | bytes 196616 | tf_op jit(solution)/shard_map/ppermute | solution.py:16
  91.3 0.8 convolution_subtract_fusion.2
  92.1 1.9 %collective-permute-done.13 = f32[64,256]{1,0:T(8,128)S(1)} collective-permute-done((f32[64,256]{1,0:T(8,128)S(1)}, f32[64,256]{1,0:T(8,128)S(1)}, u32[]{:S(2)}, u32[]{:S(2)}) %collective-permute-start.13) | collective-permute-done | bytes 65568 | tf_op jit(solution)/shard_map/ppermute | solution.py:16
  94.0 2.7 %collective-permute-start.14 = (f32[64,256]{1,0:T(8,128)S(1)}, f32[64,256]{1,0:T(8,128)S(1)}, u32[]{:S(2)}, u32[]{:S(2)}) collective-permute-start(f32[64,256]{1,0:T(8,128)S(1)} %add.72), channel_id=1, source_target_pairs={{0,17},{1,16},{2,19},{3,18},{4,21},{5,20},{6,23},{7,22},{8,25},{9,... | collective-permute-start | bytes 196616 | tf_op jit(solution)/shard_map/ppermute | solution.py:16
  96.7 0.8 convolution_subtract_fusion.1
  97.6 2.0 %collective-permute-done.14 = f32[64,256]{1,0:T(8,128)S(1)} collective-permute-done((f32[64,256]{1,0:T(8,128)S(1)}, f32[64,256]{1,0:T(8,128)S(1)}, u32[]{:S(2)}, u32[]{:S(2)}) %collective-permute-start.14) | collective-permute-done | bytes 65568 | tf_op jit(solution)/shard_map/ppermute | solution.py:16
  99.6 0.2 fusion.65
  99.8 0.2 convolution_add_fusion
  100.0 1.6 %convolution_subtract_fusion = f32[64,2048]{1,0:T(8,128)} fusion(f32[64,2048]{1,0:T(8,128)S(1)} %convolution_subtract_fusion.1, f32[64,256]{1,0:T(8,128)S(1)} %convolution_add_fusion, f32[4,256,2048]{2,1,0:T(8,128)S(1)} %bitcast.127), kind=kOutput, calls=%fused_computation.2 | convolution fusion | flops 201457664 | bytes 3211264 | tf_op jit(solution)/shard_map/dot_general | solution.py:11
  (36 shorter events, 0.6 us)
Async XLA Ops:
  0.0 14.7 %collective-permute-start = (f32[64,2048]{1,0:T(8,128)}, f32[64,2048]{1,0:T(8,128)S(1)}, u32[]{:S(2)}, u32[]{:S(2)}) collective-permute-start(f32[64,2048]{1,0:T(8,128)} %param.8), channel_id=1, source_target_pairs={{0,1},{1,0},{2,3},{3,2},{4,5},{5,4},{6,7},{7,6},{8,9},{9,8},{10,11... | collective-permute-start | bytes 1572872 | tf_op jit(solution)/shard_map/ppermute | solution.py:16
  7.8 3.3 %copy-start.1 = (s32[16,4]{0,1:T(4,128)S(1)}, s32[16,4]{0,1:T(4,128)}, u32[]{:S(2)}) copy-start(s32[16,4]{0,1:T(4,128)} %param.11) | copy-start | bytes 772
  7.8 3.5 %copy-start.2 = (s32[16]{0:T(128)S(1)}, s32[16]{0:T(128)}, u32[]{:S(2)}) copy-start(s32[16]{0:T(128)} %param.12) | copy-start | bytes 196
  37.1 15.2 %slice-start = ((s8[8388608]{0:T(1024)(128)(4,1)}), s8[4194304]{0:T(1024)(128)(4,1)S(1)}, s32[]{:S(2)}) async-start(s8[8388608]{0:T(1024)(128)(4,1)} %bitcast.124), calls=%async_computation | async-start | bytes 8388608
  41.0 11.2 %slice-start.1 = ((s8[8388608]{0:T(1024)(128)(4,1)}), s8[4194304]{0:T(1024)(128)(4,1)S(1)}, s32[]{:S(2)}) async-start(s8[8388608]{0:T(1024)(128)(4,1)} %bitcast.124), calls=%async_computation.1 | async-start | bytes 8388608
  43.5 6.8 %copy-start = (f32[1,4,2,256,256]{4,3,2,1,0:T(8,128)S(1)}, f32[1,4,2,256,256]{4,3,2,1,0:T(8,128)}, u32[]{:S(2)}) copy-start(f32[1,4,2,256,256]{4,3,2,1,0:T(8,128)} %param.15) | copy-start | bytes 6291460
  43.5 4.3 %collective-permute-start.1 = (f32[64,256]{1,0:T(8,128)S(1)}, f32[64,256]{1,0:T(8,128)S(1)}, u32[]{:S(2)}, u32[]{:S(2)}) collective-permute-start(f32[64,256]{1,0:T(8,128)S(1)} %fusion.28), channel_id=1, source_target_pairs={{0,1},{1,0},{2,3},{3,2},{4,5},{5,4},{6,7},{7,6},{8,9},{9,8},{10,11... | collective-permute-start | bytes 196616 | tf_op jit(solution)/shard_map/ppermute | solution.py:16
  44.4 19.0 %slice-start.2 = ((s8[8388608]{0:T(1024)(128)(4,1)}), s8[4194304]{0:T(1024)(128)(4,1)S(1)}, s32[]{:S(2)}) async-start(s8[8388608]{0:T(1024)(128)(4,1)} %bitcast.126), calls=%async_computation.2 | async-start | bytes 8388608
  47.9 2.4 %collective-permute-start.2 = (f32[64,256]{1,0:T(8,128)S(1)}, f32[64,256]{1,0:T(8,128)S(1)}, u32[]{:S(2)}, u32[]{:S(2)}) collective-permute-start(f32[64,256]{1,0:T(8,128)S(1)} %add.60), channel_id=1, source_target_pairs={{0,2},{2,0},{1,3},{3,1},{4,6},{6,4},{5,7},{7,5},{8,10},{10,8},{9,1... | collective-permute-start | bytes 196616 | tf_op jit(solution)/shard_map/ppermute | solution.py:16
  51.0 12.4 %slice-start.3 = ((s8[8388608]{0:T(1024)(128)(4,1)}), s8[4194304]{0:T(1024)(128)(4,1)S(1)}, s32[]{:S(2)}) async-start(s8[8388608]{0:T(1024)(128)(4,1)} %bitcast.126), calls=%async_computation.3 | async-start | bytes 8388608
  51.0 4.6 %collective-permute-start.3 = (f32[64,256]{1,0:T(8,128)S(1)}, f32[64,256]{1,0:T(8,128)S(1)}, u32[]{:S(2)}, u32[]{:S(2)}) collective-permute-start(f32[64,256]{1,0:T(8,128)S(1)} %convolution_subtract_fusion.9), channel_id=1, source_target_pairs={{0,1},{1,0},{2,3},{3,2},{4,5},{5,4},{6,7},{7,6},{8,9},{9,8},{10,11... | collective-permute-start | bytes 196616 | tf_op jit(solution)/shard_map/ppermute | solution.py:16
  55.6 1.5 %collective-permute-start.4 = (f32[64,256]{1,0:T(8,128)S(1)}, f32[64,256]{1,0:T(8,128)S(1)}, u32[]{:S(2)}, u32[]{:S(2)}) collective-permute-start(f32[64,256]{1,0:T(8,128)S(1)} %add.62), channel_id=1, source_target_pairs={{0,2},{2,0},{1,3},{3,1},{4,6},{6,4},{5,7},{7,5},{8,10},{10,8},{9,1... | collective-permute-start | bytes 196616 | tf_op jit(solution)/shard_map/ppermute | solution.py:16
  57.1 4.3 %collective-permute-start.5 = (f32[64,256]{1,0:T(8,128)S(1)}, f32[64,256]{1,0:T(8,128)S(1)}, u32[]{:S(2)}, u32[]{:S(2)}) collective-permute-start(f32[64,256]{1,0:T(8,128)S(1)} %add.63), channel_id=1, source_target_pairs={{0,4},{4,0},{1,5},{5,1},{2,6},{6,2},{3,7},{7,3},{8,12},{12,8},{9,1... | collective-permute-start | bytes 196616 | tf_op jit(solution)/shard_map/ppermute | solution.py:16
  62.1 4.3 %collective-permute-start.6 = (f32[64,256]{1,0:T(8,128)S(1)}, f32[64,256]{1,0:T(8,128)S(1)}, u32[]{:S(2)}, u32[]{:S(2)}) collective-permute-start(f32[64,256]{1,0:T(8,128)S(1)} %convolution_subtract_fusion.7), channel_id=1, source_target_pairs={{0,1},{1,0},{2,3},{3,2},{4,5},{5,4},{6,7},{7,6},{8,9},{9,8},{10,11... | collective-permute-start | bytes 196616 | tf_op jit(solution)/shard_map/ppermute | solution.py:16
  66.5 1.3 %collective-permute-start.7 = (f32[64,256]{1,0:T(8,128)S(1)}, f32[64,256]{1,0:T(8,128)S(1)}, u32[]{:S(2)}, u32[]{:S(2)}) collective-permute-start(f32[64,256]{1,0:T(8,128)S(1)} %add.65), channel_id=1, source_target_pairs={{0,2},{2,0},{1,3},{3,1},{4,6},{6,4},{5,7},{7,5},{8,10},{10,8},{9,1... | collective-permute-start | bytes 196616 | tf_op jit(solution)/shard_map/ppermute | solution.py:16
  67.8 4.3 %collective-permute-start.8 = (f32[64,256]{1,0:T(8,128)S(1)}, f32[64,256]{1,0:T(8,128)S(1)}, u32[]{:S(2)}, u32[]{:S(2)}) collective-permute-start(f32[64,256]{1,0:T(8,128)S(1)} %add.66), channel_id=1, source_target_pairs={{0,4},{4,0},{1,5},{5,1},{2,6},{6,2},{3,7},{7,3},{8,12},{12,8},{9,1... | collective-permute-start | bytes 196616 | tf_op jit(solution)/shard_map/ppermute | solution.py:16
  72.2 5.6 %collective-permute-start.9 = (f32[64,256]{1,0:T(8,128)S(1)}, f32[64,256]{1,0:T(8,128)S(1)}, u32[]{:S(2)}, u32[]{:S(2)}) collective-permute-start(f32[64,256]{1,0:T(8,128)S(1)} %add.67), channel_id=1, source_target_pairs={{0,12},{4,8},{8,4},{12,0},{1,13},{5,9},{9,5},{13,1},{2,14},{6,10},... | collective-permute-start | bytes 196616 | tf_op jit(solution)/shard_map/ppermute | solution.py:16
  78.4 4.3 %collective-permute-start.10 = (f32[64,256]{1,0:T(8,128)S(1)}, f32[64,256]{1,0:T(8,128)S(1)}, u32[]{:S(2)}, u32[]{:S(2)}) collective-permute-start(f32[64,256]{1,0:T(8,128)S(1)} %convolution_subtract_fusion.4), channel_id=1, source_target_pairs={{0,1},{1,0},{2,3},{3,2},{4,5},{5,4},{6,7},{7,6},{8,9},{9,8},{10,11... | collective-permute-start | bytes 196616 | tf_op jit(solution)/shard_map/ppermute | solution.py:16
  82.7 1.3 %collective-permute-start.11 = (f32[64,256]{1,0:T(8,128)S(1)}, f32[64,256]{1,0:T(8,128)S(1)}, u32[]{:S(2)}, u32[]{:S(2)}) collective-permute-start(f32[64,256]{1,0:T(8,128)S(1)} %add.69), channel_id=1, source_target_pairs={{0,2},{2,0},{1,3},{3,1},{4,6},{6,4},{5,7},{7,5},{8,10},{10,8},{9,1... | collective-permute-start | bytes 196616 | tf_op jit(solution)/shard_map/ppermute | solution.py:16
  84.1 4.3 %collective-permute-start.12 = (f32[64,256]{1,0:T(8,128)S(1)}, f32[64,256]{1,0:T(8,128)S(1)}, u32[]{:S(2)}, u32[]{:S(2)}) collective-permute-start(f32[64,256]{1,0:T(8,128)S(1)} %add.70), channel_id=1, source_target_pairs={{0,4},{4,0},{1,5},{5,1},{2,6},{6,2},{3,7},{7,3},{8,12},{12,8},{9,1... | collective-permute-start | bytes 196616 | tf_op jit(solution)/shard_map/ppermute | solution.py:16
  88.4 5.6 %collective-permute-start.13 = (f32[64,256]{1,0:T(8,128)S(1)}, f32[64,256]{1,0:T(8,128)S(1)}, u32[]{:S(2)}, u32[]{:S(2)}) collective-permute-start(f32[64,256]{1,0:T(8,128)S(1)} %add.71), channel_id=1, source_target_pairs={{0,12},{4,8},{8,4},{12,0},{1,13},{5,9},{9,5},{13,1},{2,14},{6,10},... | collective-permute-start | bytes 196616 | tf_op jit(solution)/shard_map/ppermute | solution.py:16
  94.0 5.6 %collective-permute-start.14 = (f32[64,256]{1,0:T(8,128)S(1)}, f32[64,256]{1,0:T(8,128)S(1)}, u32[]{:S(2)}, u32[]{:S(2)}) collective-permute-start(f32[64,256]{1,0:T(8,128)S(1)} %add.72), channel_id=1, source_target_pairs={{0,17},{1,16},{2,19},{3,18},{4,21},{5,20},{6,23},{7,22},{8,25},{9,... | collective-permute-start | bytes 196616 | tf_op jit(solution)/shard_map/ppermute | solution.py:16

commit v3 on v2

v3 whole, which is shorter than its diff:
```python
import jax
import jax.numpy as jnp
from jax import lax
from jax.experimental import pallas as pl
from jax.experimental.pallas import tpu as pltpu
from jax.sharding import Mesh, PartitionSpec as P

AXES = ("z", "y", "x1", "x0", "core", "rhs")
FAST = lax.Precision.HIGH


def dot(a, b):
    return jnp.dot(a, b, precision=FAST, preferred_element_type=jnp.float32)


def swap(block, axes, mask):
    count = lax.axis_size(axes)
    return lax.ppermute(block, axes, [(i, i ^ mask) for i in range(count)])


def over_rhs(block):
    return swap(block, ("rhs",), 1)


RING = ("y", "x1", "x0", "core", "rhs")


def mm(a, b):
    return jnp.dot(a, b, preferred_element_type=jnp.float32)

def parts(value):
    high = value.astype(jnp.bfloat16)
    low = (value - high.astype(jnp.float32)).astype(jnp.bfloat16)
    return high, low

def stacked(value):
    high, low = parts(value)
    return jnp.concatenate([high, low], axis=0)

def near_kernel(order, index, count, side, own, other, tiles_hbm, proj_hbm, current, reduced,
                source, gathered, operand, tiles, proj, needed, tile_sem, proj_sem):
    rows, half = own.shape
    size = tiles.shape[-1]
    slots = index.shape[1]
    leaf_tiles = operand.shape[0]
    out_tiles = tiles.shape[0]
    load_tiles = pltpu.make_async_copy(tiles_hbm, tiles, tile_sem)
    load_tiles.start()
    load_proj = pltpu.make_async_copy(proj_hbm.at[0], proj, proj_sem)
    load_proj.start()
    own_start = side[0] * half
    other_start = half - own_start
    for block, start in ((own, own_start), (other, other_start)):
        for c in range(half // size):
            at = pl.multiple_of(start + c * size, size)
            source[pl.ds(at, size), :] = block[:, c * size:(c + 1) * size].T

    for tile in range(leaf_tiles):
        needed[tile] = 0
    def mark(t, _):
        for slot in range(slots):
            @pl.when(slot < count[t])
            def _():
                needed[index[t, slot]] = 1
        return 0
    lax.fori_loop(0, out_tiles, mark, 0)

    def gather(tile, _):
        @pl.when(needed[tile] == 1)
        def _():
            def rows_of(step, _):
                base = tile * size + step * 16
                for u in range(16):
                    gathered[pl.ds(step * 16 + u, 1), :] = source[pl.ds(order[base + u], 1), :]
                return 0
            lax.fori_loop(0, size // 16, rows_of, 0)
            operand[tile] = stacked(gathered[...].T)
        return 0
    lax.fori_loop(0, leaf_tiles, gather, 0)

    load_tiles.wait()
    def near(t, _):
        pieces = []
        for slot in range(slots):
            live = slot < count[t]
            picked = operand[jnp.where(live, index[t, slot], index[t, 0])]
            pieces.append(jnp.where(live, picked, jnp.zeros_like(picked)))
        left = jnp.concatenate(pieces, axis=1)
        high, low = parts(tiles[t].reshape(slots * size, size))
        both = mm(left, high)
        out = both[:rows] + both[rows:] + mm(left[:rows], low)
        current[:, pl.ds(pl.multiple_of(t * size, size), size)] = out
        return 0
    lax.fori_loop(0, out_tiles, near, 0, unroll=4)
    load_proj.wait()
    total = jnp.zeros(reduced.shape, jnp.float32)
    for c in range(half // 256):
        left = stacked(current[:, c * 256:(c + 1) * 256])
        high, low = parts(proj[c * 256:(c + 1) * 256, :])
        both = mm(left, high)
        total = total + (both[:rows] + both[rows:] + mm(left[:rows], low))
    reduced[...] = total

def near_call(order, index, count, side, own, other, tiles, proj):
    rows, half = own.shape
    out_tiles, slots, size, _ = tiles.shape
    rank = proj.shape[-1]
    smem = pl.BlockSpec(memory_space=pltpu.SMEM)
    vmem = pl.BlockSpec(memory_space=pltpu.VMEM)
    hbm = pl.BlockSpec(memory_space=pl.ANY)
    return pl.pallas_call(
        near_kernel,
        out_shape=(jax.ShapeDtypeStruct((rows, half), jnp.float32), jax.ShapeDtypeStruct((rows, rank), jnp.float32)),
        in_specs=[smem, smem, smem, smem, vmem, vmem, hbm, hbm],
        out_specs=(vmem, vmem),
        scratch_shapes=[
            pltpu.VMEM((order.shape[0], rows), jnp.float32),
            pltpu.VMEM((size, rows), jnp.float32),
            pltpu.VMEM((order.shape[0] // size, 2 * rows, size), jnp.bfloat16),
            pltpu.VMEM(tiles.shape, jnp.float32),
            pltpu.VMEM((half, rank), jnp.float32),
            pltpu.SMEM((order.shape[0] // size,), jnp.int32),
            pltpu.SemaphoreType.DMA,
            pltpu.SemaphoreType.DMA,
        ],
        compiler_params=pltpu.CompilerParams(vmem_limit_bytes=54 << 20),
        cost_estimate=pl.CostEstimate(flops=200_000_000, bytes_accessed=8 << 20, transcendentals=0),
        name="near",
    )(order, index, count, side, own, other, tiles, proj)

def gram_kernel(corr_hbm, proj_hbm, *rest):
    levels, points, rank = proj_hbm.shape
    pairs = levels * (levels - 1) // 2
    grams = rest[:pairs]
    corr, proj, sems = rest[pairs:]
    loads = {}
    for level in range(levels - 1):
        loads["c", level] = pltpu.make_async_copy(corr_hbm.at[level], corr.at[level], sems.at[level])
        loads["p", level] = pltpu.make_async_copy(
            proj_hbm.at[level + 1], proj.at[level], sems.at[levels - 1 + level])
        loads["c", level].start()
        loads["p", level].start()
    lefts = []
    for above in range(levels - 1):
        loads["c", above].wait()
        left_high, left_low = parts(corr[above])
        lefts.append((left_high, left_low))
        loads["p", above].wait()
        high, low = parts(proj[above])
        for below in range(above + 1):
            left_high, left_low = lefts[below]
            grams[above * (above + 1) // 2 + below][...] = (
                mm(left_high, high) + mm(left_high, low) + mm(left_low, high))

def gram_call(corr, proj):
    levels, points, rank = proj.shape
    pairs = levels * (levels - 1) // 2
    hbm = pl.BlockSpec(memory_space=pl.ANY)
    vmem = pl.BlockSpec(memory_space=pltpu.VMEM)
    return pl.pallas_call(
        gram_kernel,
        out_shape=[jax.ShapeDtypeStruct((rank, rank), jnp.float32)] * pairs,
        in_specs=[hbm, hbm],
        out_specs=[vmem] * pairs,
        scratch_shapes=[
            pltpu.VMEM((levels - 1, rank, points), jnp.float32),
            pltpu.VMEM((levels - 1, points, rank), jnp.float32),
            pltpu.SemaphoreType.DMA((2 * levels - 2,)),
        ],
        compiler_params=pltpu.CompilerParams(vmem_limit_bytes=54 << 20),
        cost_estimate=pl.CostEstimate(
            flops=6 * pairs * points * rank * rank, bytes_accessed=12 << 20, transcendentals=0),
        name="gram",
    )(corr, proj)


def local(
    charges, cluster_order, near_tiles, near_index, near_count, proj_basis, corr_basis, coupling
):
    levels = proj_basis.shape[0]
    other = over_rhs(charges)
    grams = gram_call(corr_basis, proj_basis)
    other, grams = lax.optimization_barrier((other, grams))
    side = lax.axis_index("rhs").astype(jnp.int32).reshape(1)
    current, first = near_call(
        cluster_order, near_index, near_count, side, charges, other, near_tiles, proj_basis
    )
    reduced = [first] + [dot(current, proj_basis[height]) for height in range(1, levels)]
    for height in range(levels):
        own_sum = reduced[height]
        if height < 3:
            own_sum = own_sum + over_rhs(own_sum)
        if height > 0:
            own_sum = own_sum + swap(own_sum, ("core",), 1)
        if height == 0:
            sib_sum = swap(own_sum, ("core",), 1)
        elif height == 1:
            sib_sum = swap(own_sum, ("x0",), 1)
        else:
            near, far, across = (swap(own_sum, ("x1", "x0"), mask) for mask in (1, 3, 2))
            own_sum = own_sum + near
            sib_sum = far + across
        if height == 3:
            own_sum = own_sum + sib_sum
            near, far, across = (swap(own_sum, RING, mask) for mask in (1, 17, 16))
            own_sum = own_sum + near
            sib_sum = far + across
        coeff = dot(own_sum, coupling[0, height, 0]) + dot(sib_sum, coupling[0, height, 1])
        for high in range(height + 1, levels):
            pair = high * (high - 1) // 2 + height
            reduced[high] = reduced[high] - dot(coeff, grams[pair])
        current = current - dot(coeff, corr_basis[height])
    return current


def solution(mesh):
    split = Mesh(mesh.devices.reshape(-1, 2, 2, 2, 2, 2), AXES)
    every = AXES
    leaf = AXES[:-1]
    return jax.shard_map(
        local,
        mesh=split,
        in_specs=(
            P(None, every),
            P(leaf),
            P(every, None, None, None),
            P(every, None),
            P(every),
            P(None, every, None),
            P(None, None, every),
            P(leaf, None, None, None, None),
        ),
        out_specs=P(None, every),
        check_vma=False,
    )
```

time: 102 us -> 82.2 us (0.81)
  matrix products: 34.5 us -> 11.7 us
  Pallas kernels: 0 us -> 21.5 us
  local copies, waits for them, and re-layouts: 21.7 us -> 2.21 us
  other arithmetic: 3.85 us -> 0.97 us
  starting transfers between devices: 18.9 us -> 20.9 us
  waiting for transfers between devices: 22.3 us -> 24.2 us
    pallas_call x0 -> x2, Pallas kernels: none -> 21.5 us  [the longest x1 10.8 us: near_call(): pl.pallas_call(near_kernel, out_shape=(jax.ShapeDtypeStruct((rows, half),...]
    gather x3 -> x0, local copies, waits for them, and re-layouts: 19.8 us -> none  [the longest x1 14.2 us: local(): ordered = jnp.take(leaf_charges, cluster_order, axis=1)]
    dot_general x28 -> x21, matrix products: 30.6 us -> 11.7 us  [dot(): return jnp.dot(a, b, precision=FAST, preferred_element_type=jnp.float32)]
    dot_general x1 -> x0, matrix products: 3.95 us -> none  [local(): current = jnp.einsum('rtki,tkio->rto', picked, near_tiles, precision=FAST)]
    ppermute x15 -> x18, starting transfers between devices: 18.9 us -> 20.9 us  [swap(): return lax.ppermute(block, axes, [(i, i ^ mask) for i in range(count)])]
    select_n x3 -> x0, other arithmetic: 2.08 us -> none  [the longest x1 1.93 us: local(): ordered = jnp.take(leaf_charges, cluster_order, axis=1)]
    ppermute x15 -> x18, waiting for transfers between devices: 22.3 us -> 24.2 us  [swap(): return lax.ppermute(block, axes, [(i, i ^ mask) for i in range(count)])]
    unnamed x15 -> x25, local copies, waits for them, and re-layouts: 1.45 us -> 2.21 us
  transfers between devices with their start and end apart: 15 -> 18, of which waited for: 12 -> 13; matrix products, arithmetic and copies ran while one was open for 27% -> 11% of each run, Pallas kernels for 0% -> 13%
where the time goes in v3:
time: 82.2 us; the launch traced here: 82 us
  waiting for transfers between devices  24.2 us (29%)
  Pallas kernels  21.5 us (26%)
  starting transfers between devices  20.9 us (25%)
  matrix products  11.7 us (14%)
  local copies, waits for them, and re-layouts  2.21 us (3%)
  other arithmetic  0.97 us (1%)
    ppermute x18, waiting for transfers between devices, swap(): return lax.ppermute(block, axes, [(i, i ^ mask) for i in range(count)])  24.2 us
    ppermute x18, starting transfers between devices, swap(): return lax.ppermute(block, axes, [(i, i ^ mask) for i in range(count)])  20.9 us
    dot_general x21, matrix products, dot(): return jnp.dot(a, b, precision=FAST, preferred_element_type=jnp.float32)  11.7 us
    pallas_call x1, Pallas kernels, near_call(): pl.pallas_call(near_kernel, out_shape=(jax.ShapeDtypeStruct((rows, half),...  10.8 us
    pallas_call x1, Pallas kernels, gram_call(): pl.pallas_call(gram_kernel, out_shape=[jax.ShapeDtypeStruct((rank, rank),...  10.7 us
    unnamed x25, local copies, waits for them, and re-layouts  2.21 us
  transfers between devices with their start and end apart: 18, of which 13 were waited for; matrix products, arithmetic and copies ran while one was open for 11% of the time, Pallas kernels for 13%

profile of v3, /device:TPU:0, one launch (start us, length us, event | category | flops | bytes accessed | tf_op | source)
XLA Modules:
  0.0 82.0 jit_solution(4184138198413371078)
XLA Ops:
  0.0 1.7 %collective-permute-start = (f32[64,2048]{1,0:T(8,128)}, f32[64,2048]{1,0:T(8,128)S(1)}, u32[]{:S(2)}, u32[]{:S(2)}) collective-permute-start(f32[64,2048]{1,0:T(8,128)} %own.1), channel_id=1, source_target_pairs={{0,1},{1,0},{2,3},{3,2},{4,5},{5,4},{6,7},{7,6},{8,9},{9,8},{10,11... | collective-permute-start | bytes 1572872 | tf_op jit(solution)/shard_map/ppermute | solution.py:18
  1.7 1.4 %copy.9.index = s32[16,4]{1,0:T(8,128)} copy(s32[16,4]{0,1:T(4,128)} %param.11) | data formatting | bytes 512 | tf_op args[3]
  3.0 10.7 %gram.1 = (f32[256,256]{1,0:T(8,128)}, f32[256,256]{1,0:T(8,128)}, f32[256,256]{1,0:T(8,128)}, f32[256,256]{1,0:T(8,128)}, f32[256,256]{1,0:T(8,128)}, /*index=5*/f32[256,256]{1,0:T(8,128)}) custom-call(f32[4,256,2048]{2,1,0:T(8,128)} %corr_hbm.1, f32[4,2048,256]{2,1,0:T(8,128)} %proj_hbm.3), custom_call_target="tpu_custom_call" | custom-call | flops 4831838208 | bytes 12582912 | tf_op jit(solution)/shard_map/gram/pallas_call | solution.py:160
  13.7 0.0 collective-permute-done.other
  13.8 0.8 copy-done.3
  14.6 10.8 %near.1 = (f32[64,2048]{1,0:T(8,128)}, f32[64,256]{1,0:T(8,128)}) custom-call(s32[4096]{0:T(1024)} %order.1, s32[16,4]{1,0:T(8,128)} %copy.9.index, s32[16]{0:T(128)} %count.1, s32[1]{0:T(128)} %bitcast.side, f32[64,2048]{1,0:T(8,128)} %own.1, f32[64,2048]{1,0:T(8,128)} %copy-done.3, f32[16,4,128,128]{3,2,1,0:T(8,128)} %tiles_hbm.1, f32[4,2048,256]{2,1,0:T(8,128)} %proj_hbm.3), custom_call_target="tpu_custom_call" | custom-call | flops 200000000 | bytes 8388608 | tf_op jit(solution)/shard_map/near/pallas_call | solution.py:111
  25.4 0.0 copy-start.2
  25.4 1.6 %collective-permute-start.1 = (f32[64,256]{1,0:T(8,128)}, f32[64,256]{1,0:T(8,128)S(1)}, u32[]{:S(2)}, u32[]{:S(2)}) collective-permute-start(f32[64,256]{1,0:T(8,128)} %get-tuple-element.28), channel_id=1, source_target_pairs={{0,1},{1,0},{2,3},{3,2},{4,5},{5,4},{6,7},{7,6},{8,9},{9,8},{10,11... | collective-permute-start | bytes 196616 | tf_op jit(solution)/shard_map/ppermute | solution.py:18
  27.0 2.9 %collective-permute-done.1 = f32[64,256]{1,0:T(8,128)S(1)} collective-permute-done((f32[64,256]{1,0:T(8,128)}, f32[64,256]{1,0:T(8,128)S(1)}, u32[]{:S(2)}, u32[]{:S(2)}) %collective-permute-start.1) | collective-permute-done | bytes 65568 | tf_op jit(solution)/shard_map/ppermute | solution.py:18
  30.0 0.9 %add.51 = f32[64,256]{1,0:T(8,128)S(1)} add(f32[64,256]{1,0:T(8,128)} %get-tuple-element.28, f32[64,256]{1,0:T(8,128)S(1)} %collective-permute-done.1) | non-fusion elementwise | flops 16384 | bytes 196608 | tf_op jit(solution)/shard_map/add | solution.py:192
  30.9 0.1 collective-permute-start.2
  31.0 0.0 slice-start
  31.0 1.9 %fusion.7 = f32[64,256]{1,0:T(8,128)S(1)} fusion(f32[64,2048]{1,0:T(8,128)} %get-tuple-element.27, f32[4,2048,256]{2,1,0:T(8,128)S(1)} %copy-done), kind=kOutput, calls=%fused_computation.11 | convolution fusion | flops 201326592 | bytes 2686976 | tf_op jit(solution)/shard_map/dot_general | solution.py:13
  32.9 0.0 collective-permute-done.2
  32.9 0.2 fusion.27
  33.2 0.2 convolution_add_fusion.3
  33.4 0.2 convolution_subtract_fusion.8
  33.6 1.6 %collective-permute-start.3 = (f32[64,256]{1,0:T(8,128)S(1)}, f32[64,256]{1,0:T(8,128)S(1)}, u32[]{:S(2)}, u32[]{:S(2)}) collective-permute-start(f32[64,256]{1,0:T(8,128)S(1)} %convolution_subtract_fusion.8), channel_id=1, source_target_pairs={{0,1},{1,0},{2,3},{3,2},{4,5},{5,4},{6,7},{7,6},{8,9},{9,8},{10,11... | collective-permute-start | bytes 196616 | tf_op jit(solution)/shard_map/ppermute | solution.py:18
  35.2 2.9 %collective-permute-done.3 = f32[64,256]{1,0:T(8,128)S(1)} collective-permute-done((f32[64,256]{1,0:T(8,128)S(1)}, f32[64,256]{1,0:T(8,128)S(1)}, u32[]{:S(2)}, u32[]{:S(2)}) %collective-permute-start.3) | collective-permute-done | bytes 65568 | tf_op jit(solution)/shard_map/ppermute | solution.py:18
  38.2 0.1 collective-permute-start.4
  38.3 0.7 fusion.4
  39.0 0.5 collective-permute-done.4
  39.5 1.5 %collective-permute-start.5 = (f32[64,256]{1,0:T(8,128)S(1)}, f32[64,256]{1,0:T(8,128)S(1)}, u32[]{:S(2)}, u32[]{:S(2)}) collective-permute-start(f32[64,256]{1,0:T(8,128)S(1)} %add.54), channel_id=1, source_target_pairs={{0,4},{4,0},{1,5},{5,1},{2,6},{6,2},{3,7},{7,3},{8,12},{12,8},{9,1... | collective-permute-start | bytes 196616 | tf_op jit(solution)/shard_map/ppermute | solution.py:18
  41.0 0.2 convolution_subtract_fusion.7
  41.3 2.6 %collective-permute-done.5 = f32[64,256]{1,0:T(8,128)S(1)} collective-permute-done((f32[64,256]{1,0:T(8,128)S(1)}, f32[64,256]{1,0:T(8,128)S(1)}, u32[]{:S(2)}, u32[]{:S(2)}) %collective-permute-start.5) | collective-permute-done | bytes 65568 | tf_op jit(solution)/shard_map/ppermute | solution.py:18
  43.9 0.2 fusion.24
  44.1 0.2 convolution_add_fusion.2
  44.3 0.2 convolution_subtract_fusion.6
  44.5 0.0 slice-start.1
  44.6 1.6 %collective-permute-start.6 = (f32[64,256]{1,0:T(8,128)S(1)}, f32[64,256]{1,0:T(8,128)S(1)}, u32[]{:S(2)}, u32[]{:S(2)}) collective-permute-start(f32[64,256]{1,0:T(8,128)S(1)} %convolution_subtract_fusion.6), channel_id=1, source_target_pairs={{0,1},{1,0},{2,3},{3,2},{4,5},{5,4},{6,7},{7,6},{8,9},{9,8},{10,11... | collective-permute-start | bytes 196616 | tf_op jit(solution)/shard_map/ppermute | solution.py:18
  46.2 2.7 %collective-permute-done.6 = f32[64,256]{1,0:T(8,128)S(1)} collective-permute-done((f32[64,256]{1,0:T(8,128)S(1)}, f32[64,256]{1,0:T(8,128)S(1)}, u32[]{:S(2)}, u32[]{:S(2)}) %collective-permute-start.6) | collective-permute-done | bytes 65568 | tf_op jit(solution)/shard_map/ppermute | solution.py:18
  48.9 0.1 collective-permute-start.7
  49.0 0.7 fusion.1
  49.7 0.5 collective-permute-done.7
  50.3 3.9 %collective-permute-start.10 = (f32[64,256]{1,0:T(8,128)S(1)}, f32[64,256]{1,0:T(8,128)S(1)}, u32[]{:S(2)}, u32[]{:S(2)}) collective-permute-start(f32[64,256]{1,0:T(8,128)S(1)} %add.57), channel_id=1, source_target_pairs={{0,8},{4,12},{8,0},{12,4},{1,9},{5,13},{9,1},{13,5},{2,10},{6,14},... | collective-permute-start | bytes 196616 | tf_op jit(solution)/shard_map/ppermute | solution.py:18
  54.2 0.4 collective-permute-start.9
  54.7 0.2 convolution_subtract_fusion.5
  54.9 0.1 collective-permute-start.8
  55.0 1.7 %collective-permute-done.10 = f32[64,256]{1,0:T(8,128)S(1)} collective-permute-done((f32[64,256]{1,0:T(8,128)S(1)}, f32[64,256]{1,0:T(8,128)S(1)}, u32[]{:S(2)}, u32[]{:S(2)}) %collective-permute-start.10) | collective-permute-done | bytes 65568 | tf_op jit(solution)/shard_map/ppermute | solution.py:18
  56.6 3.1 %collective-permute-done.9 = f32[64,256]{1,0:T(8,128)S(1)} collective-permute-done((f32[64,256]{1,0:T(8,128)S(1)}, f32[64,256]{1,0:T(8,128)S(1)}, u32[]{:S(2)}, u32[]{:S(2)}) %collective-permute-start.9) | collective-permute-done | bytes 65568 | tf_op jit(solution)/shard_map/ppermute | solution.py:18
  59.7 0.2 fusion.21
  59.9 0.0 collective-permute-done.8
  59.9 0.2 convolution_add_fusion.1
  60.2 0.2 fusion.42
  60.4 0.2 fusion.17
  60.6 0.1 collective-permute-start.11
  60.7 2.4 %convolution_subtract_fusion.3 = f32[64,2048]{1,0:T(8,128)S(1)} fusion(f32[64,2048]{1,0:T(8,128)S(1)} %copy-done.1, f32[64,256]{1,0:T(8,128)S(1)} %convolution_add_fusion.3, f32[4,256,2048]{2,1,0:T(8,128)} %corr_hbm.1), kind=kOutput, calls=%fused_computation.3 | convolution fusion | flops 201457664 | bytes 3211264 | tf_op jit(solution)/shard_map/dot_general | solution.py:13
  63.1 1.6 %collective-permute-start.14 = (f32[64,256]{1,0:T(8,128)S(1)}, f32[64,256]{1,0:T(8,128)S(1)}, u32[]{:S(2)}, u32[]{:S(2)}) collective-permute-start(f32[64,256]{1,0:T(8,128)S(1)} %add.61), channel_id=1, source_target_pairs={{0,8},{4,12},{8,0},{12,4},{1,9},{5,13},{9,1},{13,5},{2,10},{6,14},... | collective-permute-start | bytes 196616 | tf_op jit(solution)/shard_map/ppermute | solution.py:18
  64.7 1.0 %collective-permute-start.13 = (f32[64,256]{1,0:T(8,128)S(1)}, f32[64,256]{1,0:T(8,128)S(1)}, u32[]{:S(2)}, u32[]{:S(2)}) collective-permute-start(f32[64,256]{1,0:T(8,128)S(1)} %add.61), channel_id=1, source_target_pairs={{0,12},{4,8},{8,4},{12,0},{1,13},{5,9},{9,5},{13,1},{2,14},{6,10},... | collective-permute-start | bytes 196616 | tf_op jit(solution)/shard_map/ppermute | solution.py:18
  65.7 1.0 %collective-permute-start.12 = (f32[64,256]{1,0:T(8,128)S(1)}, f32[64,256]{1,0:T(8,128)S(1)}, u32[]{:S(2)}, u32[]{:S(2)}) collective-permute-start(f32[64,256]{1,0:T(8,128)S(1)} %add.61), channel_id=1, source_target_pairs={{0,4},{4,0},{8,12},{12,8},{1,5},{5,1},{9,13},{13,9},{2,6},{6,2},{1... | collective-permute-start | bytes 196616 | tf_op jit(solution)/shard_map/ppermute | solution.py:18
  66.7 0.8 convolution_subtract_fusion.2
  67.4 1.8 %collective-permute-done.14 = f32[64,256]{1,0:T(8,128)S(1)} collective-permute-done((f32[64,256]{1,0:T(8,128)S(1)}, f32[64,256]{1,0:T(8,128)S(1)}, u32[]{:S(2)}, u32[]{:S(2)}) %collective-permute-start.14) | collective-permute-done | bytes 65568 | tf_op jit(solution)/shard_map/ppermute | solution.py:18
  69.2 1.4 %collective-permute-done.13 = f32[64,256]{1,0:T(8,128)S(1)} collective-permute-done((f32[64,256]{1,0:T(8,128)S(1)}, f32[64,256]{1,0:T(8,128)S(1)}, u32[]{:S(2)}, u32[]{:S(2)}) %collective-permute-start.13) | collective-permute-done | bytes 65568 | tf_op jit(solution)/shard_map/ppermute | solution.py:18
  70.6 0.0 collective-permute-done.12
  70.6 3.2 %collective-permute-start.17 = (f32[64,256]{1,0:T(8,128)S(1)}, f32[64,256]{1,0:T(8,128)S(1)}, u32[]{:S(2)}, u32[]{:S(2)}) collective-permute-start(f32[64,256]{1,0:T(8,128)S(1)} %add_add_fusion), channel_id=1, source_target_pairs={{0,16},{1,17},{2,18},{3,19},{4,20},{5,21},{6,22},{7,23},{8,24},{9,... | collective-permute-start | bytes 196616 | tf_op jit(solution)/shard_map/ppermute | solution.py:18
  73.8 1.3 %collective-permute-start.16 = (f32[64,256]{1,0:T(8,128)S(1)}, f32[64,256]{1,0:T(8,128)S(1)}, u32[]{:S(2)}, u32[]{:S(2)}) collective-permute-start(f32[64,256]{1,0:T(8,128)S(1)} %add_add_fusion), channel_id=1, source_target_pairs={{0,17},{1,16},{2,19},{3,18},{4,21},{5,20},{6,23},{7,22},{8,25},{9,... | collective-permute-start | bytes 196616 | tf_op jit(solution)/shard_map/ppermute | solution.py:18
  75.1 0.8 convolution_subtract_fusion.1
  75.8 0.1 collective-permute-start.15
  75.9 0.5 collective-permute-done.17
  76.4 2.8 %collective-permute-done.16 = f32[64,256]{1,0:T(8,128)S(1)} collective-permute-done((f32[64,256]{1,0:T(8,128)S(1)}, f32[64,256]{1,0:T(8,128)S(1)}, u32[]{:S(2)}, u32[]{:S(2)}) %collective-permute-start.16) | collective-permute-done | bytes 65568 | tf_op jit(solution)/shard_map/ppermute | solution.py:18
  79.3 0.2 fusion.18
  79.5 0.7 collective-permute-done.15
  80.2 0.2 convolution_add_fusion
  80.4 1.6 %convolution_subtract_fusion = f32[64,2048]{1,0:T(8,128)} fusion(f32[64,2048]{1,0:T(8,128)S(1)} %convolution_subtract_fusion.1, f32[64,256]{1,0:T(8,128)S(1)} %convolution_add_fusion, f32[4,256,2048]{2,1,0:T(8,128)S(1)} %bitcast.70), kind=kOutput, calls=%fused_computation | convolution fusion | flops 201457664 | bytes 3211264 | tf_op jit(solution)/shard_map/dot_general | solution.py:13
  (28 shorter events, 0.1 us)
Async XLA Ops:
  0.0 13.8 %collective-permute-start = (f32[64,2048]{1,0:T(8,128)}, f32[64,2048]{1,0:T(8,128)S(1)}, u32[]{:S(2)}, u32[]{:S(2)}) collective-permute-start(f32[64,2048]{1,0:T(8,128)} %own.1), channel_id=1, source_target_pairs={{0,1},{1,0},{2,3},{3,2},{4,5},{5,4},{6,7},{7,6},{8,9},{9,8},{10,11... | collective-permute-start | bytes 1572872 | tf_op jit(solution)/shard_map/ppermute | solution.py:18
  13.8 0.8 copy-start.3
  14.6 16.4 %copy-start = (f32[4,2048,256]{2,1,0:T(8,128)S(1)}, f32[4,2048,256]{2,1,0:T(8,128)}, u32[]{:S(2)}) copy-start(f32[4,2048,256]{2,1,0:T(8,128)} %proj_hbm.3) | copy-start | bytes 25165828
  14.6 18.8 %copy-start.7 = (f32[256,256]{1,0:T(8,128)S(1)}, f32[256,256]{1,0:T(8,128)}, u32[]{:S(2)}) copy-start(f32[256,256]{1,0:T(8,128)} %get-tuple-element.29) | copy-start | bytes 786436
  25.4 7.5 %copy-start.2 = (f32[1,4,2,256,256]{4,3,2,1,0:T(8,128)S(1)}, f32[1,4,2,256,256]{4,3,2,1,0:T(8,128)}, u32[]{:S(2)}) copy-start(f32[1,4,2,256,256]{4,3,2,1,0:T(8,128)} %param.15) | copy-start | bytes 6291460
  25.4 4.6 %collective-permute-start.1 = (f32[64,256]{1,0:T(8,128)}, f32[64,256]{1,0:T(8,128)S(1)}, u32[]{:S(2)}, u32[]{:S(2)}) collective-permute-start(f32[64,256]{1,0:T(8,128)} %get-tuple-element.28), channel_id=1, source_target_pairs={{0,1},{1,0},{2,3},{3,2},{4,5},{5,4},{6,7},{7,6},{8,9},{9,8},{10,11... | collective-permute-start | bytes 196616 | tf_op jit(solution)/shard_map/ppermute | solution.py:18
  30.0 8.3 %copy-start.1 = (f32[64,2048]{1,0:T(8,128)S(1)}, f32[64,2048]{1,0:T(8,128)}, u32[]{:S(2)}) copy-start(f32[64,2048]{1,0:T(8,128)} %get-tuple-element.27) | copy-start | bytes 1572868
  30.9 2.0 %collective-permute-start.2 = (f32[64,256]{1,0:T(8,128)S(1)}, f32[64,256]{1,0:T(8,128)S(1)}, u32[]{:S(2)}, u32[]{:S(2)}) collective-permute-start(f32[64,256]{1,0:T(8,128)S(1)} %add.51), channel_id=1, source_target_pairs={{0,2},{2,0},{1,3},{3,1},{4,6},{6,4},{5,7},{7,5},{8,10},{10,8},{9,1... | collective-permute-start | bytes 196616 | tf_op jit(solution)/shard_map/ppermute | solution.py:18
  31.0 35.7 %slice-start = ((s8[8388608]{0:T(1024)(128)(4,1)}), s8[4194304]{0:T(1024)(128)(4,1)S(1)}, s32[]{:S(2)}) async-start(s8[8388608]{0:T(1024)(128)(4,1)} %bitcast.69), calls=%async_computation | async-start | bytes 8388608
  33.1 7.9 %copy-start.6 = (f32[256,256]{1,0:T(8,128)S(1)}, f32[256,256]{1,0:T(8,128)}, u32[]{:S(2)}) copy-start(f32[256,256]{1,0:T(8,128)} %get-tuple-element.30) | copy-start | bytes 786436
  33.6 4.6 %collective-permute-start.3 = (f32[64,256]{1,0:T(8,128)S(1)}, f32[64,256]{1,0:T(8,128)S(1)}, u32[]{:S(2)}, u32[]{:S(2)}) collective-permute-start(f32[64,256]{1,0:T(8,128)S(1)} %convolution_subtract_fusion.8), channel_id=1, source_target_pairs={{0,1},{1,0},{2,3},{3,2},{4,5},{5,4},{6,7},{7,6},{8,9},{9,8},{10,11... | collective-permute-start | bytes 196616 | tf_op jit(solution)/shard_map/ppermute | solution.py:18
  38.2 6.2 %copy-start.5 = (f32[256,256]{1,0:T(8,128)S(1)}, f32[256,256]{1,0:T(8,128)}, u32[]{:S(2)}) copy-start(f32[256,256]{1,0:T(8,128)} %get-tuple-element.31) | copy-start | bytes 786436
  38.2 1.3 %collective-permute-start.4 = (f32[64,256]{1,0:T(8,128)S(1)}, f32[64,256]{1,0:T(8,128)S(1)}, u32[]{:S(2)}, u32[]{:S(2)}) collective-permute-start(f32[64,256]{1,0:T(8,128)S(1)} %add.53), channel_id=1, source_target_pairs={{0,2},{2,0},{1,3},{3,1},{4,6},{6,4},{5,7},{7,5},{8,10},{10,8},{9,1... | collective-permute-start | bytes 196616 | tf_op jit(solution)/shard_map/ppermute | solution.py:18
  39.5 4.3 %collective-permute-start.5 = (f32[64,256]{1,0:T(8,128)S(1)}, f32[64,256]{1,0:T(8,128)S(1)}, u32[]{:S(2)}, u32[]{:S(2)}) collective-permute-start(f32[64,256]{1,0:T(8,128)S(1)} %add.54), channel_id=1, source_target_pairs={{0,4},{4,0},{1,5},{5,1},{2,6},{6,2},{3,7},{7,3},{8,12},{12,8},{9,1... | collective-permute-start | bytes 196616 | tf_op jit(solution)/shard_map/ppermute | solution.py:18
  44.1 10.6 %copy-start.4 = (f32[256,256]{1,0:T(8,128)S(1)}, f32[256,256]{1,0:T(8,128)}, u32[]{:S(2)}) copy-start(f32[256,256]{1,0:T(8,128)} %get-tuple-element.32) | copy-start | bytes 786436
  44.5 22.1 %slice-start.1 = ((s8[8388608]{0:T(1024)(128)(4,1)}), s8[4194304]{0:T(1024)(128)(4,1)S(1)}, s32[]{:S(2)}) async-start(s8[8388608]{0:T(1024)(128)(4,1)} %bitcast.69), calls=%async_computation.1 | async-start | bytes 8388608
  44.6 4.3 %collective-permute-start.6 = (f32[64,256]{1,0:T(8,128)S(1)}, f32[64,256]{1,0:T(8,128)S(1)}, u32[]{:S(2)}, u32[]{:S(2)}) collective-permute-start(f32[64,256]{1,0:T(8,128)S(1)} %convolution_subtract_fusion.6), channel_id=1, source_target_pairs={{0,1},{1,0},{2,3},{3,2},{4,5},{5,4},{6,7},{7,6},{8,9},{9,8},{10,11... | collective-permute-start | bytes 196616 | tf_op jit(solution)/shard_map/ppermute | solution.py:18
  48.9 11.2 %copy-start.8 = (f32[256,256]{1,0:T(8,128)S(1)}, f32[256,256]{1,0:T(8,128)}, u32[]{:S(2)}) copy-start(f32[256,256]{1,0:T(8,128)} %get-tuple-element.34) | copy-start | bytes 786436
  48.9 11.5 %copy-start.9 = (f32[256,256]{1,0:T(8,128)S(1)}, f32[256,256]{1,0:T(8,128)}, u32[]{:S(2)}) copy-start(f32[256,256]{1,0:T(8,128)} %get-tuple-element.33) | copy-start | bytes 786436
  48.9 1.3 %collective-permute-start.7 = (f32[64,256]{1,0:T(8,128)S(1)}, f32[64,256]{1,0:T(8,128)S(1)}, u32[]{:S(2)}, u32[]{:S(2)}) collective-permute-start(f32[64,256]{1,0:T(8,128)S(1)} %add.56), channel_id=1, source_target_pairs={{0,2},{2,0},{1,3},{3,1},{4,6},{6,4},{5,7},{7,5},{8,10},{10,8},{9,1... | collective-permute-start | bytes 196616 | tf_op jit(solution)/shard_map/ppermute | solution.py:18
  50.3 6.4 %collective-permute-start.10 = (f32[64,256]{1,0:T(8,128)S(1)}, f32[64,256]{1,0:T(8,128)S(1)}, u32[]{:S(2)}, u32[]{:S(2)}) collective-permute-start(f32[64,256]{1,0:T(8,128)S(1)} %add.57), channel_id=1, source_target_pairs={{0,8},{4,12},{8,0},{12,4},{1,9},{5,13},{9,1},{13,5},{2,10},{6,14},... | collective-permute-start | bytes 196616 | tf_op jit(solution)/shard_map/ppermute | solution.py:18
  54.2 5.5 %collective-permute-start.9 = (f32[64,256]{1,0:T(8,128)S(1)}, f32[64,256]{1,0:T(8,128)S(1)}, u32[]{:S(2)}, u32[]{:S(2)}) collective-permute-start(f32[64,256]{1,0:T(8,128)S(1)} %add.57), channel_id=1, source_target_pairs={{0,12},{4,8},{8,4},{12,0},{1,13},{5,9},{9,5},{13,1},{2,14},{6,10},... | collective-permute-start | bytes 196616 | tf_op jit(solution)/shard_map/ppermute | solution.py:18
  54.9 5.0 %collective-permute-start.8 = (f32[64,256]{1,0:T(8,128)S(1)}, f32[64,256]{1,0:T(8,128)S(1)}, u32[]{:S(2)}, u32[]{:S(2)}) collective-permute-start(f32[64,256]{1,0:T(8,128)S(1)} %add.57), channel_id=1, source_target_pairs={{0,4},{4,0},{8,12},{12,8},{1,5},{5,1},{9,13},{13,9},{2,6},{6,2},{1... | collective-permute-start | bytes 196616 | tf_op jit(solution)/shard_map/ppermute | solution.py:18
  60.6 2.4 %collective-permute-start.11 = (f32[64,256]{1,0:T(8,128)S(1)}, f32[64,256]{1,0:T(8,128)S(1)}, u32[]{:S(2)}, u32[]{:S(2)}) collective-permute-start(f32[64,256]{1,0:T(8,128)S(1)} %fusion.17), channel_id=1, source_target_pairs={{0,2},{2,0},{1,3},{3,1},{4,6},{6,4},{5,7},{7,5},{8,10},{10,8},{9,1... | collective-permute-start | bytes 196616 | tf_op jit(solution)/shard_map/ppermute | solution.py:18
  63.1 6.1 %collective-permute-start.14 = (f32[64,256]{1,0:T(8,128)S(1)}, f32[64,256]{1,0:T(8,128)S(1)}, u32[]{:S(2)}, u32[]{:S(2)}) collective-permute-start(f32[64,256]{1,0:T(8,128)S(1)} %add.61), channel_id=1, source_target_pairs={{0,8},{4,12},{8,0},{12,4},{1,9},{5,13},{9,1},{13,5},{2,10},{6,14},... | collective-permute-start | bytes 196616 | tf_op jit(solution)/shard_map/ppermute | solution.py:18
  64.7 5.9 %collective-permute-start.13 = (f32[64,256]{1,0:T(8,128)S(1)}, f32[64,256]{1,0:T(8,128)S(1)}, u32[]{:S(2)}, u32[]{:S(2)}) collective-permute-start(f32[64,256]{1,0:T(8,128)S(1)} %add.61), channel_id=1, source_target_pairs={{0,12},{4,8},{8,4},{12,0},{1,13},{5,9},{9,5},{13,1},{2,14},{6,10},... | collective-permute-start | bytes 196616 | tf_op jit(solution)/shard_map/ppermute | solution.py:18
  65.7 4.9 %collective-permute-start.12 = (f32[64,256]{1,0:T(8,128)S(1)}, f32[64,256]{1,0:T(8,128)S(1)}, u32[]{:S(2)}, u32[]{:S(2)}) collective-permute-start(f32[64,256]{1,0:T(8,128)S(1)} %add.61), channel_id=1, source_target_pairs={{0,4},{4,0},{8,12},{12,8},{1,5},{5,1},{9,13},{13,9},{2,6},{6,2},{1... | collective-permute-start | bytes 196616 | tf_op jit(solution)/shard_map/ppermute | solution.py:18
  70.6 5.8 %collective-permute-start.17 = (f32[64,256]{1,0:T(8,128)S(1)}, f32[64,256]{1,0:T(8,128)S(1)}, u32[]{:S(2)}, u32[]{:S(2)}) collective-permute-start(f32[64,256]{1,0:T(8,128)S(1)} %add_add_fusion), channel_id=1, source_target_pairs={{0,16},{1,17},{2,18},{3,19},{4,20},{5,21},{6,22},{7,23},{8,24},{9,... | collective-permute-start | bytes 196616 | tf_op jit(solution)/shard_map/ppermute | solution.py:18
  73.8 5.5 %collective-permute-start.16 = (f32[64,256]{1,0:T(8,128)S(1)}, f32[64,256]{1,0:T(8,128)S(1)}, u32[]{:S(2)}, u32[]{:S(2)}) collective-permute-start(f32[64,256]{1,0:T(8,128)S(1)} %add_add_fusion), channel_id=1, source_target_pairs={{0,17},{1,16},{2,19},{3,18},{4,21},{5,20},{6,23},{7,22},{8,25},{9,... | collective-permute-start | bytes 196616 | tf_op jit(solution)/shard_map/ppermute | solution.py:18
  75.8 4.3 %collective-permute-start.15 = (f32[64,256]{1,0:T(8,128)S(1)}, f32[64,256]{1,0:T(8,128)S(1)}, u32[]{:S(2)}, u32[]{:S(2)}) collective-permute-start(f32[64,256]{1,0:T(8,128)S(1)} %add_add_fusion), channel_id=1, source_target_pairs={{0,1},{1,0},{2,3},{3,2},{4,5},{5,4},{6,7},{7,6},{8,9},{9,8},{10,11... | collective-permute-start | bytes 196616 | tf_op jit(solution)/shard_map/ppermute | solution.py:18

commit v4 on v3

v4 whole, which is shorter than its diff:
```python
import jax
import jax.numpy as jnp
from jax import lax
from jax.experimental import pallas as pl
from jax.experimental.pallas import tpu as pltpu
from jax.sharding import Mesh, PartitionSpec as P

AXES = ("z", "y", "x1", "x0", "core", "rhs")
FAST = lax.Precision.HIGH


def dot(a, b):
    return jnp.dot(a, b, precision=FAST, preferred_element_type=jnp.float32)


def swap(block, axes, mask):
    count = lax.axis_size(axes)
    return lax.ppermute(block, axes, [(i, i ^ mask) for i in range(count)])


def over_rhs(block):
    return swap(block, ("rhs",), 1)


RING = ("y", "x1", "x0", "core", "rhs")


def mm(a, b):
    return jnp.dot(a, b, preferred_element_type=jnp.float32)

def parts(value):
    high = value.astype(jnp.bfloat16)
    low = (value - high.astype(jnp.float32)).astype(jnp.bfloat16)
    return high, low

def stacked(value):
    high, low = parts(value)
    return jnp.concatenate([high, low], axis=0)

def near_kernel(order, index, count, side, own, other, tiles_hbm, proj_hbm, current, reduced,
                source, gathered, operand, tiles, proj, needed, wanted, tile_sem, proj_sem):
    rows, half = own.shape
    size = tiles.shape[-1]
    slots = index.shape[1]
    leaf_tiles = operand.shape[0]
    out_tiles = tiles.shape[0]
    load_tiles = pltpu.make_async_copy(tiles_hbm, tiles, tile_sem)
    load_tiles.start()
    load_proj = pltpu.make_async_copy(proj_hbm.at[pl.ds(0, 2)], proj, proj_sem)
    load_proj.start()
    own_start = side[0] * half
    other_start = half - own_start
    for block, start in ((own, own_start), (other, other_start)):
        for c in range(half // size):
            at = pl.multiple_of(start + c * size, size)
            source[pl.ds(at, size), :] = block[:, c * size:(c + 1) * size].T

    for tile in range(leaf_tiles):
        needed[tile] = 0
    for t in range(out_tiles):
        for slot in range(slots):
            needed[index[t, jnp.where(slot < count[t], slot, 0)]] = 1

    def note(tile, found):
        wanted[found] = tile
        return found + needed[tile]
    found = lax.fori_loop(0, leaf_tiles, note, 0, unroll=True)
    wanted[found] = wanted[found - 1]

    def fetch(base, slot):
        for u in range(size):
            gathered[slot, pl.ds(u, 1), :] = source[pl.ds(order[base + u], 1), :]

    fetch(wanted[0] * size, 0)
    def gather(n, _):
        slot = n & 1
        ready = stacked(gathered[slot].T)
        fetch(wanted[n + 1] * size, 1 - slot)
        operand[wanted[n]] = ready
        return 0
    lax.fori_loop(0, found, gather, 0)

    load_tiles.wait()
    def near(t, _):
        pieces = []
        for slot in range(slots):
            live = slot < count[t]
            picked = operand[jnp.where(live, index[t, slot], index[t, 0])]
            pieces.append(jnp.where(live, picked, jnp.zeros_like(picked)))
        left = jnp.concatenate(pieces, axis=1)
        high, low = parts(tiles[t].reshape(slots * size, size))
        both = mm(left, high)
        out = both[:rows] + both[rows:] + mm(left[:rows], low)
        current[:, pl.ds(pl.multiple_of(t * size, size), size)] = out
        return 0
    lax.fori_loop(0, out_tiles, near, 0, unroll=8)
    load_proj.wait()
    left = stacked(current[...])
    for level in range(2):
        high, low = parts(proj[level])
        both = mm(left, high)
        reduced[level * rows:(level + 1) * rows, :] = (
            both[:rows] + both[rows:] + mm(left[:rows], low))

def near_call(order, index, count, side, own, other, tiles, proj):
    rows, half = own.shape
    out_tiles, slots, size, _ = tiles.shape
    rank = proj.shape[-1]
    smem = pl.BlockSpec(memory_space=pltpu.SMEM)
    vmem = pl.BlockSpec(memory_space=pltpu.VMEM)
    hbm = pl.BlockSpec(memory_space=pltpu.HBM)
    return pl.pallas_call(
        near_kernel,
        out_shape=(jax.ShapeDtypeStruct((rows, half), jnp.float32), jax.ShapeDtypeStruct((2 * rows, rank), jnp.float32)),
        in_specs=[smem, smem, smem, smem, vmem, vmem, hbm, hbm],
        out_specs=(vmem, vmem),
        scratch_shapes=[
            pltpu.VMEM((order.shape[0], rows), jnp.float32),
            pltpu.VMEM((2, size, rows), jnp.float32),
            pltpu.VMEM((order.shape[0] // size, 2 * rows, size), jnp.bfloat16),
            pltpu.VMEM(tiles.shape, jnp.float32),
            pltpu.VMEM((2, half, rank), jnp.float32),
            pltpu.SMEM((order.shape[0] // size,), jnp.int32),
            pltpu.SMEM((order.shape[0] // size + 1,), jnp.int32),
            pltpu.SemaphoreType.DMA,
            pltpu.SemaphoreType.DMA,
        ],
        compiler_params=pltpu.CompilerParams(vmem_limit_bytes=48 << 20),
        cost_estimate=pl.CostEstimate(flops=200_000_000, bytes_accessed=8 << 20, transcendentals=0),
        name="near",
    )(order, index, count, side, own, other,
      *(pltpu.with_memory_space_constraint(v, pltpu.HBM) for v in (tiles, proj)))

def gram_kernel(corr_hbm, proj_hbm, *rest):
    levels, points, rank = proj_hbm.shape
    early, second, mid, late, corr, proj, sems = rest
    targets = {(0, 0): (early, 0), (1, 0): (second, 0), (1, 1): (mid, 0),
               (2, 0): (late, 0), (2, 1): (late, 1), (2, 2): (late, 2)}
    loads = {}
    for level in range(levels - 1):
        loads["c", level] = pltpu.make_async_copy(corr_hbm.at[level], corr.at[level], sems.at[level])
        loads["p", level] = pltpu.make_async_copy(
            proj_hbm.at[level + 1], proj.at[level], sems.at[levels - 1 + level])
        loads["c", level].start()
        loads["p", level].start()
    lefts = []
    for above in range(levels - 1):
        loads["c", above].wait()
        left_high, left_low = parts(corr[above])
        lefts.append((left_high, left_low))
        loads["p", above].wait()
        high, low = parts(proj[above])
        for below in range(above + 1):
            left_high, left_low = lefts[below]
            target, place = targets[above, below]
            target[place * rank:(place + 1) * rank, :] = (
                mm(left_high, high) + mm(left_high, low) + mm(left_low, high))

def gram_call(corr, proj):
    levels, points, rank = proj.shape
    pairs = levels * (levels - 1) // 2
    hbm = pl.BlockSpec(memory_space=pltpu.HBM)
    vmem = pl.BlockSpec(memory_space=pltpu.VMEM)
    return pl.pallas_call(
        gram_kernel,
        out_shape=[jax.ShapeDtypeStruct((above * rank, rank), jnp.float32) for above in (1, 1, 1, 3)],
        in_specs=[hbm, hbm],
        out_specs=[vmem] * levels,
        scratch_shapes=[
            pltpu.VMEM((levels - 1, rank, points), jnp.float32),
            pltpu.VMEM((levels - 1, points, rank), jnp.float32),
            pltpu.SemaphoreType.DMA((2 * levels - 2,)),
        ],
        compiler_params=pltpu.CompilerParams(vmem_limit_bytes=54 << 20),
        cost_estimate=pl.CostEstimate(
            flops=6 * pairs * points * rank * rank, bytes_accessed=12 << 20, transcendentals=0),
        name="gram",
    )(*(pltpu.with_memory_space_constraint(v, pltpu.HBM) for v in (corr, proj)))


def local(
    charges, cluster_order, near_tiles, near_index, near_count, proj_basis, corr_basis, coupling
):
    tie = lax.optimization_barrier
    rank = proj_basis.shape[-1]
    other = over_rhs(charges)
    early, second, mid, late = gram_call(corr_basis, proj_basis)
    early_other = over_rhs(early)
    second_other = over_rhs(second)
    other, early, second, mid, late = tie((other, early, second, mid, late))
    side = lax.axis_index("rhs").astype(jnp.int32).reshape(1)
    current, pair = near_call(
        cluster_order, near_index, near_count, side, charges, other, near_tiles, proj_basis
    )
    pair, early_other = tie((pair, early_other))
    early = early + early_other
    pair = pair + over_rhs(pair)
    own, sum1 = pair[:charges.shape[0]], pair[charges.shape[0]:]
    own, mid, second_other = tie((own, mid, second_other))
    second = second + second_other
    mid = mid + over_rhs(mid)
    part2 = dot(current, proj_basis[2])
    sum2 = part2 + over_rhs(part2)
    part3 = dot(current, proj_basis[3])

    def coefficients(height, own, sib):
        return dot(own, coupling[0, height, 0]) + dot(sib, coupling[0, height, 1])

    coeff0 = coefficients(0, own, swap(own, ("core",), 1))
    own = sum1 - dot(coeff0, early)
    own = own + swap(own, ("core",), 1)
    current = current - dot(coeff0, corr_basis[0])
    sum2 = sum2 - dot(coeff0, second)
    part3 = part3 - dot(coeff0, late[:rank])
    coeff1 = coefficients(1, own, swap(own, ("x0",), 1))
    own = sum2 - dot(coeff1, mid)
    own = own + swap(own, ("core",), 1)
    current = current - dot(coeff1, corr_basis[1])
    part3 = part3 - dot(coeff1, late[rank:2 * rank])
    near, far, across = (swap(own, ("x1", "x0"), mask) for mask in (1, 3, 2))
    coeff2 = coefficients(2, own + near, far + across)
    own = part3 - dot(coeff2, late[2 * rank:])
    own = own + swap(own, ("core",), 1)
    current = current - dot(coeff2, corr_basis[2])
    near, far, across = (swap(own, ("x1", "x0"), mask) for mask in (1, 3, 2))
    own = (own + near) + (far + across)
    near, far, across = (swap(own, RING, mask) for mask in (1, 17, 16))
    coeff3 = coefficients(3, own + near, far + across)
    return current - dot(coeff3, corr_basis[3])


def solution(mesh):
    split = Mesh(mesh.devices.reshape(-1, 2, 2, 2, 2, 2), AXES)
    every = AXES
    leaf = AXES[:-1]
    return jax.shard_map(
        local,
        mesh=split,
        in_specs=(
            P(None, every),
            P(leaf),
            P(every, None, None, None),
            P(every, None),
            P(every),
            P(None, every, None),
            P(None, None, every),
            P(leaf, None, None, None, None),
        ),
        out_specs=P(None, every),
        check_vma=False,
    )
```

time: 82.2 us -> 73.1 us (0.89)
  Pallas kernels: 21.5 us -> 17.9 us
  matrix products: 11.7 us -> 8.22 us
  local copies, waits for them, and re-layouts: 2.21 us -> 0.14 us
  other arithmetic: 0.97 us -> 0.06 us
    pallas_call x1, Pallas kernels: 10.8 us -> 7.06 us  [near_call(): pl.pallas_call(near_kernel, out_shape=(jax.ShapeDtypeStruct((rows, half),...]
    dot_general x21 -> x20, matrix products: 11.7 us -> 8.22 us  [dot(): return jnp.dot(a, b, precision=FAST, preferred_element_type=jnp.float32)]
    unnamed x25 -> x23, local copies, waits for them, and re-layouts: 2.21 us -> 0.13 us
    add x7 -> x5, other arithmetic: 0.97 us -> 0.06 us  [the longest x3 0.03 us: local(): own = own + swap(own, ('core',), 1)]
    ppermute x18 -> x20, waiting for transfers between devices: 24.2 us -> 24.9 us  [swap(): return lax.ppermute(block, axes, [(i, i ^ mask) for i in range(count)])]
    ppermute x18 -> x20, starting transfers between devices: 20.9 us -> 21.4 us  [swap(): return lax.ppermute(block, axes, [(i, i ^ mask) for i in range(count)])]
  transfers between devices with their start and end apart: 18 -> 20, of which waited for: 13 -> 13; matrix products, arithmetic and copies ran while one was open for 11% -> 7% of each run, Pallas kernels for 13% -> 25%
where the time goes in v4:
time: 73.1 us; the launch traced here: 73 us
  waiting for transfers between devices  24.9 us (34%)
  starting transfers between devices  21.4 us (29%)
  Pallas kernels  17.9 us (24%)
  matrix products  8.22 us (11%)
    ppermute x20, waiting for transfers between devices, swap(): return lax.ppermute(block, axes, [(i, i ^ mask) for i in range(count)])  24.9 us
    ppermute x20, starting transfers between devices, swap(): return lax.ppermute(block, axes, [(i, i ^ mask) for i in range(count)])  21.4 us
    pallas_call x1, Pallas kernels, gram_call(): pl.pallas_call(gram_kernel, out_shape=[jax.ShapeDtypeStruct((above * rank...  10.9 us
    dot_general x20, matrix products, dot(): return jnp.dot(a, b, precision=FAST, preferred_element_type=jnp.float32)  8.22 us
    pallas_call x1, Pallas kernels, near_call(): pl.pallas_call(near_kernel, out_shape=(jax.ShapeDtypeStruct((rows, half),...  7.06 us
  transfers between devices with their start and end apart: 20, of which 13 were waited for; matrix products, arithmetic and copies ran while one was open for 7% of the time, Pallas kernels for 25%

profile of v4, /device:TPU:0, one launch (start us, length us, event | category | flops | bytes accessed | tf_op | source)
XLA Modules:
  0.0 73.0 jit_solution(5797969769640964312)
XLA Ops:
  0.0 1.7 %collective-permute-start = (f32[64,2048]{1,0:T(8,128)}, f32[64,2048]{1,0:T(8,128)S(1)}, u32[]{:S(2)}, u32[]{:S(2)}) collective-permute-start(f32[64,2048]{1,0:T(8,128)} %own.1), channel_id=1, source_target_pairs={{0,1},{1,0},{2,3},{3,2},{4,5},{5,4},{6,7},{7,6},{8,9},{9,8},{10,11... | collective-permute-start | bytes 1572872 | tf_op jit(solution)/shard_map/ppermute | solution.py:18
  1.8 10.9 %gram.1 = (f32[256,256]{1,0:T(8,128)}, f32[256,256]{1,0:T(8,128)}, f32[256,256]{1,0:T(8,128)}, f32[768,256]{1,0:T(8,128)}) custom-call(f32[4,256,2048]{2,1,0:T(8,128)} %corr_hbm.1, f32[4,2048,256]{2,1,0:T(8,128)} %proj_hbm.3), custom_call_target="tpu_custom_call" | custom-call | flops 4831838208 | bytes 12582912 | tf_op jit(solution)/shard_map/gram/pallas_call | solution.py:164
  12.6 0.4 collective-permute-start.1
  13.1 1.7 %collective-permute-start.3 = (f32[256,256]{1,0:T(8,128)}, f32[256,256]{1,0:T(8,128)S(1)}, u32[]{:S(2)}, u32[]{:S(2)}) collective-permute-start(f32[256,256]{1,0:T(8,128)} %get-tuple-element.33), channel_id=1, source_target_pairs={{0,1},{1,0},{2,3},{3,2},{4,5},{5,4},{6,7},{7,6},{8,9},{9,8},{10,11... | collective-permute-start | bytes 786440 | tf_op jit(solution)/shard_map/ppermute | solution.py:18
  14.7 0.1 copy.9.index
  14.8 0.0 collective-permute-done.other
  14.9 0.0 copy-start.3
  14.9 7.1 %near.1 = (f32[64,2048]{1,0:T(8,128)S(1)}, f32[128,256]{1,0:T(8,128)S(1)}) custom-call(s32[4096]{0:T(1024)S(1)} %copy-done.1, s32[16,4]{1,0:T(8,128)S(1)} %copy.9.index, s32[16]{0:T(128)S(1)} %copy-done.2, s32[1]{0:T(128)} %bitcast.side, f32[64,2048]{1,0:T(8,128)S(1)} %copy-done, f32[64,2048]{1,0:T(8,128)S(1)} %collective-permute-done.other, ...), custom_call_target="tpu_custom_call" | custom-call | flops 200000000 | bytes 8388608 | tf_op jit(solution)/shard_map/near/pallas_call | solution.py:112
  21.9 0.0 copy-start.5
  21.9 0.0 copy-start.9
  22.0 0.2 collective-permute-done.1
  22.2 0.5 collective-permute-start.2
  22.7 6.5 %collective-permute-done.2 = f32[128,256]{1,0:T(8,128)S(1)} collective-permute-done((f32[128,256]{1,0:T(8,128)S(1)}, f32[128,256]{1,0:T(8,128)S(1)}, u32[]{:S(2)}, u32[]{:S(2)}) %collective-permute-start.2) | collective-permute-done | bytes 131104 | tf_op jit(solution)/shard_map/ppermute | solution.py:18
  29.2 0.1 collective-permute-start.4
  29.3 0.7 fusion.1
  30.0 0.5 collective-permute-done.4
  30.5 0.2 fusion.23
  30.7 0.2 convolution_add_fusion.3
  31.0 0.0 copy-start.4
  31.0 0.2 slice_subtract_fusion
  31.2 0.2 collective-permute-start.5
  31.4 0.7 fusion.4
  32.1 0.6 collective-permute-start.7
  32.8 1.5 %collective-permute-start.8 = (f32[256,256]{1,0:T(8,128)S(1)}, f32[256,256]{1,0:T(8,128)S(1)}, u32[]{:S(2)}, u32[]{:S(2)}) collective-permute-start(f32[256,256]{1,0:T(8,128)S(1)} %copy-done.7), channel_id=1, source_target_pairs={{0,1},{1,0},{2,3},{3,2},{4,5},{5,4},{6,7},{7,6},{8,9},{9,8},{10,11... | collective-permute-start | bytes 786440 | tf_op jit(solution)/shard_map/ppermute | solution.py:18
  34.3 1.7 %collective-permute-start.6 = (f32[64,256]{1,0:T(8,128)S(1)}, f32[64,256]{1,0:T(8,128)S(1)}, u32[]{:S(2)}, u32[]{:S(2)}) collective-permute-start(f32[64,256]{1,0:T(8,128)S(1)} %add.60), channel_id=1, source_target_pairs={{0,4},{4,0},{1,5},{5,1},{2,6},{6,2},{3,7},{7,3},{8,12},{12,8},{9,1... | collective-permute-start | bytes 196616 | tf_op jit(solution)/shard_map/ppermute | solution.py:18
  36.0 0.2 fusion.35
  36.2 2.5 %collective-permute-done.6 = f32[64,256]{1,0:T(8,128)S(1)} collective-permute-done((f32[64,256]{1,0:T(8,128)S(1)}, f32[64,256]{1,0:T(8,128)S(1)}, u32[]{:S(2)}, u32[]{:S(2)}) %collective-permute-start.6) | collective-permute-done | bytes 65568 | tf_op jit(solution)/shard_map/ppermute | solution.py:18
  38.8 0.2 fusion.20
  39.0 0.2 convolution_add_fusion.2
  39.2 0.0 collective-permute-done.7
  39.2 2.9 %collective-permute-done.8 = f32[256,256]{1,0:T(8,128)S(1)} collective-permute-done((f32[256,256]{1,0:T(8,128)S(1)}, f32[256,256]{1,0:T(8,128)S(1)}, u32[]{:S(2)}, u32[]{:S(2)}) %collective-permute-start.8) | collective-permute-done | bytes 262176 | tf_op jit(solution)/shard_map/ppermute | solution.py:18
  42.2 0.2 subtract_subtract_fusion
  42.4 0.1 collective-permute-start.9
  42.5 0.2 convolution_subtract_fusion.6
  42.7 1.0 %collective-permute-done.9 = f32[64,256]{1,0:T(8,128)S(1)} collective-permute-done((f32[64,256]{1,0:T(8,128)S(1)}, f32[64,256]{1,0:T(8,128)S(1)}, u32[]{:S(2)}, u32[]{:S(2)}) %collective-permute-start.9) | collective-permute-done | bytes 65568 | tf_op jit(solution)/shard_map/ppermute | solution.py:18
  43.8 2.8 %collective-permute-start.11 = (f32[64,256]{1,0:T(8,128)S(1)}, f32[64,256]{1,0:T(8,128)S(1)}, u32[]{:S(2)}, u32[]{:S(2)}) collective-permute-start(f32[64,256]{1,0:T(8,128)S(1)} %add.65), channel_id=1, source_target_pairs={{0,12},{4,8},{8,4},{12,0},{1,13},{5,9},{9,5},{13,1},{2,14},{6,10},... | collective-permute-start | bytes 196616 | tf_op jit(solution)/shard_map/ppermute | solution.py:18
  46.6 0.8 %collective-permute-start.12 = (f32[64,256]{1,0:T(8,128)S(1)}, f32[64,256]{1,0:T(8,128)S(1)}, u32[]{:S(2)}, u32[]{:S(2)}) collective-permute-start(f32[64,256]{1,0:T(8,128)S(1)} %add.65), channel_id=1, source_target_pairs={{0,8},{4,12},{8,0},{12,4},{1,9},{5,13},{9,1},{13,5},{2,10},{6,14},... | collective-permute-start | bytes 196616 | tf_op jit(solution)/shard_map/ppermute | solution.py:18
  47.4 0.2 convolution_subtract_fusion.5
  47.6 0.6 collective-permute-start.10
  48.2 1.5 %collective-permute-done.11 = f32[64,256]{1,0:T(8,128)S(1)} collective-permute-done((f32[64,256]{1,0:T(8,128)S(1)}, f32[64,256]{1,0:T(8,128)S(1)}, u32[]{:S(2)}, u32[]{:S(2)}) %collective-permute-start.11) | collective-permute-done | bytes 65568 | tf_op jit(solution)/shard_map/ppermute | solution.py:18
  49.7 3.1 %collective-permute-done.12 = f32[64,256]{1,0:T(8,128)S(1)} collective-permute-done((f32[64,256]{1,0:T(8,128)S(1)}, f32[64,256]{1,0:T(8,128)S(1)}, u32[]{:S(2)}, u32[]{:S(2)}) %collective-permute-start.12) | collective-permute-done | bytes 65568 | tf_op jit(solution)/shard_map/ppermute | solution.py:18
  52.8 0.2 fusion.17
  53.0 0.0 collective-permute-done.10
  53.1 0.2 convolution_add_fusion.1
  53.3 0.2 convolution_subtract_fusion.4
  53.5 0.1 collective-permute-start.13
  53.6 0.8 %convolution_subtract_fusion.3 = f32[64,2048]{1,0:T(8,128)S(1)} fusion(f32[64,2048]{1,0:T(8,128)S(1)} %get-tuple-element.26, f32[64,256]{1,0:T(8,128)S(1)} %convolution_add_fusion.3, f32[4,256,2048]{2,1,0:T(8,128)S(1)} %copy-done.4), kind=kOutput, calls=%fused_computation.3 | convolution fusion | flops 201457664 | bytes 3211264 | tf_op jit(solution)/shard_map/dot_general | solution.py:13
  54.4 0.5 collective-permute-done.13
  54.8 0.4 collective-permute-start.14
  55.3 1.9 %collective-permute-start.15 = (f32[64,256]{1,0:T(8,128)S(1)}, f32[64,256]{1,0:T(8,128)S(1)}, u32[]{:S(2)}, u32[]{:S(2)}) collective-permute-start(f32[64,256]{1,0:T(8,128)S(1)} %add.69), channel_id=1, source_target_pairs={{0,12},{4,8},{8,4},{12,0},{1,13},{5,9},{9,5},{13,1},{2,14},{6,10},... | collective-permute-start | bytes 196616 | tf_op jit(solution)/shard_map/ppermute | solution.py:18
  57.1 1.9 %collective-permute-start.16 = (f32[64,256]{1,0:T(8,128)S(1)}, f32[64,256]{1,0:T(8,128)S(1)}, u32[]{:S(2)}, u32[]{:S(2)}) collective-permute-start(f32[64,256]{1,0:T(8,128)S(1)} %add.69), channel_id=1, source_target_pairs={{0,8},{4,12},{8,0},{12,4},{1,9},{5,13},{9,1},{13,5},{2,10},{6,14},... | collective-permute-start | bytes 196616 | tf_op jit(solution)/shard_map/ppermute | solution.py:18
  59.0 0.8 %convolution_subtract_fusion.2 = f32[64,2048]{1,0:T(8,128)S(1)} fusion(f32[64,2048]{1,0:T(8,128)S(1)} %convolution_subtract_fusion.3, f32[64,256]{1,0:T(8,128)S(1)} %convolution_add_fusion.2, f32[4,256,2048]{2,1,0:T(8,128)S(1)} %copy-done.4), kind=kOutput, calls=%fused_computation.2 | convolution fusion | flops 201457664 | bytes 3211264 | tf_op jit(solution)/shard_map/dot_general | solution.py:13
  59.8 0.0 collective-permute-done.14
  59.8 1.0 %collective-permute-done.15 = f32[64,256]{1,0:T(8,128)S(1)} collective-permute-done((f32[64,256]{1,0:T(8,128)S(1)}, f32[64,256]{1,0:T(8,128)S(1)}, u32[]{:S(2)}, u32[]{:S(2)}) %collective-permute-start.15) | collective-permute-done | bytes 65568 | tf_op jit(solution)/shard_map/ppermute | solution.py:18
  60.7 2.2 %collective-permute-done.16 = f32[64,256]{1,0:T(8,128)S(1)} collective-permute-done((f32[64,256]{1,0:T(8,128)S(1)}, f32[64,256]{1,0:T(8,128)S(1)}, u32[]{:S(2)}, u32[]{:S(2)}) %collective-permute-start.16) | collective-permute-done | bytes 65568 | tf_op jit(solution)/shard_map/ppermute | solution.py:18
  62.9 2.3 %collective-permute-start.18 = (f32[64,256]{1,0:T(8,128)S(1)}, f32[64,256]{1,0:T(8,128)S(1)}, u32[]{:S(2)}, u32[]{:S(2)}) collective-permute-start(f32[64,256]{1,0:T(8,128)S(1)} %add_add_fusion), channel_id=1, source_target_pairs={{0,17},{1,16},{2,19},{3,18},{4,21},{5,20},{6,23},{7,22},{8,25},{9,... | collective-permute-start | bytes 196616 | tf_op jit(solution)/shard_map/ppermute | solution.py:18
  65.2 0.8 %collective-permute-start.19 = (f32[64,256]{1,0:T(8,128)S(1)}, f32[64,256]{1,0:T(8,128)S(1)}, u32[]{:S(2)}, u32[]{:S(2)}) collective-permute-start(f32[64,256]{1,0:T(8,128)S(1)} %add_add_fusion), channel_id=1, source_target_pairs={{0,16},{1,17},{2,18},{3,19},{4,20},{5,21},{6,22},{7,23},{8,24},{9,... | collective-permute-start | bytes 196616 | tf_op jit(solution)/shard_map/ppermute | solution.py:18
  66.0 0.8 %convolution_subtract_fusion.1 = f32[64,2048]{1,0:T(8,128)S(1)} fusion(f32[64,2048]{1,0:T(8,128)S(1)} %convolution_subtract_fusion.2, f32[64,256]{1,0:T(8,128)S(1)} %convolution_add_fusion.1, f32[4,256,2048]{2,1,0:T(8,128)S(1)} %copy-done.4), kind=kOutput, calls=%fused_computation.1 | convolution fusion | flops 201457664 | bytes 3211264 | tf_op jit(solution)/shard_map/dot_general | solution.py:13
  66.7 1.2 %collective-permute-start.17 = (f32[64,256]{1,0:T(8,128)S(1)}, f32[64,256]{1,0:T(8,128)S(1)}, u32[]{:S(2)}, u32[]{:S(2)}) collective-permute-start(f32[64,256]{1,0:T(8,128)S(1)} %add_add_fusion), channel_id=1, source_target_pairs={{0,1},{1,0},{2,3},{3,2},{4,5},{5,4},{6,7},{7,6},{8,9},{9,8},{10,11... | collective-permute-start | bytes 196616 | tf_op jit(solution)/shard_map/ppermute | solution.py:18
  67.9 0.9 %collective-permute-done.18 = f32[64,256]{1,0:T(8,128)S(1)} collective-permute-done((f32[64,256]{1,0:T(8,128)S(1)}, f32[64,256]{1,0:T(8,128)S(1)}, u32[]{:S(2)}, u32[]{:S(2)}) %collective-permute-start.18) | collective-permute-done | bytes 65568 | tf_op jit(solution)/shard_map/ppermute | solution.py:18
  68.8 2.1 %collective-permute-done.19 = f32[64,256]{1,0:T(8,128)S(1)} collective-permute-done((f32[64,256]{1,0:T(8,128)S(1)}, f32[64,256]{1,0:T(8,128)S(1)}, u32[]{:S(2)}, u32[]{:S(2)}) %collective-permute-start.19) | collective-permute-done | bytes 65568 | tf_op jit(solution)/shard_map/ppermute | solution.py:18
  70.9 0.2 fusion.14
  71.2 0.2 convolution_add_fusion
  71.4 1.6 %convolution_subtract_fusion = f32[64,2048]{1,0:T(8,128)} fusion(f32[64,2048]{1,0:T(8,128)S(1)} %convolution_subtract_fusion.1, f32[64,256]{1,0:T(8,128)S(1)} %convolution_add_fusion, f32[4,256,2048]{2,1,0:T(8,128)S(1)} %copy-done.4), kind=kOutput, calls=%fused_computation | convolution fusion | flops 201457664 | bytes 3211264 | tf_op jit(solution)/shard_map/dot_general | solution.py:13
  (27 shorter events, 0.1 us)
Async XLA Ops:
  0.0 14.8 %copy-start = (f32[64,2048]{1,0:T(8,128)S(1)}, f32[64,2048]{1,0:T(8,128)}, u32[]{:S(2)}) copy-start(f32[64,2048]{1,0:T(8,128)} %own.1) | copy-start | bytes 1572868
  0.0 14.7 %copy-start.10 = (s32[16,4]{0,1:T(4,128)S(1)}, s32[16,4]{0,1:T(4,128)}, u32[]{:S(2)}) copy-start(s32[16,4]{0,1:T(4,128)} %param.11) | copy-start | bytes 772
  0.0 14.8 %copy-start.2 = (s32[16]{0:T(128)S(1)}, s32[16]{0:T(128)}, u32[]{:S(2)}) copy-start(s32[16]{0:T(128)} %count.1) | copy-start | bytes 196
  0.0 14.8 %copy-start.1 = (s32[4096]{0:T(1024)S(1)}, s32[4096]{0:T(1024)}, u32[]{:S(2)}) copy-start(s32[4096]{0:T(1024)} %order.1) | copy-start | bytes 49156
  0.0 14.8 %collective-permute-start = (f32[64,2048]{1,0:T(8,128)}, f32[64,2048]{1,0:T(8,128)S(1)}, u32[]{:S(2)}, u32[]{:S(2)}) collective-permute-start(f32[64,2048]{1,0:T(8,128)} %own.1), channel_id=1, source_target_pairs={{0,1},{1,0},{2,3},{3,2},{4,5},{5,4},{6,7},{7,6},{8,9},{9,8},{10,11... | collective-permute-start | bytes 1572872 | tf_op jit(solution)/shard_map/ppermute | solution.py:18
  12.6 9.5 %collective-permute-start.1 = (f32[256,256]{1,0:T(8,128)}, f32[256,256]{1,0:T(8,128)S(1)}, u32[]{:S(2)}, u32[]{:S(2)}) collective-permute-start(f32[256,256]{1,0:T(8,128)} %get-tuple-element.31), channel_id=1, source_target_pairs={{0,1},{1,0},{2,3},{3,2},{4,5},{5,4},{6,7},{7,6},{8,9},{9,8},{10,11... | collective-permute-start | bytes 786440 | tf_op jit(solution)/shard_map/ppermute | solution.py:18
  13.1 16.1 %collective-permute-start.3 = (f32[256,256]{1,0:T(8,128)}, f32[256,256]{1,0:T(8,128)S(1)}, u32[]{:S(2)}, u32[]{:S(2)}) collective-permute-start(f32[256,256]{1,0:T(8,128)} %get-tuple-element.33), channel_id=1, source_target_pairs={{0,1},{1,0},{2,3},{3,2},{4,5},{5,4},{6,7},{7,6},{8,9},{9,8},{10,11... | collective-permute-start | bytes 786440 | tf_op jit(solution)/shard_map/ppermute | solution.py:18
  14.9 14.4 %copy-start.3 = (f32[4,2048,256]{2,1,0:T(8,128)S(1)}, f32[4,2048,256]{2,1,0:T(8,128)}, u32[]{:S(2)}) copy-start(f32[4,2048,256]{2,1,0:T(8,128)} %proj_hbm.3) | copy-start | bytes 25165828
  21.9 8.6 %copy-start.5 = (f32[1,4,2,256,256]{4,3,2,1,0:T(8,128)S(1)}, f32[1,4,2,256,256]{4,3,2,1,0:T(8,128)}, u32[]{:S(2)}) copy-start(f32[1,4,2,256,256]{4,3,2,1,0:T(8,128)} %param.15) | copy-start | bytes 6291460
  21.9 9.0 %copy-start.9 = (f32[256,256]{1,0:T(8,128)S(1)}, f32[256,256]{1,0:T(8,128)}, u32[]{:S(2)}) copy-start(f32[256,256]{1,0:T(8,128)} %get-tuple-element.31) | copy-start | bytes 786436
  22.2 7.0 %collective-permute-start.2 = (f32[128,256]{1,0:T(8,128)S(1)}, f32[128,256]{1,0:T(8,128)S(1)}, u32[]{:S(2)}, u32[]{:S(2)}) collective-permute-start(f32[128,256]{1,0:T(8,128)S(1)} %get-tuple-element.28), channel_id=1, source_target_pairs={{0,1},{1,0},{2,3},{3,2},{4,5},{5,4},{6,7},{7,6},{8,9},{9,8},{10,11... | collective-permute-start | bytes 393224 | tf_op jit(solution)/shard_map/ppermute | solution.py:18
  29.2 1.3 %collective-permute-start.4 = (f32[64,256]{1,0:T(8,128)S(1)}, f32[64,256]{1,0:T(8,128)S(1)}, u32[]{:S(2)}, u32[]{:S(2)}) collective-permute-start(f32[64,256]{1,0:T(8,128)S(1)} %slice.76), channel_id=1, source_target_pairs={{0,2},{2,0},{1,3},{3,1},{4,6},{6,4},{5,7},{7,5},{8,10},{10,8},{9,1... | collective-permute-start | bytes 196616 | tf_op jit(solution)/shard_map/ppermute | solution.py:18
  29.3 3.5 %copy-start.7 = (f32[256,256]{1,0:T(8,128)S(1)}, f32[256,256]{1,0:T(8,128)}, u32[]{:S(2)}) copy-start(f32[256,256]{1,0:T(8,128)} %get-tuple-element.35) | copy-start | bytes 786436
  29.3 6.7 %copy-start.8 = (f32[256,256]{1,0:T(8,128)S(1)}, f32[256,256]{1,0:T(8,128)}, u32[]{:S(2)}) copy-start(f32[256,256]{1,0:T(8,128)} %get-tuple-element.33) | copy-start | bytes 786436
  30.5 12.0 %copy-start.6 = (f32[768,256]{1,0:T(8,128)S(1)}, f32[768,256]{1,0:T(8,128)}, u32[]{:S(2)}) copy-start(f32[768,256]{1,0:T(8,128)} %get-tuple-element.36) | copy-start | bytes 2359300
  31.0 22.6 %copy-start.4 = (f32[4,256,2048]{2,1,0:T(8,128)S(1)}, f32[4,256,2048]{2,1,0:T(8,128)}, u32[]{:S(2)}) copy-start(f32[4,256,2048]{2,1,0:T(8,128)} %corr_hbm.1) | copy-start | bytes 25165828
  31.2 3.1 %collective-permute-start.5 = (f32[64,256]{1,0:T(8,128)S(1)}, f32[64,256]{1,0:T(8,128)S(1)}, u32[]{:S(2)}, u32[]{:S(2)}) collective-permute-start(f32[64,256]{1,0:T(8,128)S(1)} %slice_subtract_fusion), channel_id=1, source_target_pairs={{0,2},{2,0},{1,3},{3,1},{4,6},{6,4},{5,7},{7,5},{8,10},{10,8},{9,1... | collective-permute-start | bytes 196616 | tf_op jit(solution)/shard_map/ppermute | solution.py:18
  32.1 7.1 %collective-permute-start.7 = (f32[64,256]{1,0:T(8,128)S(1)}, f32[64,256]{1,0:T(8,128)S(1)}, u32[]{:S(2)}, u32[]{:S(2)}) collective-permute-start(f32[64,256]{1,0:T(8,128)S(1)} %fusion.4), channel_id=1, source_target_pairs={{0,1},{1,0},{2,3},{3,2},{4,5},{5,4},{6,7},{7,6},{8,9},{9,8},{10,11... | collective-permute-start | bytes 196616 | tf_op jit(solution)/shard_map/ppermute | solution.py:18
  32.8 9.4 %collective-permute-start.8 = (f32[256,256]{1,0:T(8,128)S(1)}, f32[256,256]{1,0:T(8,128)S(1)}, u32[]{:S(2)}, u32[]{:S(2)}) collective-permute-start(f32[256,256]{1,0:T(8,128)S(1)} %copy-done.7), channel_id=1, source_target_pairs={{0,1},{1,0},{2,3},{3,2},{4,5},{5,4},{6,7},{7,6},{8,9},{9,8},{10,11... | collective-permute-start | bytes 786440 | tf_op jit(solution)/shard_map/ppermute | solution.py:18
  34.3 4.5 %collective-permute-start.6 = (f32[64,256]{1,0:T(8,128)S(1)}, f32[64,256]{1,0:T(8,128)S(1)}, u32[]{:S(2)}, u32[]{:S(2)}) collective-permute-start(f32[64,256]{1,0:T(8,128)S(1)} %add.60), channel_id=1, source_target_pairs={{0,4},{4,0},{1,5},{5,1},{2,6},{6,2},{3,7},{7,3},{8,12},{12,8},{9,1... | collective-permute-start | bytes 196616 | tf_op jit(solution)/shard_map/ppermute | solution.py:18
  42.4 1.3 %collective-permute-start.9 = (f32[64,256]{1,0:T(8,128)S(1)}, f32[64,256]{1,0:T(8,128)S(1)}, u32[]{:S(2)}, u32[]{:S(2)}) collective-permute-start(f32[64,256]{1,0:T(8,128)S(1)} %subtract_subtract_fusion), channel_id=1, source_target_pairs={{0,2},{2,0},{1,3},{3,1},{4,6},{6,4},{5,7},{7,5},{8,10},{10,8},{9,1... | collective-permute-start | bytes 196616 | tf_op jit(solution)/shard_map/ppermute | solution.py:18
  43.8 5.9 %collective-permute-start.11 = (f32[64,256]{1,0:T(8,128)S(1)}, f32[64,256]{1,0:T(8,128)S(1)}, u32[]{:S(2)}, u32[]{:S(2)}) collective-permute-start(f32[64,256]{1,0:T(8,128)S(1)} %add.65), channel_id=1, source_target_pairs={{0,12},{4,8},{8,4},{12,0},{1,13},{5,9},{9,5},{13,1},{2,14},{6,10},... | collective-permute-start | bytes 196616 | tf_op jit(solution)/shard_map/ppermute | solution.py:18
  46.6 6.2 %collective-permute-start.12 = (f32[64,256]{1,0:T(8,128)S(1)}, f32[64,256]{1,0:T(8,128)S(1)}, u32[]{:S(2)}, u32[]{:S(2)}) collective-permute-start(f32[64,256]{1,0:T(8,128)S(1)} %add.65), channel_id=1, source_target_pairs={{0,8},{4,12},{8,0},{12,4},{1,9},{5,13},{9,1},{13,5},{2,10},{6,14},... | collective-permute-start | bytes 196616 | tf_op jit(solution)/shard_map/ppermute | solution.py:18
  47.6 5.4 %collective-permute-start.10 = (f32[64,256]{1,0:T(8,128)S(1)}, f32[64,256]{1,0:T(8,128)S(1)}, u32[]{:S(2)}, u32[]{:S(2)}) collective-permute-start(f32[64,256]{1,0:T(8,128)S(1)} %add.65), channel_id=1, source_target_pairs={{0,4},{4,0},{8,12},{12,8},{1,5},{5,1},{9,13},{13,9},{2,6},{6,2},{1... | collective-permute-start | bytes 196616 | tf_op jit(solution)/shard_map/ppermute | solution.py:18
  53.5 1.3 %collective-permute-start.13 = (f32[64,256]{1,0:T(8,128)S(1)}, f32[64,256]{1,0:T(8,128)S(1)}, u32[]{:S(2)}, u32[]{:S(2)}) collective-permute-start(f32[64,256]{1,0:T(8,128)S(1)} %convolution_subtract_fusion.4), channel_id=1, source_target_pairs={{0,2},{2,0},{1,3},{3,1},{4,6},{6,4},{5,7},{7,5},{8,10},{10,8},{9,1... | collective-permute-start | bytes 196616 | tf_op jit(solution)/shard_map/ppermute | solution.py:18
  54.8 4.9 %collective-permute-start.14 = (f32[64,256]{1,0:T(8,128)S(1)}, f32[64,256]{1,0:T(8,128)S(1)}, u32[]{:S(2)}, u32[]{:S(2)}) collective-permute-start(f32[64,256]{1,0:T(8,128)S(1)} %add.69), channel_id=1, source_target_pairs={{0,4},{4,0},{8,12},{12,8},{1,5},{5,1},{9,13},{13,9},{2,6},{6,2},{1... | collective-permute-start | bytes 196616 | tf_op jit(solution)/shard_map/ppermute | solution.py:18
  55.3 5.5 %collective-permute-start.15 = (f32[64,256]{1,0:T(8,128)S(1)}, f32[64,256]{1,0:T(8,128)S(1)}, u32[]{:S(2)}, u32[]{:S(2)}) collective-permute-start(f32[64,256]{1,0:T(8,128)S(1)} %add.69), channel_id=1, source_target_pairs={{0,12},{4,8},{8,4},{12,0},{1,13},{5,9},{9,5},{13,1},{2,14},{6,10},... | collective-permute-start | bytes 196616 | tf_op jit(solution)/shard_map/ppermute | solution.py:18
  57.1 5.8 %collective-permute-start.16 = (f32[64,256]{1,0:T(8,128)S(1)}, f32[64,256]{1,0:T(8,128)S(1)}, u32[]{:S(2)}, u32[]{:S(2)}) collective-permute-start(f32[64,256]{1,0:T(8,128)S(1)} %add.69), channel_id=1, source_target_pairs={{0,8},{4,12},{8,0},{12,4},{1,9},{5,13},{9,1},{13,5},{2,10},{6,14},... | collective-permute-start | bytes 196616 | tf_op jit(solution)/shard_map/ppermute | solution.py:18
  62.9 5.9 %collective-permute-start.18 = (f32[64,256]{1,0:T(8,128)S(1)}, f32[64,256]{1,0:T(8,128)S(1)}, u32[]{:S(2)}, u32[]{:S(2)}) collective-permute-start(f32[64,256]{1,0:T(8,128)S(1)} %add_add_fusion), channel_id=1, source_target_pairs={{0,17},{1,16},{2,19},{3,18},{4,21},{5,20},{6,23},{7,22},{8,25},{9,... | collective-permute-start | bytes 196616 | tf_op jit(solution)/shard_map/ppermute | solution.py:18
  65.2 5.8 %collective-permute-start.19 = (f32[64,256]{1,0:T(8,128)S(1)}, f32[64,256]{1,0:T(8,128)S(1)}, u32[]{:S(2)}, u32[]{:S(2)}) collective-permute-start(f32[64,256]{1,0:T(8,128)S(1)} %add_add_fusion), channel_id=1, source_target_pairs={{0,16},{1,17},{2,18},{3,19},{4,20},{5,21},{6,22},{7,23},{8,24},{9,... | collective-permute-start | bytes 196616 | tf_op jit(solution)/shard_map/ppermute | solution.py:18
  66.7 4.4 %collective-permute-start.17 = (f32[64,256]{1,0:T(8,128)S(1)}, f32[64,256]{1,0:T(8,128)S(1)}, u32[]{:S(2)}, u32[]{:S(2)}) collective-permute-start(f32[64,256]{1,0:T(8,128)S(1)} %add_add_fusion), channel_id=1, source_target_pairs={{0,1},{1,0},{2,3},{3,2},{4,5},{5,4},{6,7},{7,6},{8,9},{9,8},{10,11... | collective-permute-start | bytes 196616 | tf_op jit(solution)/shard_map/ppermute | solution.py:18

commit v5 on v4

--- a/solution.py
+++ b/solution.py
@@ -125,17 +125,49 @@
             pltpu.SemaphoreType.DMA,
             pltpu.SemaphoreType.DMA,
         ],
-        compiler_params=pltpu.CompilerParams(vmem_limit_bytes=48 << 20),
+        compiler_params=pltpu.CompilerParams(vmem_limit_bytes=24 << 20),
         cost_estimate=pl.CostEstimate(flops=200_000_000, bytes_accessed=8 << 20, transcendentals=0),
         name="near",
     )(order, index, count, side, own, other,
       *(pltpu.with_memory_space_constraint(v, pltpu.HBM) for v in (tiles, proj)))
 
-def gram_kernel(corr_hbm, proj_hbm, *rest):
+def later_kernel(current, proj_hbm, reduced, proj, sems):
+    rows = current.shape[0]
+    loads = [pltpu.make_async_copy(proj_hbm.at[level + 2], proj.at[level], sems.at[level])
+             for level in range(2)]
+    for load in loads:
+        load.start()
+    left = stacked(current[...])
+    for level in range(2):
+        loads[level].wait()
+        high, low = parts(proj[level])
+        both = mm(left, high)
+        reduced[level * rows:(level + 1) * rows, :] = (
+            both[:rows] + both[rows:] + mm(left[:rows], low))
+
+
+def later_call(current, proj):
+    rows, points = current.shape
+    rank = proj.shape[-1]
+    vmem = pl.BlockSpec(memory_space=pltpu.VMEM)
+    return pl.pallas_call(
+        later_kernel,
+        out_shape=jax.ShapeDtypeStruct((2 * rows, rank), jnp.float32),
+        in_specs=[vmem, pl.BlockSpec(memory_space=pltpu.HBM)],
+        out_specs=vmem,
+        scratch_shapes=[pltpu.VMEM((2, points, rank), jnp.float32), pltpu.SemaphoreType.DMA((2,))],
+        compiler_params=pltpu.CompilerParams(vmem_limit_bytes=16 << 20),
+        cost_estimate=pl.CostEstimate(
+            flops=12 * rows * points * rank, bytes_accessed=4 << 20, transcendentals=0),
+        name="later",
+    )(current, pltpu.with_memory_space_constraint(proj, pltpu.HBM))
+
+
+def gram_kernel(corr_hbm, proj_hbm, coup_hbm, *rest):
     levels, points, rank = proj_hbm.shape
-    early, second, mid, late, corr, proj, sems = rest
-    targets = {(0, 0): (early, 0), (1, 0): (second, 0), (1, 1): (mid, 0),
-               (2, 0): (late, 0), (2, 1): (late, 1), (2, 2): (late, 2)}
+    early, second, mid, late, fold, corr, proj, coup, sems, coup_sem = rest
+    load_coup = pltpu.make_async_copy(coup_hbm.at[0, levels - 2], coup, coup_sem)
+    load_coup.start()
     loads = {}
     for level in range(levels - 1):
         loads["c", level] = pltpu.make_async_copy(corr_hbm.at[level], corr.at[level], sems.at[level])
@@ -143,6 +175,8 @@
             proj_hbm.at[level + 1], proj.at[level], sems.at[levels - 1 + level])
         loads["c", level].start()
         loads["p", level].start()
+    targets = {(0, 0): (early, 0), (1, 0): (second, 0), (1, 1): (mid, 0),
+               (2, 0): (late, 0), (2, 1): (late, 1), (2, 2): (late, 2)}
     lefts = []
     for above in range(levels - 1):
         loads["c", above].wait()
@@ -155,27 +189,37 @@
             target, place = targets[above, below]
             target[place * rank:(place + 1) * rank, :] = (
                 mm(left_high, high) + mm(left_high, low) + mm(left_low, high))
-
-def gram_call(corr, proj):
+    load_coup.wait()
+    left_high, left_low = parts(coup[...].reshape(2 * rank, rank))
+    high, low = parts(late[2 * rank:3 * rank, :])
+    out = mm(left_high, high) + mm(left_high, low) + mm(left_low, high)
+    for part in range(2):
+        fold[part] = out[:, part * rank // 2:(part + 1) * rank // 2]
+
+
+def gram_call(corr, proj, coup):
     levels, points, rank = proj.shape
     pairs = levels * (levels - 1) // 2
     hbm = pl.BlockSpec(memory_space=pltpu.HBM)
     vmem = pl.BlockSpec(memory_space=pltpu.VMEM)
     return pl.pallas_call(
         gram_kernel,
-        out_shape=[jax.ShapeDtypeStruct((above * rank, rank), jnp.float32) for above in (1, 1, 1, 3)],
-        in_specs=[hbm, hbm],
-        out_specs=[vmem] * levels,
+        out_shape=[jax.ShapeDtypeStruct((above * rank, rank), jnp.float32) for above in (1, 1, 1, 3)]
+        + [jax.ShapeDtypeStruct((2, 2 * rank, rank // 2), jnp.float32)],
+        in_specs=[hbm, hbm, hbm],
+        out_specs=[vmem] * (levels + 1),
         scratch_shapes=[
             pltpu.VMEM((levels - 1, rank, points), jnp.float32),
             pltpu.VMEM((levels - 1, points, rank), jnp.float32),
+            pltpu.VMEM((2, rank, rank), jnp.float32),
             pltpu.SemaphoreType.DMA((2 * levels - 2,)),
+            pltpu.SemaphoreType.DMA,
         ],
-        compiler_params=pltpu.CompilerParams(vmem_limit_bytes=54 << 20),
+        compiler_params=pltpu.CompilerParams(vmem_limit_bytes=32 << 20),
         cost_estimate=pl.CostEstimate(
             flops=6 * pairs * points * rank * rank, bytes_accessed=12 << 20, transcendentals=0),
         name="gram",
-    )(*(pltpu.with_memory_space_constraint(v, pltpu.HBM) for v in (corr, proj)))
+    )(*(pltpu.with_memory_space_constraint(v, pltpu.HBM) for v in (corr, proj, coup)))
 
 
 def local(
@@ -184,24 +228,29 @@
     tie = lax.optimization_barrier
     rank = proj_basis.shape[-1]
     other = over_rhs(charges)
-    early, second, mid, late = gram_call(corr_basis, proj_basis)
+    early, second, mid, late, fold = gram_call(corr_basis, proj_basis, coupling)
     early_other = over_rhs(early)
-    second_other = over_rhs(second)
-    other, early, second, mid, late = tie((other, early, second, mid, late))
+    other, early, second, mid, late, fold = tie((other, early, second, mid, late, fold))
     side = lax.axis_index("rhs").astype(jnp.int32).reshape(1)
+    rows = charges.shape[0]
+    core = lax.axis_index("core") == 0
+
+    def swapped(value):
+        return jnp.concatenate([value[rank:], value[:rank]], axis=0)
+
+    fold = jnp.where(core, fold[0], fold[1]) + swap(jnp.where(core, fold[1], fold[0]), ("core",), 1)
+    fold_other = swap(fold, ("x0",), 1)
     current, pair = near_call(
         cluster_order, near_index, near_count, side, charges, other, near_tiles, proj_basis
     )
-    pair, early_other = tie((pair, early_other))
+    pair, early_other, fold_other = tie((pair, early_other, fold_other))
     early = early + early_other
+    fold = fold + fold_other
     pair = pair + over_rhs(pair)
-    own, sum1 = pair[:charges.shape[0]], pair[charges.shape[0]:]
-    own, mid, second_other = tie((own, mid, second_other))
-    second = second + second_other
-    mid = mid + over_rhs(mid)
-    part2 = dot(current, proj_basis[2])
-    sum2 = part2 + over_rhs(part2)
-    part3 = dot(current, proj_basis[3])
+    own, sum1 = pair[:rows], pair[rows:]
+    later = later_call(current, proj_basis)
+    own, later = tie((own, later))
+    part2, part3 = later[:rows], later[rows:]
 
     def coefficients(height, own, sib):
         return dot(own, coupling[0, height, 0]) + dot(sib, coupling[0, height, 1])
@@ -209,22 +258,30 @@
     coeff0 = coefficients(0, own, swap(own, ("core",), 1))
     own = sum1 - dot(coeff0, early)
     own = own + swap(own, ("core",), 1)
-    current = current - dot(coeff0, corr_basis[0])
-    sum2 = sum2 - dot(coeff0, second)
+    own, fold = tie((own, fold))
+    fold = fold + swapped(swap(fold, ("x1", "x0"), 3))
+    part2 = part2 - dot(coeff0, second)
     part3 = part3 - dot(coeff0, late[:rank])
     coeff1 = coefficients(1, own, swap(own, ("x0",), 1))
-    own = sum2 - dot(coeff1, mid)
-    own = own + swap(own, ("core",), 1)
-    current = current - dot(coeff1, corr_basis[1])
+    own = part2 - dot(coeff1, mid)
+    own = own + over_rhs(own)
     part3 = part3 - dot(coeff1, late[rank:2 * rank])
-    near, far, across = (swap(own, ("x1", "x0"), mask) for mask in (1, 3, 2))
-    coeff2 = coefficients(2, own + near, far + across)
-    own = part3 - dot(coeff2, late[2 * rank:])
-    own = own + swap(own, ("core",), 1)
+    both = jnp.concatenate([own, part3], axis=0)
+    both = both + swap(both, ("core",), 1)
+    both, fold, coeff0, coeff1 = tie((both, fold, coeff0, coeff1))
+    fold_other = swap(fold, ("core",), 1)
+    fold = jnp.concatenate(
+        [jnp.where(core, fold, fold_other), jnp.where(core, fold_other, fold)], axis=1)
+    current = current - dot(
+        jnp.concatenate([coeff0, coeff1], axis=1), corr_basis[:2].reshape(2 * rank, -1))
+    near, far, across = (swap(both, ("x1", "x0"), mask) for mask in (1, 3, 2))
+    near = both + near
+    far = far + across
+    own, sib = near[:rows], far[:rows]
+    coeff2 = coefficients(2, own, sib)
+    own = (near[rows:] + far[rows:]) - (dot(own, fold[:rank]) + dot(sib, fold[rank:]))
+    near, far, across = (swap(own, RING, mask) for mask in (1, 17, 16))
     current = current - dot(coeff2, corr_basis[2])
-    near, far, across = (swap(own, ("x1", "x0"), mask) for mask in (1, 3, 2))
-    own = (own + near) + (far + across)
-    near, far, across = (swap(own, RING, mask) for mask in (1, 17, 16))
     coeff3 = coefficients(3, own + near, far + across)
     return current - dot(coeff3, corr_basis[3])
 

time: 73.1 us -> 66.5 us (0.910)
  waiting for transfers between devices: 24.9 us -> 18.6 us
  Pallas kernels: 17.9 us -> 20.2 us
  starting transfers between devices: 21.4 us -> 19.6 us
  matrix products: 8.22 us -> 7.12 us
    ppermute x20 -> x18, waiting for transfers between devices: 24.9 us -> 18.6 us  [swap(): return lax.ppermute(block, axes, [(i, i ^ mask) for i in range(count)])]
    pallas_call x0 -> x1, Pallas kernels: none -> 3.15 us  [later_call(): pl.pallas_call(later_kernel, out_shape=jax.ShapeDtypeStruct((2 * rows, ra...]
    ppermute x20 -> x18, starting transfers between devices: 21.4 us -> 19.6 us  [swap(): return lax.ppermute(block, axes, [(i, i ^ mask) for i in range(count)])]
    dot_general x20 -> x18, matrix products: 8.22 us -> 7.12 us  [dot(): return jnp.dot(a, b, precision=FAST, preferred_element_type=jnp.float32)]
  transfers between devices with their start and end apart: 20 -> 18, of which waited for: 13 -> 14; matrix products, arithmetic and copies ran while one was open for 7% -> 7% of each run, Pallas kernels for 25% -> 31%
where the time goes in v5:
time: 66.5 us; the launch traced here: 66.3 us
  Pallas kernels  20.2 us (30%)
  starting transfers between devices  19.6 us (29%)
  waiting for transfers between devices  18.6 us (28%)
  matrix products  7.12 us (11%)
    ppermute x18, starting transfers between devices, swap(): return lax.ppermute(block, axes, [(i, i ^ mask) for i in range(count)])  19.6 us
    ppermute x18, waiting for transfers between devices, swap(): return lax.ppermute(block, axes, [(i, i ^ mask) for i in range(count)])  18.6 us
    pallas_call x1, Pallas kernels, gram_call(): pl.pallas_call(gram_kernel, out_shape=[jax.ShapeDtypeStruct((above * rank...  10.4 us
    dot_general x18, matrix products, dot(): return jnp.dot(a, b, precision=FAST, preferred_element_type=jnp.float32)  7.12 us
    pallas_call x1, Pallas kernels, near_call(): pl.pallas_call(near_kernel, out_shape=(jax.ShapeDtypeStruct((rows, half),...  6.69 us
    pallas_call x1, Pallas kernels, later_call(): pl.pallas_call(later_kernel, out_shape=jax.ShapeDtypeStruct((2 * rows, ra...  3.15 us
  transfers between devices with their start and end apart: 18, of which 14 were waited for; matrix products, arithmetic and copies ran while one was open for 7% of the time, Pallas kernels for 31%

profile of v5, /device:TPU:0, one launch (start us, length us, event | category | flops | bytes accessed | tf_op | source)
XLA Modules:
  0.0 66.3 jit_solution(10832062531937989608)
XLA Ops:
  0.0 1.7 %collective-permute-start = (f32[64,2048]{1,0:T(8,128)}, f32[64,2048]{1,0:T(8,128)S(1)}, u32[]{:S(2)}, u32[]{:S(2)}) collective-permute-start(f32[64,2048]{1,0:T(8,128)} %own.1), channel_id=1, source_target_pairs={{0,1},{1,0},{2,3},{3,2},{4,5},{5,4},{6,7},{7,6},{8,9},{9,8},{10,11... | collective-permute-start | bytes 1572872 | tf_op jit(solution)/shard_map/ppermute | solution.py:18
  1.7 10.4 %gram.1 = (f32[256,256]{1,0:T(8,128)S(1)}, f32[256,256]{1,0:T(8,128)S(1)}, f32[256,256]{1,0:T(8,128)S(1)}, f32[768,256]{1,0:T(8,128)S(1)}, f32[2,512,128]{2,1,0:T(8,128)S(1)}) custom-call(f32[4,256,2048]{2,1,0:T(8,128)} %corr_hbm.1, f32[4,2048,256]{2,1,0:T(8,128)} %proj_hbm.5, f32[1,4,2,256,256]{4,3,2,1,0:T(8,128)} %coup_hbm.1), custom_call_target="tpu_custom_call" | custom-call | flops 4831838208 | bytes 12582912 | tf_op jit(solution)/shard_map/gram/pallas_call | solution.py:205
  12.1 0.0 copy-start
  12.1 1.7 %collective-permute-done.other = f32[64,2048]{1,0:T(8,128)S(1)} collective-permute-done((f32[64,2048]{1,0:T(8,128)}, f32[64,2048]{1,0:T(8,128)S(1)}, u32[]{:S(2)}, u32[]{:S(2)}) %collective-permute-start) | collective-permute-done | bytes 524320 | tf_op jit(solution)/shard_map/ppermute | solution.py:18
  13.8 0.1 collective-permute-start.2
  13.9 1.8 %collective-permute-start.1 = (f32[256,256]{1,0:T(8,128)S(1)}, f32[256,256]{1,0:T(8,128)S(1)}, u32[]{:S(2)}, u32[]{:S(2)}) collective-permute-start(f32[256,256]{1,0:T(8,128)S(1)} %get-tuple-element.42), channel_id=1, source_target_pairs={{0,1},{1,0},{2,3},{3,2},{4,5},{5,4},{6,7},{7,6},{8,9},{9,8},{10,11... | collective-permute-start | bytes 786440 | tf_op jit(solution)/shard_map/ppermute | solution.py:18
  15.7 0.0 collective-permute-done.2
  15.8 1.6 %collective-permute-start.3 = (f32[512,128]{1,0:T(8,128)S(1)}, f32[512,128]{1,0:T(8,128)S(1)}, u32[]{:S(2)}, u32[]{:S(2)}) collective-permute-start(f32[512,128]{1,0:T(8,128)S(1)} %bitcast_add_fusion), channel_id=1, source_target_pairs={{0,4},{4,0},{1,5},{5,1},{2,6},{6,2},{3,7},{7,3},{8,12},{12,8},{9,1... | collective-permute-start | bytes 786440 | tf_op jit(solution)/shard_map/ppermute | solution.py:18
  17.4 0.0 copy-done.4
  17.4 0.1 copy.9.index
  17.4 0.0 copy-done.1
  17.4 0.0 copy-done.2
  17.4 0.0 copy-done
  17.5 6.7 %near.1 = (f32[64,2048]{1,0:T(8,128)S(1)}, f32[128,256]{1,0:T(8,128)S(1)}) custom-call(s32[4096]{0:T(1024)S(1)} %copy-done.1, s32[16,4]{1,0:T(8,128)S(1)} %copy.9.index, s32[16]{0:T(128)S(1)} %copy-done.2, s32[1]{0:T(128)} %bitcast.side, f32[64,2048]{1,0:T(8,128)S(1)} %copy-done, f32[64,2048]{1,0:T(8,128)S(1)} %collective-permute-done.other, ...), custom_call_target="tpu_custom_call" | custom-call | flops 200000000 | bytes 8388608 | tf_op jit(solution)/shard_map/near/pallas_call | solution.py:112
  24.2 0.0 collective-permute-done.1
  24.2 0.1 collective-permute-done.3
  24.2 1.5 %collective-permute-start.4 = (f32[128,256]{1,0:T(8,128)S(1)}, f32[128,256]{1,0:T(8,128)S(1)}, u32[]{:S(2)}, u32[]{:S(2)}) collective-permute-start(f32[128,256]{1,0:T(8,128)S(1)} %get-tuple-element.38), channel_id=1, source_target_pairs={{0,1},{1,0},{2,3},{3,2},{4,5},{5,4},{6,7},{7,6},{8,9},{9,8},{10,11... | collective-permute-start | bytes 393224 | tf_op jit(solution)/shard_map/ppermute | solution.py:18
  25.7 3.2 %later.1 = f32[128,256]{1,0:T(8,128)S(1)} custom-call(f32[64,2048]{1,0:T(8,128)S(1)} %get-tuple-element.35.current, f32[4,2048,256]{2,1,0:T(8,128)} %proj_hbm.5), custom_call_target="tpu_custom_call" | custom-call | flops 402653184 | bytes 4194304 | tf_op jit(solution)/shard_map/later/pallas_call | solution.py:153
  28.8 1.2 %collective-permute-done.4 = f32[128,256]{1,0:T(8,128)S(1)} collective-permute-done((f32[128,256]{1,0:T(8,128)S(1)}, f32[128,256]{1,0:T(8,128)S(1)}, u32[]{:S(2)}, u32[]{:S(2)}) %collective-permute-start.4) | collective-permute-done | bytes 131104 | tf_op jit(solution)/shard_map/ppermute | solution.py:18
  30.1 0.1 collective-permute-start.5
  30.2 0.2 fusion.19
  30.4 1.0 %collective-permute-done.5 = f32[64,256]{1,0:T(8,128)S(1)} collective-permute-done((f32[64,256]{1,0:T(8,128)S(1)}, f32[64,256]{1,0:T(8,128)S(1)}, u32[]{:S(2)}, u32[]{:S(2)}) %collective-permute-start.5) | collective-permute-done | bytes 65568 | tf_op jit(solution)/shard_map/ppermute | solution.py:18
  31.4 0.2 convolution_add_fusion.4
  31.6 0.2 slice_subtract_fusion
  31.8 0.2 collective-permute-start.6
  32.1 1.1 %collective-permute-done.6 = f32[64,256]{1,0:T(8,128)S(1)} collective-permute-done((f32[64,256]{1,0:T(8,128)S(1)}, f32[64,256]{1,0:T(8,128)S(1)}, u32[]{:S(2)}, u32[]{:S(2)}) %collective-permute-start.6) | collective-permute-done | bytes 65568 | tf_op jit(solution)/shard_map/ppermute | solution.py:18
  33.2 0.9 %collective-permute-start.7 = (f32[64,256]{1,0:T(8,128)S(1)}, f32[64,256]{1,0:T(8,128)S(1)}, u32[]{:S(2)}, u32[]{:S(2)}) collective-permute-start(f32[64,256]{1,0:T(8,128)S(1)} %add.58), channel_id=1, source_target_pairs={{0,4},{4,0},{1,5},{5,1},{2,6},{6,2},{3,7},{7,3},{8,12},{12,8},{9,1... | collective-permute-start | bytes 196616 | tf_op jit(solution)/shard_map/ppermute | solution.py:18
  34.1 0.2 convolution_subtract_fusion.4
  34.3 2.7 %collective-permute-start.10 = (f32[512,128]{1,0:T(8,128)S(1)}, f32[512,128]{1,0:T(8,128)S(1)}, u32[]{:S(2)}, u32[]{:S(2)}) collective-permute-start(f32[512,128]{1,0:T(8,128)S(1)} %add.59), channel_id=1, source_target_pairs={{0,12},{4,8},{8,4},{12,0},{1,13},{5,9},{9,5},{13,1},{2,14},{6,10},... | collective-permute-start | bytes 786440 | tf_op jit(solution)/shard_map/ppermute | solution.py:18
  37.1 0.6 collective-permute-done.7
  37.7 0.2 fusion.15
  37.9 0.2 convolution_add_fusion.3
  38.1 0.2 fusion.52
  38.4 0.2 fusion.4
  38.6 0.0 slice-start.1
  38.6 1.3 %collective-permute-start.8 = (f32[64,256]{1,0:T(8,128)S(1)}, f32[64,256]{1,0:T(8,128)S(1)}, u32[]{:S(2)}, u32[]{:S(2)}) collective-permute-start(f32[64,256]{1,0:T(8,128)S(1)} %fusion.4), channel_id=1, source_target_pairs={{0,1},{1,0},{2,3},{3,2},{4,5},{5,4},{6,7},{7,6},{8,9},{9,8},{10,11... | collective-permute-start | bytes 196616 | tf_op jit(solution)/shard_map/ppermute | solution.py:18
  39.8 0.2 convolution_subtract_fusion.3
  40.1 2.9 %collective-permute-done.8 = f32[64,256]{1,0:T(8,128)S(1)} collective-permute-done((f32[64,256]{1,0:T(8,128)S(1)}, f32[64,256]{1,0:T(8,128)S(1)}, u32[]{:S(2)}, u32[]{:S(2)}) %collective-permute-start.8) | collective-permute-done | bytes 65568 | tf_op jit(solution)/shard_map/ppermute | solution.py:18
  43.0 0.1 collective-permute-start.9
  43.1 0.6 collective-permute-done.10
  43.8 0.6 collective-permute-done.9
  44.4 2.9 %collective-permute-start.13 = (f32[128,256]{1,0:T(8,128)S(1)}, f32[128,256]{1,0:T(8,128)S(1)}, u32[]{:S(2)}, u32[]{:S(2)}) collective-permute-start(f32[128,256]{1,0:T(8,128)S(1)} %fusion.50), channel_id=1, source_target_pairs={{0,8},{4,12},{8,0},{12,4},{1,9},{5,13},{9,1},{13,5},{2,10},{6,14},... | collective-permute-start | bytes 393224 | tf_op jit(solution)/shard_map/ppermute | solution.py:18
  47.3 0.6 collective-permute-start.12
  47.8 0.1 collective-permute-start.11
  48.0 0.0 collective-permute-start.14
  48.0 1.6 %convolution_subtract_fusion.2 = f32[64,2048]{1,0:T(8,128)S(1)} fusion(f32[64,2048]{1,0:T(8,128)S(1)} %get-tuple-element.35.current, f32[512,2048]{1,0:T(8,128)S(1)} %bitcast.52, f32[64,256]{1,0:T(8,128)S(1)} %convolution_add_fusion.3, f32[64,256]{1,0:T(8,128)S(1)} %convolution_add_fusion.4), kind=kOutput, calls=%fused_computation.2 | convolution fusion | flops 402817024 | bytes 5373952 | tf_op jit(solution)/shard_map/dot_general | solution.py:13
  49.6 2.0 %collective-permute-done.13 = f32[128,256]{1,0:T(8,128)S(1)} collective-permute-done((f32[128,256]{1,0:T(8,128)S(1)}, f32[128,256]{1,0:T(8,128)S(1)}, u32[]{:S(2)}, u32[]{:S(2)}) %collective-permute-start.13) | collective-permute-done | bytes 131104 | tf_op jit(solution)/shard_map/ppermute | solution.py:18
  51.6 2.7 %collective-permute-done.12 = f32[128,256]{1,0:T(8,128)S(1)} collective-permute-done((f32[128,256]{1,0:T(8,128)S(1)}, f32[128,256]{1,0:T(8,128)S(1)}, u32[]{:S(2)}, u32[]{:S(2)}) %collective-permute-start.12) | collective-permute-done | bytes 131104 | tf_op jit(solution)/shard_map/ppermute | solution.py:18
  54.4 0.2 fusion.12
  54.6 0.0 collective-permute-done.11
  54.6 0.2 convolution_add_fusion.2
  54.9 0.0 collective-permute-done.14
  54.9 0.2 fusion.7
  55.1 0.2 fusion.36
  55.4 3.1 %collective-permute-start.17 = (f32[64,256]{1,0:T(8,128)S(1)}, f32[64,256]{1,0:T(8,128)S(1)}, u32[]{:S(2)}, u32[]{:S(2)}) collective-permute-start(f32[64,256]{1,0:T(8,128)S(1)} %fusion.36), channel_id=1, source_target_pairs={{0,16},{1,17},{2,18},{3,19},{4,20},{5,21},{6,22},{7,23},{8,24},{9,... | collective-permute-start | bytes 196616 | tf_op jit(solution)/shard_map/ppermute | solution.py:18
  58.5 0.9 %collective-permute-start.16 = (f32[64,256]{1,0:T(8,128)S(1)}, f32[64,256]{1,0:T(8,128)S(1)}, u32[]{:S(2)}, u32[]{:S(2)}) collective-permute-start(f32[64,256]{1,0:T(8,128)S(1)} %fusion.36), channel_id=1, source_target_pairs={{0,17},{1,16},{2,19},{3,18},{4,21},{5,20},{6,23},{7,22},{8,25},{9,... | collective-permute-start | bytes 196616 | tf_op jit(solution)/shard_map/ppermute | solution.py:18
  59.4 0.8 %convolution_subtract_fusion.1 = f32[64,2048]{1,0:T(8,128)S(1)} fusion(f32[64,2048]{1,0:T(8,128)S(1)} %convolution_subtract_fusion.2, f32[64,256]{1,0:T(8,128)S(1)} %convolution_add_fusion.2, f32[4,256,2048]{2,1,0:T(8,128)S(1)} %bitcast.51), kind=kOutput, calls=%fused_computation.1 | convolution fusion | flops 201457664 | bytes 3211264 | tf_op jit(solution)/shard_map/dot_general | solution.py:13
  60.2 0.1 collective-permute-start.15
  60.2 1.0 %collective-permute-done.17 = f32[64,256]{1,0:T(8,128)S(1)} collective-permute-done((f32[64,256]{1,0:T(8,128)S(1)}, f32[64,256]{1,0:T(8,128)S(1)}, u32[]{:S(2)}, u32[]{:S(2)}) %collective-permute-start.17) | collective-permute-done | bytes 65568 | tf_op jit(solution)/shard_map/ppermute | solution.py:18
  61.2 2.7 %collective-permute-done.16 = f32[64,256]{1,0:T(8,128)S(1)} collective-permute-done((f32[64,256]{1,0:T(8,128)S(1)}, f32[64,256]{1,0:T(8,128)S(1)}, u32[]{:S(2)}, u32[]{:S(2)}) %collective-permute-start.16) | collective-permute-done | bytes 65568 | tf_op jit(solution)/shard_map/ppermute | solution.py:18
  63.9 0.2 fusion.9
  64.2 0.3 collective-permute-done.15
  64.5 0.2 convolution_add_fusion
  64.7 1.6 %convolution_subtract_fusion = f32[64,2048]{1,0:T(8,128)} fusion(f32[64,2048]{1,0:T(8,128)S(1)} %convolution_subtract_fusion.1, f32[64,256]{1,0:T(8,128)S(1)} %convolution_add_fusion, f32[4,256,2048]{2,1,0:T(8,128)S(1)} %bitcast.51), kind=kOutput, calls=%fused_computation | convolution fusion | flops 201457664 | bytes 3211264 | tf_op jit(solution)/shard_map/dot_general | solution.py:13
  (25 shorter events, 0.3 us)
Async XLA Ops:
  0.0 13.8 %collective-permute-start = (f32[64,2048]{1,0:T(8,128)}, f32[64,2048]{1,0:T(8,128)S(1)}, u32[]{:S(2)}, u32[]{:S(2)}) collective-permute-start(f32[64,2048]{1,0:T(8,128)} %own.1), channel_id=1, source_target_pairs={{0,1},{1,0},{2,3},{3,2},{4,5},{5,4},{6,7},{7,6},{8,9},{9,8},{10,11... | collective-permute-start | bytes 1572872 | tf_op jit(solution)/shard_map/ppermute | solution.py:18
  1.7 15.7 %copy-start.4 = (s32[16,4]{0,1:T(4,128)S(1)}, s32[16,4]{0,1:T(4,128)}, u32[]{:S(2)}) copy-start(s32[16,4]{0,1:T(4,128)} %param.11) | copy-start | bytes 772
  1.7 15.8 %copy-start.1 = (s32[4096]{0:T(1024)S(1)}, s32[4096]{0:T(1024)}, u32[]{:S(2)}) copy-start(s32[4096]{0:T(1024)} %order.1) | copy-start | bytes 49156
  1.7 15.8 %copy-start.2 = (s32[16]{0:T(128)S(1)}, s32[16]{0:T(128)}, u32[]{:S(2)}) copy-start(s32[16]{0:T(128)} %count.1) | copy-start | bytes 196
  12.1 5.4 %copy-start = (f32[64,2048]{1,0:T(8,128)S(1)}, f32[64,2048]{1,0:T(8,128)}, u32[]{:S(2)}) copy-start(f32[64,2048]{1,0:T(8,128)} %own.1) | copy-start | bytes 1572868
  13.8 1.9 %collective-permute-start.2 = (f32[512,128]{1,0:T(8,128)S(1)}, f32[512,128]{1,0:T(8,128)S(1)}, u32[]{:S(2)}, u32[]{:S(2)}) collective-permute-start(f32[512,128]{1,0:T(8,128)S(1)} %select_bitcast_fusion), channel_id=1, source_target_pairs={{0,2},{2,0},{1,3},{3,1},{4,6},{6,4},{5,7},{7,5},{8,10},{10,8},{9,1... | collective-permute-start | bytes 786440 | tf_op jit(solution)/shard_map/ppermute | solution.py:18
  13.9 10.2 %collective-permute-start.1 = (f32[256,256]{1,0:T(8,128)S(1)}, f32[256,256]{1,0:T(8,128)S(1)}, u32[]{:S(2)}, u32[]{:S(2)}) collective-permute-start(f32[256,256]{1,0:T(8,128)S(1)} %get-tuple-element.42), channel_id=1, source_target_pairs={{0,1},{1,0},{2,3},{3,2},{4,5},{5,4},{6,7},{7,6},{8,9},{9,8},{10,11... | collective-permute-start | bytes 786440 | tf_op jit(solution)/shard_map/ppermute | solution.py:18
  15.8 8.4 %collective-permute-start.3 = (f32[512,128]{1,0:T(8,128)S(1)}, f32[512,128]{1,0:T(8,128)S(1)}, u32[]{:S(2)}, u32[]{:S(2)}) collective-permute-start(f32[512,128]{1,0:T(8,128)S(1)} %bitcast_add_fusion), channel_id=1, source_target_pairs={{0,4},{4,0},{1,5},{5,1},{2,6},{6,2},{3,7},{7,3},{8,12},{12,8},{9,1... | collective-permute-start | bytes 786440 | tf_op jit(solution)/shard_map/ppermute | solution.py:18
  24.2 5.8 %collective-permute-start.4 = (f32[128,256]{1,0:T(8,128)S(1)}, f32[128,256]{1,0:T(8,128)S(1)}, u32[]{:S(2)}, u32[]{:S(2)}) collective-permute-start(f32[128,256]{1,0:T(8,128)S(1)} %get-tuple-element.38), channel_id=1, source_target_pairs={{0,1},{1,0},{2,3},{3,2},{4,5},{5,4},{6,7},{7,6},{8,9},{9,8},{10,11... | collective-permute-start | bytes 393224 | tf_op jit(solution)/shard_map/ppermute | solution.py:18
  25.7 4.5 %copy-start.3 = (f32[1,4,2,256,256]{4,3,2,1,0:T(8,128)S(1)}, f32[1,4,2,256,256]{4,3,2,1,0:T(8,128)}, u32[]{:S(2)}) copy-start(f32[1,4,2,256,256]{4,3,2,1,0:T(8,128)} %coup_hbm.1) | copy-start | bytes 6291460
  30.1 1.3 %collective-permute-start.5 = (f32[64,256]{1,0:T(8,128)S(1)}, f32[64,256]{1,0:T(8,128)S(1)}, u32[]{:S(2)}, u32[]{:S(2)}) collective-permute-start(f32[64,256]{1,0:T(8,128)S(1)} %slice.110), channel_id=1, source_target_pairs={{0,2},{2,0},{1,3},{3,1},{4,6},{6,4},{5,7},{7,5},{8,10},{10,8},{9,1... | collective-permute-start | bytes 196616 | tf_op jit(solution)/shard_map/ppermute | solution.py:18
  31.8 1.3 %collective-permute-start.6 = (f32[64,256]{1,0:T(8,128)S(1)}, f32[64,256]{1,0:T(8,128)S(1)}, u32[]{:S(2)}, u32[]{:S(2)}) collective-permute-start(f32[64,256]{1,0:T(8,128)S(1)} %slice_subtract_fusion), channel_id=1, source_target_pairs={{0,2},{2,0},{1,3},{3,1},{4,6},{6,4},{5,7},{7,5},{8,10},{10,8},{9,1... | collective-permute-start | bytes 196616 | tf_op jit(solution)/shard_map/ppermute | solution.py:18
  32.1 27.3 %slice-start = ((s8[8388608]{0:T(1024)(128)(4,1)}), s8[4194304]{0:T(1024)(128)(4,1)S(1)}, s32[]{:S(2)}) async-start(s8[8388608]{0:T(1024)(128)(4,1)} %bitcast.50), calls=%async_computation | async-start | bytes 8388608
  33.2 4.5 %collective-permute-start.7 = (f32[64,256]{1,0:T(8,128)S(1)}, f32[64,256]{1,0:T(8,128)S(1)}, u32[]{:S(2)}, u32[]{:S(2)}) collective-permute-start(f32[64,256]{1,0:T(8,128)S(1)} %add.58), channel_id=1, source_target_pairs={{0,4},{4,0},{1,5},{5,1},{2,6},{6,2},{3,7},{7,3},{8,12},{12,8},{9,1... | collective-permute-start | bytes 196616 | tf_op jit(solution)/shard_map/ppermute | solution.py:18
  34.3 9.4 %collective-permute-start.10 = (f32[512,128]{1,0:T(8,128)S(1)}, f32[512,128]{1,0:T(8,128)S(1)}, u32[]{:S(2)}, u32[]{:S(2)}) collective-permute-start(f32[512,128]{1,0:T(8,128)S(1)} %add.59), channel_id=1, source_target_pairs={{0,12},{4,8},{8,4},{12,0},{1,13},{5,9},{9,5},{13,1},{2,14},{6,10},... | collective-permute-start | bytes 786440 | tf_op jit(solution)/shard_map/ppermute | solution.py:18
  37.7 10.3 %slice-start.2 = ((f32[4,256,2048]{2,1,0:T(8,128)}), f32[2,256,2048]{2,1,0:T(8,128)S(1)}, s32[]{:S(2)}) async-start(f32[4,256,2048]{2,1,0:T(8,128)} %corr_hbm.1), calls=%async_computation.2 | async-start | bytes 8388608 | tf_op jit(solution)/shard_map/slice | solution.py:276
  38.6 20.8 %slice-start.1 = ((s8[8388608]{0:T(1024)(128)(4,1)}), s8[4194304]{0:T(1024)(128)(4,1)S(1)}, s32[]{:S(2)}) async-start(s8[8388608]{0:T(1024)(128)(4,1)} %bitcast.50), calls=%async_computation.1 | async-start | bytes 8388608
  38.6 4.3 %collective-permute-start.8 = (f32[64,256]{1,0:T(8,128)S(1)}, f32[64,256]{1,0:T(8,128)S(1)}, u32[]{:S(2)}, u32[]{:S(2)}) collective-permute-start(f32[64,256]{1,0:T(8,128)S(1)} %fusion.4), channel_id=1, source_target_pairs={{0,1},{1,0},{2,3},{3,2},{4,5},{5,4},{6,7},{7,6},{8,9},{9,8},{10,11... | collective-permute-start | bytes 196616 | tf_op jit(solution)/shard_map/ppermute | solution.py:18
  43.0 1.4 %collective-permute-start.9 = (f32[128,256]{1,0:T(8,128)S(1)}, f32[128,256]{1,0:T(8,128)S(1)}, u32[]{:S(2)}, u32[]{:S(2)}) collective-permute-start(f32[128,256]{1,0:T(8,128)S(1)} %pad_maximum_fusion.2), channel_id=1, source_target_pairs={{0,2},{2,0},{1,3},{3,1},{4,6},{6,4},{5,7},{7,5},{8,10},{10,8},{9,1... | collective-permute-start | bytes 393224 | tf_op jit(solution)/shard_map/ppermute | solution.py:18
  44.4 7.2 %collective-permute-start.13 = (f32[128,256]{1,0:T(8,128)S(1)}, f32[128,256]{1,0:T(8,128)S(1)}, u32[]{:S(2)}, u32[]{:S(2)}) collective-permute-start(f32[128,256]{1,0:T(8,128)S(1)} %fusion.50), channel_id=1, source_target_pairs={{0,8},{4,12},{8,0},{12,4},{1,9},{5,13},{9,1},{13,5},{2,10},{6,14},... | collective-permute-start | bytes 393224 | tf_op jit(solution)/shard_map/ppermute | solution.py:18
  47.3 7.1 %collective-permute-start.12 = (f32[128,256]{1,0:T(8,128)S(1)}, f32[128,256]{1,0:T(8,128)S(1)}, u32[]{:S(2)}, u32[]{:S(2)}) collective-permute-start(f32[128,256]{1,0:T(8,128)S(1)} %fusion.50), channel_id=1, source_target_pairs={{0,12},{4,8},{8,4},{12,0},{1,13},{5,9},{9,5},{13,1},{2,14},{6,10},... | collective-permute-start | bytes 393224 | tf_op jit(solution)/shard_map/ppermute | solution.py:18
  47.8 6.8 %collective-permute-start.11 = (f32[128,256]{1,0:T(8,128)S(1)}, f32[128,256]{1,0:T(8,128)S(1)}, u32[]{:S(2)}, u32[]{:S(2)}) collective-permute-start(f32[128,256]{1,0:T(8,128)S(1)} %fusion.50), channel_id=1, source_target_pairs={{0,4},{4,0},{8,12},{12,8},{1,5},{5,1},{9,13},{13,9},{2,6},{6,2},{1... | collective-permute-start | bytes 393224 | tf_op jit(solution)/shard_map/ppermute | solution.py:18
  48.0 6.9 %collective-permute-start.14 = (f32[512,128]{1,0:T(8,128)S(1)}, f32[512,128]{1,0:T(8,128)S(1)}, u32[]{:S(2)}, u32[]{:S(2)}) collective-permute-start(f32[512,128]{1,0:T(8,128)S(1)} %maximum_add_fusion), channel_id=1, source_target_pairs={{0,2},{2,0},{1,3},{3,1},{4,6},{6,4},{5,7},{7,5},{8,10},{10,8},{9,1... | collective-permute-start | bytes 786440 | tf_op jit(solution)/shard_map/ppermute | solution.py:18
  55.4 5.8 %collective-permute-start.17 = (f32[64,256]{1,0:T(8,128)S(1)}, f32[64,256]{1,0:T(8,128)S(1)}, u32[]{:S(2)}, u32[]{:S(2)}) collective-permute-start(f32[64,256]{1,0:T(8,128)S(1)} %fusion.36), channel_id=1, source_target_pairs={{0,16},{1,17},{2,18},{3,19},{4,20},{5,21},{6,22},{7,23},{8,24},{9,... | collective-permute-start | bytes 196616 | tf_op jit(solution)/shard_map/ppermute | solution.py:18
  58.5 5.5 %collective-permute-start.16 = (f32[64,256]{1,0:T(8,128)S(1)}, f32[64,256]{1,0:T(8,128)S(1)}, u32[]{:S(2)}, u32[]{:S(2)}) collective-permute-start(f32[64,256]{1,0:T(8,128)S(1)} %fusion.36), channel_id=1, source_target_pairs={{0,17},{1,16},{2,19},{3,18},{4,21},{5,20},{6,23},{7,22},{8,25},{9,... | collective-permute-start | bytes 196616 | tf_op jit(solution)/shard_map/ppermute | solution.py:18
  60.2 4.3 %collective-permute-start.15 = (f32[64,256]{1,0:T(8,128)S(1)}, f32[64,256]{1,0:T(8,128)S(1)}, u32[]{:S(2)}, u32[]{:S(2)}) collective-permute-start(f32[64,256]{1,0:T(8,128)S(1)} %fusion.36), channel_id=1, source_target_pairs={{0,1},{1,0},{2,3},{3,2},{4,5},{5,4},{6,7},{7,6},{8,9},{9,8},{10,11... | collective-permute-start | bytes 196616 | tf_op jit(solution)/shard_map/ppermute | solution.py:18

commit v6 on v5

--- a/solution.py
+++ b/solution.py
@@ -68,8 +68,9 @@
     wanted[found] = wanted[found - 1]
 
     def fetch(base, slot):
-        for u in range(size):
-            gathered[slot, pl.ds(u, 1), :] = source[pl.ds(order[base + u], 1), :]
+        for u in range(0, size, 8):
+            gathered[slot, u:u + 8, :] = jnp.concatenate(
+                [source[pl.ds(order[base + u + v], 1), :] for v in range(8)], axis=0)
 
     fetch(wanted[0] * size, 0)
     def gather(n, _):
@@ -93,7 +94,7 @@
         out = both[:rows] + both[rows:] + mm(left[:rows], low)
         current[:, pl.ds(pl.multiple_of(t * size, size), size)] = out
         return 0
-    lax.fori_loop(0, out_tiles, near, 0, unroll=8)
+    lax.fori_loop(0, out_tiles, near, 0, unroll=True)
     load_proj.wait()
     left = stacked(current[...])
     for level in range(2):
@@ -222,6 +223,114 @@
     )(*(pltpu.with_memory_space_constraint(v, pltpu.HBM) for v in (corr, proj, coup)))
 
 
+def apply(value, matrix):
+    rows = value.shape[0]
+    left = stacked(value)
+    high, low = parts(matrix)
+    both = mm(left, high)
+    return both[:rows] + both[rows:] + mm(left[:rows], low)
+
+
+def level_coefficients(height, own, sib, coupling):
+    rank = own.shape[1]
+    pair = jnp.concatenate([own, sib], axis=1)
+    return apply(pair, coupling[0, height].reshape(2 * rank, rank))
+
+
+def first_kernel(own, sib, total, coupling, gram, coeff, after):
+    value = level_coefficients(0, own[...], sib[...], coupling)
+    coeff[...] = value
+    after[...] = total[...] - apply(value, gram[...])
+
+
+def second_kernel(own, sib, part2, part3, coupling, gram2, gram3, coeff, after2, after3):
+    rank = own.shape[1]
+    value = level_coefficients(1, own[...], sib[...], coupling)
+    coeff[...] = value
+    after2[...] = part2[...] - apply(value, gram2[...])
+    after3[...] = part3[...] - apply(value, gram3[rank:2 * rank, :])
+
+
+def third_kernel(both, near, far, across, fold, coupling, coeff, after):
+    rows, rank = coeff.shape
+    mine = both[...] + near[...]
+    others = far[...] + across[...]
+    own, sib = mine[:rows], others[:rows]
+    coeff[...] = level_coefficients(2, own, sib, coupling)
+    after[...] = (mine[rows:] + others[rows:]) - apply(
+        jnp.concatenate([own, sib], axis=1), fold[...])
+
+
+def middle_kernel(current, coeff, corr_hbm, after, last_high, last_low, corr, sems):
+    loads = [pltpu.make_async_copy(corr_hbm.at[level + 2], corr.at[level], sems.at[level])
+             for level in range(2)]
+    for load in loads:
+        load.start()
+    loads[0].wait()
+    after[...] = current[...] - apply(coeff[...], corr[0])
+    loads[1].wait()
+    last_high[...], last_low[...] = parts(corr[1])
+
+
+def final_kernel(part, near, far, across, coupling, current, last_high, last_low, out_hbm, out, sems):
+    rows, points = current.shape
+    coeff = level_coefficients(3, part[...] + near[...], far[...] + across[...], coupling)
+    left = stacked(coeff)
+    step = points // 4
+    copies = []
+    for piece in range(4):
+        cols = slice(piece * step, (piece + 1) * step)
+        value = mm(left, last_high[:, cols])
+        out[:, cols] = current[:, cols] - (
+            value[:rows] + value[rows:] + mm(left[:rows], last_low[:, cols]))
+        copies.append(pltpu.make_async_copy(out.at[:, cols], out_hbm.at[:, cols], sems.at[piece]))
+        copies[-1].start()
+    for copy in copies:
+        copy.wait()
+
+
+def small_call(kernel, shapes, *args):
+    vmem = pl.BlockSpec(memory_space=pltpu.VMEM)
+    return pl.pallas_call(
+        kernel,
+        out_shape=[jax.ShapeDtypeStruct(shape, jnp.float32) for shape in shapes],
+        in_specs=[vmem] * len(args),
+        out_specs=[vmem] * len(shapes),
+        compiler_params=pltpu.CompilerParams(vmem_limit_bytes=8 << 20),
+        cost_estimate=pl.CostEstimate(flops=100_000_000, bytes_accessed=1 << 20, transcendentals=0),
+    )(*args)
+
+
+def middle_call(current, coeff, corr):
+    rank, points = corr.shape[1:]
+    vmem = pl.BlockSpec(memory_space=pltpu.VMEM)
+    half = jax.ShapeDtypeStruct((rank, points), jnp.bfloat16)
+    return pl.pallas_call(
+        middle_kernel,
+        out_shape=[jax.ShapeDtypeStruct(current.shape, jnp.float32), half, half],
+        in_specs=[vmem, vmem, pl.BlockSpec(memory_space=pltpu.HBM)],
+        out_specs=[vmem] * 3,
+        scratch_shapes=[pltpu.VMEM((2, rank, points), jnp.float32), pltpu.SemaphoreType.DMA((2,))],
+        compiler_params=pltpu.CompilerParams(vmem_limit_bytes=20 << 20),
+        cost_estimate=pl.CostEstimate(flops=400_000_000, bytes_accessed=4 << 20, transcendentals=0),
+        name="middle",
+    )(current, coeff, pltpu.with_memory_space_constraint(corr, pltpu.HBM))
+
+
+def final_call(part, near, far, across, coupling, current, last_high, last_low):
+    vmem = pl.BlockSpec(memory_space=pltpu.VMEM)
+    return pl.pallas_call(
+        final_kernel,
+        out_shape=jax.ShapeDtypeStruct(current.shape, jnp.float32),
+        in_specs=[vmem] * 8,
+        out_specs=pl.BlockSpec(memory_space=pltpu.HBM),
+        scratch_shapes=[pltpu.VMEM(current.shape, jnp.float32), pltpu.SemaphoreType.DMA((4,))],
+        compiler_params=pltpu.CompilerParams(vmem_limit_bytes=12 << 20),
+        cost_estimate=pl.CostEstimate(flops=400_000_000, bytes_accessed=4 << 20, transcendentals=0),
+        name="final",
+    )(part, near, far, across, coupling, current, last_high, last_low)
+
+
 def local(
     charges, cluster_order, near_tiles, near_index, near_count, proj_basis, corr_basis, coupling
 ):
@@ -252,20 +361,17 @@
     own, later = tie((own, later))
     part2, part3 = later[:rows], later[rows:]
 
-    def coefficients(height, own, sib):
-        return dot(own, coupling[0, height, 0]) + dot(sib, coupling[0, height, 1])
-
-    coeff0 = coefficients(0, own, swap(own, ("core",), 1))
-    own = sum1 - dot(coeff0, early)
+    small = own.shape
+    coeff0, own = small_call(
+        first_kernel, [small] * 2, own, swap(own, ("core",), 1), sum1, coupling, early)
     own = own + swap(own, ("core",), 1)
     own, fold = tie((own, fold))
     fold = fold + swapped(swap(fold, ("x1", "x0"), 3))
     part2 = part2 - dot(coeff0, second)
     part3 = part3 - dot(coeff0, late[:rank])
-    coeff1 = coefficients(1, own, swap(own, ("x0",), 1))
-    own = part2 - dot(coeff1, mid)
+    coeff1, own, part3 = small_call(
+        second_kernel, [small] * 3, own, swap(own, ("x0",), 1), part2, part3, coupling, mid, late)
     own = own + over_rhs(own)
-    part3 = part3 - dot(coeff1, late[rank:2 * rank])
     both = jnp.concatenate([own, part3], axis=0)
     both = both + swap(both, ("core",), 1)
     both, fold, coeff0, coeff1 = tie((both, fold, coeff0, coeff1))
@@ -275,15 +381,10 @@
     current = current - dot(
         jnp.concatenate([coeff0, coeff1], axis=1), corr_basis[:2].reshape(2 * rank, -1))
     near, far, across = (swap(both, ("x1", "x0"), mask) for mask in (1, 3, 2))
-    near = both + near
-    far = far + across
-    own, sib = near[:rows], far[:rows]
-    coeff2 = coefficients(2, own, sib)
-    own = (near[rows:] + far[rows:]) - (dot(own, fold[:rank]) + dot(sib, fold[rank:]))
+    coeff2, own = small_call(third_kernel, [small] * 2, both, near, far, across, fold, coupling)
     near, far, across = (swap(own, RING, mask) for mask in (1, 17, 16))
-    current = current - dot(coeff2, corr_basis[2])
-    coeff3 = coefficients(3, own + near, far + across)
-    return current - dot(coeff3, corr_basis[3])
+    current, last_high, last_low = middle_call(current, coeff2, corr_basis)
+    return final_call(own, near, far, across, coupling, current, last_high, last_low)
 
 
 def solution(mesh):

time: 66.5 us -> 65 us (0.977)
  Pallas kernels: 20.2 us -> 26 us
  matrix products: 7.12 us -> 1.91 us
  waiting for transfers between devices: 18.6 us -> 16 us
    pallas_call x0 -> x5, Pallas kernels: none -> 5.24 us  [the longest x1 2.54 us: middle_call(): pl.pallas_call(middle_kernel, out_shape=[jax.ShapeDtypeStruct(current.sha...]
    dot_general x18 -> x3, matrix products: 7.12 us -> 1.91 us  [dot(): return jnp.dot(a, b, precision=FAST, preferred_element_type=jnp.float32)]
    ppermute x18, waiting for transfers between devices: 18.6 us -> 16 us  [swap(): return lax.ppermute(block, axes, [(i, i ^ mask) for i in range(count)])]
  transfers between devices with their start and end apart: 18 -> 18, of which waited for: 14 -> 11; matrix products, arithmetic and copies ran while one was open for 7% -> 3% of each run, Pallas kernels for 31% -> 37%
where the time goes in v6:
time: 65 us; the launch traced here: 64.6 us
  Pallas kernels  26 us (40%)
  starting transfers between devices  19.9 us (31%)
  waiting for transfers between devices  16 us (25%)
  matrix products  1.91 us (3%)
    ppermute x18, starting transfers between devices, swap(): return lax.ppermute(block, axes, [(i, i ^ mask) for i in range(count)])  19.9 us
    ppermute x18, waiting for transfers between devices, swap(): return lax.ppermute(block, axes, [(i, i ^ mask) for i in range(count)])  16 us
    pallas_call x1, Pallas kernels, gram_call(): pl.pallas_call(gram_kernel, out_shape=[jax.ShapeDtypeStruct((above * rank...  10.4 us
    pallas_call x1, Pallas kernels, near_call(): pl.pallas_call(near_kernel, out_shape=(jax.ShapeDtypeStruct((rows, half),...  7.17 us
    pallas_call x1, Pallas kernels, later_call(): pl.pallas_call(later_kernel, out_shape=jax.ShapeDtypeStruct((2 * rows, ra...  3.15 us
    pallas_call x1, Pallas kernels, middle_call(): pl.pallas_call(middle_kernel, out_shape=[jax.ShapeDtypeStruct(current.sha...  2.54 us
    dot_general x3, matrix products, dot(): return jnp.dot(a, b, precision=FAST, preferred_element_type=jnp.float32)  1.91 us
    pallas_call x1, Pallas kernels, final_call(): pl.pallas_call(final_kernel, out_shape=jax.ShapeDtypeStruct(current.shape...  1.44 us
  transfers between devices with their start and end apart: 18, of which 11 were waited for; matrix products, arithmetic and copies ran while one was open for 3% of the time, Pallas kernels for 37%

profile of v6, /device:TPU:0, one launch (start us, length us, event | category | flops | bytes accessed | tf_op | source)
XLA Modules:
  0.0 64.6 jit_solution(6571511071261685834)
XLA Ops:
  0.0 1.7 %collective-permute-start = (f32[64,2048]{1,0:T(8,128)}, f32[64,2048]{1,0:T(8,128)S(1)}, u32[]{:S(2)}, u32[]{:S(2)}) collective-permute-start(f32[64,2048]{1,0:T(8,128)} %own.1), channel_id=1, source_target_pairs={{0,1},{1,0},{2,3},{3,2},{4,5},{5,4},{6,7},{7,6},{8,9},{9,8},{10,11... | collective-permute-start | bytes 1572872 | tf_op jit(solution)/shard_map/ppermute | solution.py:18
  1.7 0.0 copy-start.4
  1.7 0.0 copy-start.1
  1.7 0.0 copy-start.2
  1.7 0.0 copy-start.3
  1.7 10.4 %gram.1 = (f32[256,256]{1,0:T(8,128)S(1)}, f32[256,256]{1,0:T(8,128)S(1)}, f32[256,256]{1,0:T(8,128)S(1)}, f32[768,256]{1,0:T(8,128)S(1)}, f32[2,512,128]{2,1,0:T(8,128)S(1)}) custom-call(f32[4,256,2048]{2,1,0:T(8,128)} %corr_hbm.3, f32[4,2048,256]{2,1,0:T(8,128)} %proj_hbm.5, f32[1,4,2,256,256]{4,3,2,1,0:T(8,128)} %coupling.7), custom_call_target="tpu_custom_call" | custom-call | flops 4831838208 | bytes 12582912 | tf_op jit(solution)/shard_map/gram/pallas_call | solution.py:206
  12.1 1.7 %collective-permute-done.other = f32[64,2048]{1,0:T(8,128)S(1)} collective-permute-done((f32[64,2048]{1,0:T(8,128)}, f32[64,2048]{1,0:T(8,128)S(1)}, u32[]{:S(2)}, u32[]{:S(2)}) %collective-permute-start) | collective-permute-done | bytes 524320 | tf_op jit(solution)/shard_map/ppermute | solution.py:18
  13.8 0.1 collective-permute-start.2
  13.9 1.8 %collective-permute-start.1 = (f32[256,256]{1,0:T(8,128)S(1)}, f32[256,256]{1,0:T(8,128)S(1)}, u32[]{:S(2)}, u32[]{:S(2)}) collective-permute-start(f32[256,256]{1,0:T(8,128)S(1)} %get-tuple-element.50), channel_id=1, source_target_pairs={{0,1},{1,0},{2,3},{3,2},{4,5},{5,4},{6,7},{7,6},{8,9},{9,8},{10,11... | collective-permute-start | bytes 786440 | tf_op jit(solution)/shard_map/ppermute | solution.py:18
  15.7 0.0 collective-permute-done.2
  15.8 1.6 %collective-permute-start.3 = (f32[512,128]{1,0:T(8,128)S(1)}, f32[512,128]{1,0:T(8,128)S(1)}, u32[]{:S(2)}, u32[]{:S(2)}) collective-permute-start(f32[512,128]{1,0:T(8,128)S(1)} %bitcast_add_fusion), channel_id=1, source_target_pairs={{0,4},{4,0},{1,5},{5,1},{2,6},{6,2},{3,7},{7,3},{8,12},{12,8},{9,1... | collective-permute-start | bytes 786440 | tf_op jit(solution)/shard_map/ppermute | solution.py:18
  17.4 0.0 copy-done.4
  17.4 0.1 copy.9.index
  17.5 0.0 copy-done.1
  17.5 0.0 copy-done.2
  17.5 0.0 copy-done.3
  17.5 7.2 %near.1 = (f32[64,2048]{1,0:T(8,128)S(1)}, f32[128,256]{1,0:T(8,128)S(1)}) custom-call(s32[4096]{0:T(1024)S(1)} %copy-done.2, s32[16,4]{1,0:T(8,128)S(1)} %copy.9.index, s32[16]{0:T(128)S(1)} %copy-done.3, s32[1]{0:T(128)} %bitcast.side, f32[64,2048]{1,0:T(8,128)S(1)} %copy-done.1, f32[64,2048]{1,0:T(8,128)S(1)} %collective-permute-done.other, ...), custom_call_target="tpu_custom_call" | custom-call | flops 200000000 | bytes 8388608 | tf_op jit(solution)/shard_map/near/pallas_call | solution.py:113
  24.6 0.0 collective-permute-done.1
  24.6 0.0 collective-permute-done.3
  24.7 1.2 %collective-permute-start.4 = (f32[128,256]{1,0:T(8,128)S(1)}, f32[128,256]{1,0:T(8,128)S(1)}, u32[]{:S(2)}, u32[]{:S(2)}) collective-permute-start(f32[128,256]{1,0:T(8,128)S(1)} %get-tuple-element.47), channel_id=1, source_target_pairs={{0,1},{1,0},{2,3},{3,2},{4,5},{5,4},{6,7},{7,6},{8,9},{9,8},{10,11... | collective-permute-start | bytes 393224 | tf_op jit(solution)/shard_map/ppermute | solution.py:18
  25.8 0.0 copy-start
  25.8 3.1 %later.1 = f32[128,256]{1,0:T(8,128)S(1)} custom-call(f32[64,2048]{1,0:T(8,128)S(1)} %get-tuple-element.48.current, f32[4,2048,256]{2,1,0:T(8,128)} %proj_hbm.5), custom_call_target="tpu_custom_call" | custom-call | flops 402653184 | bytes 4194304 | tf_op jit(solution)/shard_map/later/pallas_call | solution.py:154
  29.0 0.7 %collective-permute-done.4 = f32[128,256]{1,0:T(8,128)S(1)} collective-permute-done((f32[128,256]{1,0:T(8,128)S(1)}, f32[128,256]{1,0:T(8,128)S(1)}, u32[]{:S(2)}, u32[]{:S(2)}) %collective-permute-start.4) | collective-permute-done | bytes 131104 | tf_op jit(solution)/shard_map/ppermute | solution.py:18
  29.7 0.3 collective-permute-start.5
  30.1 1.2 %collective-permute-done.5.sib = f32[64,256]{1,0:T(8,128)S(1)} collective-permute-done((f32[64,256]{1,0:T(8,128)S(1)}, f32[64,256]{1,0:T(8,128)S(1)}, u32[]{:S(2)}, u32[]{:S(2)}) %collective-permute-start.5) | collective-permute-done | bytes 65568 | tf_op jit(solution)/shard_map/ppermute | solution.py:18
  31.3 0.0 copy-done
  31.3 0.4 shard_map.82
  31.7 0.2 collective-permute-start.6
  31.9 0.2 convolution_subtract_fusion.2.part2
  32.1 0.9 %collective-permute-done.6 = f32[64,256]{1,0:T(8,128)S(1)} collective-permute-done((f32[64,256]{1,0:T(8,128)S(1)}, f32[64,256]{1,0:T(8,128)S(1)}, u32[]{:S(2)}, u32[]{:S(2)}) %collective-permute-start.6) | collective-permute-done | bytes 65568 | tf_op jit(solution)/shard_map/ppermute | solution.py:18
  33.0 1.1 %collective-permute-start.7 = (f32[64,256]{1,0:T(8,128)S(1)}, f32[64,256]{1,0:T(8,128)S(1)}, u32[]{:S(2)}, u32[]{:S(2)}) collective-permute-start(f32[64,256]{1,0:T(8,128)S(1)} %add.27.own), channel_id=1, source_target_pairs={{0,4},{4,0},{1,5},{5,1},{2,6},{6,2},{3,7},{7,3},{8,12},{12,8},{9,1... | collective-permute-start | bytes 196616 | tf_op jit(solution)/shard_map/ppermute | solution.py:18
  34.1 2.4 %collective-permute-start.10 = (f32[512,128]{1,0:T(8,128)S(1)}, f32[512,128]{1,0:T(8,128)S(1)}, u32[]{:S(2)}, u32[]{:S(2)}) collective-permute-start(f32[512,128]{1,0:T(8,128)S(1)} %add.28), channel_id=1, source_target_pairs={{0,12},{4,8},{8,4},{12,0},{1,13},{5,9},{9,5},{13,1},{2,14},{6,10},... | collective-permute-start | bytes 786440 | tf_op jit(solution)/shard_map/ppermute | solution.py:18
  36.5 0.2 convolution_subtract_fusion.1.part3
  36.7 0.7 %collective-permute-done.7.sib = f32[64,256]{1,0:T(8,128)S(1)} collective-permute-done((f32[64,256]{1,0:T(8,128)S(1)}, f32[64,256]{1,0:T(8,128)S(1)}, u32[]{:S(2)}, u32[]{:S(2)}) %collective-permute-start.7) | collective-permute-done | bytes 65568 | tf_op jit(solution)/shard_map/ppermute | solution.py:18
  37.4 0.5 shard_map.83
  37.9 1.5 %collective-permute-start.8 = (f32[64,256]{1,0:T(8,128)S(1)}, f32[64,256]{1,0:T(8,128)S(1)}, u32[]{:S(2)}, u32[]{:S(2)}) collective-permute-start(f32[64,256]{1,0:T(8,128)S(1)} %get-tuple-element.60), channel_id=1, source_target_pairs={{0,1},{1,0},{2,3},{3,2},{4,5},{5,4},{6,7},{7,6},{8,9},{9,8},{10,11... | collective-permute-start | bytes 196616 | tf_op jit(solution)/shard_map/ppermute | solution.py:18
  39.3 2.9 %collective-permute-done.8 = f32[64,256]{1,0:T(8,128)S(1)} collective-permute-done((f32[64,256]{1,0:T(8,128)S(1)}, f32[64,256]{1,0:T(8,128)S(1)}, u32[]{:S(2)}, u32[]{:S(2)}) %collective-permute-start.8) | collective-permute-done | bytes 65568 | tf_op jit(solution)/shard_map/ppermute | solution.py:18
  42.2 0.1 collective-permute-start.9
  42.3 1.0 %collective-permute-done.10 = f32[512,128]{1,0:T(8,128)S(1)} collective-permute-done((f32[512,128]{1,0:T(8,128)S(1)}, f32[512,128]{1,0:T(8,128)S(1)}, u32[]{:S(2)}, u32[]{:S(2)}) %collective-permute-start.10) | collective-permute-done | bytes 262176 | tf_op jit(solution)/shard_map/ppermute | solution.py:18
  43.4 0.2 collective-permute-done.9
  43.7 0.2 collective-permute-start.14
  43.9 0.0 slice-start
  43.9 2.8 %collective-permute-start.13 = (f32[128,256]{1,0:T(8,128)S(1)}, f32[128,256]{1,0:T(8,128)S(1)}, u32[]{:S(2)}, u32[]{:S(2)}) collective-permute-start(f32[128,256]{1,0:T(8,128)S(1)} %fusion.5.both), channel_id=1, source_target_pairs={{0,8},{4,12},{8,0},{12,4},{1,9},{5,13},{9,1},{13,5},{2,10},{6,14},... | collective-permute-start | bytes 393224 | tf_op jit(solution)/shard_map/ppermute | solution.py:18
  46.7 0.9 %collective-permute-start.12 = (f32[128,256]{1,0:T(8,128)S(1)}, f32[128,256]{1,0:T(8,128)S(1)}, u32[]{:S(2)}, u32[]{:S(2)}) collective-permute-start(f32[128,256]{1,0:T(8,128)S(1)} %fusion.5.both), channel_id=1, source_target_pairs={{0,12},{4,8},{8,4},{12,0},{1,13},{5,9},{9,5},{13,1},{2,14},{6,10},... | collective-permute-start | bytes 393224 | tf_op jit(solution)/shard_map/ppermute | solution.py:18
  47.6 0.0 collective-permute-start.11
  47.6 0.0 collective-permute-done.14
  47.7 3.6 %collective-permute-done.13.across = f32[128,256]{1,0:T(8,128)S(1)} collective-permute-done((f32[128,256]{1,0:T(8,128)S(1)}, f32[128,256]{1,0:T(8,128)S(1)}, u32[]{:S(2)}, u32[]{:S(2)}) %collective-permute-start.13) | collective-permute-done | bytes 131104 | tf_op jit(solution)/shard_map/ppermute | solution.py:18
  51.3 2.7 %collective-permute-done.12.far = f32[128,256]{1,0:T(8,128)S(1)} collective-permute-done((f32[128,256]{1,0:T(8,128)S(1)}, f32[128,256]{1,0:T(8,128)S(1)}, u32[]{:S(2)}, u32[]{:S(2)}) %collective-permute-start.12) | collective-permute-done | bytes 131104 | tf_op jit(solution)/shard_map/ppermute | solution.py:18
  54.0 0.0 collective-permute-done.11.near
  54.0 0.4 shard_map.84
  54.4 3.1 %collective-permute-start.17 = (f32[64,256]{1,0:T(8,128)S(1)}, f32[64,256]{1,0:T(8,128)S(1)}, u32[]{:S(2)}, u32[]{:S(2)}) collective-permute-start(f32[64,256]{1,0:T(8,128)S(1)} %get-tuple-element.66.part), channel_id=1, source_target_pairs={{0,16},{1,17},{2,18},{3,19},{4,20},{5,21},{6,22},{7,23},{8,24},{9,... | collective-permute-start | bytes 196616 | tf_op jit(solution)/shard_map/ppermute | solution.py:18
  57.5 1.0 %collective-permute-start.16 = (f32[64,256]{1,0:T(8,128)S(1)}, f32[64,256]{1,0:T(8,128)S(1)}, u32[]{:S(2)}, u32[]{:S(2)}) collective-permute-start(f32[64,256]{1,0:T(8,128)S(1)} %get-tuple-element.66.part), channel_id=1, source_target_pairs={{0,17},{1,16},{2,19},{3,18},{4,21},{5,20},{6,23},{7,22},{8,25},{9,... | collective-permute-start | bytes 196616 | tf_op jit(solution)/shard_map/ppermute | solution.py:18
  58.5 0.0 collective-permute-start.15
  58.5 0.0 slice-done
  58.5 1.5 %convolution_subtract_fusion.current = f32[64,2048]{1,0:T(8,128)S(1)} fusion(f32[64,2048]{1,0:T(8,128)S(1)} %get-tuple-element.48.current, f32[512,2048]{1,0:T(8,128)S(1)} %bitcast.10, f32[64,256]{1,0:T(8,128)S(1)} %get-tuple-element.68, f32[64,256]{1,0:T(8,128)S(1)} %get-tuple-element.67), kind=kOutput, calls=%fused_computation | convolution fusion | flops 402817024 | bytes 5373952 | tf_op jit(solution)/shard_map/dot_general | solution.py:13
  60.0 2.5 %middle.1 = (f32[64,2048]{1,0:T(8,128)S(1)}, bf16[256,2048]{1,0:T(8,128)(2,1)S(1)}, bf16[256,2048]{1,0:T(8,128)(2,1)S(1)}) custom-call(f32[64,2048]{1,0:T(8,128)S(1)} %convolution_subtract_fusion.current, f32[64,256]{1,0:T(8,128)S(1)} %get-tuple-element.69.coeff, f32[4,256,2048]{2,1,0:T(8,128)} %corr_hbm.3), custom_call_target="tpu_custom_call" | custom-call | flops 400000000 | bytes 4194304 | tf_op jit(solution)/shard_map/middle/pallas_call | solution.py:308
  62.6 0.0 collective-permute-done.17.across
  62.6 0.4 collective-permute-done.16.far
  63.0 0.0 collective-permute-done.15.near
  63.0 1.4 %final.1 = f32[64,2048]{1,0:T(8,128)} custom-call(f32[64,256]{1,0:T(8,128)S(1)} %get-tuple-element.66.part, f32[64,256]{1,0:T(8,128)S(1)} %collective-permute-done.15.near, f32[64,256]{1,0:T(8,128)S(1)} %collective-permute-done.16.far, f32[64,256]{1,0:T(8,128)S(1)} %collective-permute-done.17.across, f32[1,4,2,256,256]{4,3,2,1,0:T(8,128)S(1)} %copy-done, ...), custom_call_target="tpu_custom_call" | custom-call | flops 400000000 | bytes 4194304 | tf_op jit(solution)/shard_map/final/pallas_call | solution.py:322
  (14 shorter events, 0.3 us)
Async XLA Ops:
  0.0 13.8 %collective-permute-start = (f32[64,2048]{1,0:T(8,128)}, f32[64,2048]{1,0:T(8,128)S(1)}, u32[]{:S(2)}, u32[]{:S(2)}) collective-permute-start(f32[64,2048]{1,0:T(8,128)} %own.1), channel_id=1, source_target_pairs={{0,1},{1,0},{2,3},{3,2},{4,5},{5,4},{6,7},{7,6},{8,9},{9,8},{10,11... | collective-permute-start | bytes 1572872 | tf_op jit(solution)/shard_map/ppermute | solution.py:18
  1.7 15.7 %copy-start.4 = (s32[16,4]{0,1:T(4,128)S(1)}, s32[16,4]{0,1:T(4,128)}, u32[]{:S(2)}) copy-start(s32[16,4]{0,1:T(4,128)} %param.11) | copy-start | bytes 772
  1.7 15.8 %copy-start.1 = (f32[64,2048]{1,0:T(8,128)S(1)}, f32[64,2048]{1,0:T(8,128)}, u32[]{:S(2)}) copy-start(f32[64,2048]{1,0:T(8,128)} %own.1) | copy-start | bytes 1572868
  1.7 15.8 %copy-start.2 = (s32[4096]{0:T(1024)S(1)}, s32[4096]{0:T(1024)}, u32[]{:S(2)}) copy-start(s32[4096]{0:T(1024)} %order.1) | copy-start | bytes 49156
  1.7 15.8 %copy-start.3 = (s32[16]{0:T(128)S(1)}, s32[16]{0:T(128)}, u32[]{:S(2)}) copy-start(s32[16]{0:T(128)} %count.1) | copy-start | bytes 196
  13.8 1.9 %collective-permute-start.2 = (f32[512,128]{1,0:T(8,128)S(1)}, f32[512,128]{1,0:T(8,128)S(1)}, u32[]{:S(2)}, u32[]{:S(2)}) collective-permute-start(f32[512,128]{1,0:T(8,128)S(1)} %select_bitcast_fusion), channel_id=1, source_target_pairs={{0,2},{2,0},{1,3},{3,1},{4,6},{6,4},{5,7},{7,5},{8,10},{10,8},{9,1... | collective-permute-start | bytes 786440 | tf_op jit(solution)/shard_map/ppermute | solution.py:18
  13.9 10.7 %collective-permute-start.1 = (f32[256,256]{1,0:T(8,128)S(1)}, f32[256,256]{1,0:T(8,128)S(1)}, u32[]{:S(2)}, u32[]{:S(2)}) collective-permute-start(f32[256,256]{1,0:T(8,128)S(1)} %get-tuple-element.50), channel_id=1, source_target_pairs={{0,1},{1,0},{2,3},{3,2},{4,5},{5,4},{6,7},{7,6},{8,9},{9,8},{10,11... | collective-permute-start | bytes 786440 | tf_op jit(solution)/shard_map/ppermute | solution.py:18
  15.8 8.9 %collective-permute-start.3 = (f32[512,128]{1,0:T(8,128)S(1)}, f32[512,128]{1,0:T(8,128)S(1)}, u32[]{:S(2)}, u32[]{:S(2)}) collective-permute-start(f32[512,128]{1,0:T(8,128)S(1)} %bitcast_add_fusion), channel_id=1, source_target_pairs={{0,4},{4,0},{1,5},{5,1},{2,6},{6,2},{3,7},{7,3},{8,12},{12,8},{9,1... | collective-permute-start | bytes 786440 | tf_op jit(solution)/shard_map/ppermute | solution.py:18
  24.7 5.0 %collective-permute-start.4 = (f32[128,256]{1,0:T(8,128)S(1)}, f32[128,256]{1,0:T(8,128)S(1)}, u32[]{:S(2)}, u32[]{:S(2)}) collective-permute-start(f32[128,256]{1,0:T(8,128)S(1)} %get-tuple-element.47), channel_id=1, source_target_pairs={{0,1},{1,0},{2,3},{3,2},{4,5},{5,4},{6,7},{7,6},{8,9},{9,8},{10,11... | collective-permute-start | bytes 393224 | tf_op jit(solution)/shard_map/ppermute | solution.py:18
  25.8 5.4 %copy-start = (f32[1,4,2,256,256]{4,3,2,1,0:T(8,128)S(1)}, f32[1,4,2,256,256]{4,3,2,1,0:T(8,128)}, u32[]{:S(2)}) copy-start(f32[1,4,2,256,256]{4,3,2,1,0:T(8,128)} %coupling.7) | copy-start | bytes 6291460
  29.7 1.5 %collective-permute-start.5 = (f32[64,256]{1,0:T(8,128)S(1)}, f32[64,256]{1,0:T(8,128)S(1)}, u32[]{:S(2)}, u32[]{:S(2)}) collective-permute-start(f32[64,256]{1,0:T(8,128)S(1)} %get-tuple-element.49.own), channel_id=1, source_target_pairs={{0,2},{2,0},{1,3},{3,1},{4,6},{6,4},{5,7},{7,5},{8,10},{10,8},{9,1... | collective-permute-start | bytes 196616 | tf_op jit(solution)/shard_map/ppermute | solution.py:18
  31.7 1.3 %collective-permute-start.6 = (f32[64,256]{1,0:T(8,128)S(1)}, f32[64,256]{1,0:T(8,128)S(1)}, u32[]{:S(2)}, u32[]{:S(2)}) collective-permute-start(f32[64,256]{1,0:T(8,128)S(1)} %get-tuple-element.52), channel_id=1, source_target_pairs={{0,2},{2,0},{1,3},{3,1},{4,6},{6,4},{5,7},{7,5},{8,10},{10,8},{9,1... | collective-permute-start | bytes 196616 | tf_op jit(solution)/shard_map/ppermute | solution.py:18
  33.0 4.3 %collective-permute-start.7 = (f32[64,256]{1,0:T(8,128)S(1)}, f32[64,256]{1,0:T(8,128)S(1)}, u32[]{:S(2)}, u32[]{:S(2)}) collective-permute-start(f32[64,256]{1,0:T(8,128)S(1)} %add.27.own), channel_id=1, source_target_pairs={{0,4},{4,0},{1,5},{5,1},{2,6},{6,2},{3,7},{7,3},{8,12},{12,8},{9,1... | collective-permute-start | bytes 196616 | tf_op jit(solution)/shard_map/ppermute | solution.py:18
  34.1 9.3 %collective-permute-start.10 = (f32[512,128]{1,0:T(8,128)S(1)}, f32[512,128]{1,0:T(8,128)S(1)}, u32[]{:S(2)}, u32[]{:S(2)}) collective-permute-start(f32[512,128]{1,0:T(8,128)S(1)} %add.28), channel_id=1, source_target_pairs={{0,12},{4,8},{8,4},{12,0},{1,13},{5,9},{9,5},{13,1},{2,14},{6,10},... | collective-permute-start | bytes 786440 | tf_op jit(solution)/shard_map/ppermute | solution.py:18
  37.9 4.3 %collective-permute-start.8 = (f32[64,256]{1,0:T(8,128)S(1)}, f32[64,256]{1,0:T(8,128)S(1)}, u32[]{:S(2)}, u32[]{:S(2)}) collective-permute-start(f32[64,256]{1,0:T(8,128)S(1)} %get-tuple-element.60), channel_id=1, source_target_pairs={{0,1},{1,0},{2,3},{3,2},{4,5},{5,4},{6,7},{7,6},{8,9},{9,8},{10,11... | collective-permute-start | bytes 196616 | tf_op jit(solution)/shard_map/ppermute | solution.py:18
  42.2 1.4 %collective-permute-start.9 = (f32[128,256]{1,0:T(8,128)S(1)}, f32[128,256]{1,0:T(8,128)S(1)}, u32[]{:S(2)}, u32[]{:S(2)}) collective-permute-start(f32[128,256]{1,0:T(8,128)S(1)} %pad_maximum_fusion.1), channel_id=1, source_target_pairs={{0,2},{2,0},{1,3},{3,1},{4,6},{6,4},{5,7},{7,5},{8,10},{10,8},{9,1... | collective-permute-start | bytes 393224 | tf_op jit(solution)/shard_map/ppermute | solution.py:18
  43.7 3.9 %collective-permute-start.14 = (f32[512,128]{1,0:T(8,128)S(1)}, f32[512,128]{1,0:T(8,128)S(1)}, u32[]{:S(2)}, u32[]{:S(2)}) collective-permute-start(f32[512,128]{1,0:T(8,128)S(1)} %maximum_add_fusion), channel_id=1, source_target_pairs={{0,2},{2,0},{1,3},{3,1},{4,6},{6,4},{5,7},{7,5},{8,10},{10,8},{9,1... | collective-permute-start | bytes 786440 | tf_op jit(solution)/shard_map/ppermute | solution.py:18
  43.9 14.6 %slice-start = ((f32[4,256,2048]{2,1,0:T(8,128)}), f32[2,256,2048]{2,1,0:T(8,128)S(1)}, s32[]{:S(2)}) async-start(f32[4,256,2048]{2,1,0:T(8,128)} %corr_hbm.3), calls=%async_computation | async-start | bytes 8388608 | tf_op jit(solution)/shard_map/slice | solution.py:382
  43.9 7.3 %collective-permute-start.13 = (f32[128,256]{1,0:T(8,128)S(1)}, f32[128,256]{1,0:T(8,128)S(1)}, u32[]{:S(2)}, u32[]{:S(2)}) collective-permute-start(f32[128,256]{1,0:T(8,128)S(1)} %fusion.5.both), channel_id=1, source_target_pairs={{0,8},{4,12},{8,0},{12,4},{1,9},{5,13},{9,1},{13,5},{2,10},{6,14},... | collective-permute-start | bytes 393224 | tf_op jit(solution)/shard_map/ppermute | solution.py:18
  46.7 7.3 %collective-permute-start.12 = (f32[128,256]{1,0:T(8,128)S(1)}, f32[128,256]{1,0:T(8,128)S(1)}, u32[]{:S(2)}, u32[]{:S(2)}) collective-permute-start(f32[128,256]{1,0:T(8,128)S(1)} %fusion.5.both), channel_id=1, source_target_pairs={{0,12},{4,8},{8,4},{12,0},{1,13},{5,9},{9,5},{13,1},{2,14},{6,10},... | collective-permute-start | bytes 393224 | tf_op jit(solution)/shard_map/ppermute | solution.py:18
  47.6 6.4 %collective-permute-start.11 = (f32[128,256]{1,0:T(8,128)S(1)}, f32[128,256]{1,0:T(8,128)S(1)}, u32[]{:S(2)}, u32[]{:S(2)}) collective-permute-start(f32[128,256]{1,0:T(8,128)S(1)} %fusion.5.both), channel_id=1, source_target_pairs={{0,4},{4,0},{8,12},{12,8},{1,5},{5,1},{9,13},{13,9},{2,6},{6,2},{1... | collective-permute-start | bytes 393224 | tf_op jit(solution)/shard_map/ppermute | solution.py:18
  54.4 8.2 %collective-permute-start.17 = (f32[64,256]{1,0:T(8,128)S(1)}, f32[64,256]{1,0:T(8,128)S(1)}, u32[]{:S(2)}, u32[]{:S(2)}) collective-permute-start(f32[64,256]{1,0:T(8,128)S(1)} %get-tuple-element.66.part), channel_id=1, source_target_pairs={{0,16},{1,17},{2,18},{3,19},{4,20},{5,21},{6,22},{7,23},{8,24},{9,... | collective-permute-start | bytes 196616 | tf_op jit(solution)/shard_map/ppermute | solution.py:18
  57.5 5.5 %collective-permute-start.16 = (f32[64,256]{1,0:T(8,128)S(1)}, f32[64,256]{1,0:T(8,128)S(1)}, u32[]{:S(2)}, u32[]{:S(2)}) collective-permute-start(f32[64,256]{1,0:T(8,128)S(1)} %get-tuple-element.66.part), channel_id=1, source_target_pairs={{0,17},{1,16},{2,19},{3,18},{4,21},{5,20},{6,23},{7,22},{8,25},{9,... | collective-permute-start | bytes 196616 | tf_op jit(solution)/shard_map/ppermute | solution.py:18
  58.5 4.5 %collective-permute-start.15 = (f32[64,256]{1,0:T(8,128)S(1)}, f32[64,256]{1,0:T(8,128)S(1)}, u32[]{:S(2)}, u32[]{:S(2)}) collective-permute-start(f32[64,256]{1,0:T(8,128)S(1)} %get-tuple-element.66.part), channel_id=1, source_target_pairs={{0,1},{1,0},{2,3},{3,2},{4,5},{5,4},{6,7},{7,6},{8,9},{9,8},{10,11... | collective-permute-start | bytes 196616 | tf_op jit(solution)/shard_map/ppermute | solution.py:18

commit v7 on v6

--- a/solution.py
+++ b/solution.py
@@ -276,9 +276,9 @@
     rows, points = current.shape
     coeff = level_coefficients(3, part[...] + near[...], far[...] + across[...], coupling)
     left = stacked(coeff)
-    step = points // 4
+    step = points // 2
     copies = []
-    for piece in range(4):
+    for piece in range(2):
         cols = slice(piece * step, (piece + 1) * step)
         value = mm(left, last_high[:, cols])
         out[:, cols] = current[:, cols] - (
@@ -324,7 +324,7 @@
         out_shape=jax.ShapeDtypeStruct(current.shape, jnp.float32),
         in_specs=[vmem] * 8,
         out_specs=pl.BlockSpec(memory_space=pltpu.HBM),
-        scratch_shapes=[pltpu.VMEM(current.shape, jnp.float32), pltpu.SemaphoreType.DMA((4,))],
+        scratch_shapes=[pltpu.VMEM(current.shape, jnp.float32), pltpu.SemaphoreType.DMA((2,))],
         compiler_params=pltpu.CompilerParams(vmem_limit_bytes=12 << 20),
         cost_estimate=pl.CostEstimate(flops=400_000_000, bytes_accessed=4 << 20, transcendentals=0),
         name="final",

time: 65 us -> 64.9 us (level)
  starting transfers between devices: 19.9 us -> 21.3 us
  waiting for transfers between devices: 16 us -> 14.9 us
    ppermute x18, starting transfers between devices: 19.9 us -> 21.3 us  [swap(): return lax.ppermute(block, axes, [(i, i ^ mask) for i in range(count)])]
    ppermute x18, waiting for transfers between devices: 16 us -> 14.9 us  [swap(): return lax.ppermute(block, axes, [(i, i ^ mask) for i in range(count)])]
  transfers between devices with their start and end apart: 18 -> 18, of which waited for: 11 -> 11; matrix products, arithmetic and copies ran while one was open for 3% -> 3% of each run, Pallas kernels for 37% -> 36%
where the time goes in v7:
time: 64.9 us; the launch traced here: 64.6 us
  Pallas kernels  25.7 us (40%)
  starting transfers between devices  21.3 us (33%)
  waiting for transfers between devices  14.9 us (23%)
  matrix products  1.91 us (3%)
    ppermute x18, starting transfers between devices, swap(): return lax.ppermute(block, axes, [(i, i ^ mask) for i in range(count)])  21.3 us
    ppermute x18, waiting for transfers between devices, swap(): return lax.ppermute(block, axes, [(i, i ^ mask) for i in range(count)])  14.9 us
    pallas_call x1, Pallas kernels, gram_call(): pl.pallas_call(gram_kernel, out_shape=[jax.ShapeDtypeStruct((above * rank...  10.4 us
    pallas_call x1, Pallas kernels, near_call(): pl.pallas_call(near_kernel, out_shape=(jax.ShapeDtypeStruct((rows, half),...  6.94 us
    pallas_call x1, Pallas kernels, later_call(): pl.pallas_call(later_kernel, out_shape=jax.ShapeDtypeStruct((2 * rows, ra...  3.15 us
    pallas_call x1, Pallas kernels, middle_call(): pl.pallas_call(middle_kernel, out_shape=[jax.ShapeDtypeStruct(current.sha...  2.54 us
    dot_general x3, matrix products, dot(): return jnp.dot(a, b, precision=FAST, preferred_element_type=jnp.float32)  1.91 us
    pallas_call x1, Pallas kernels, final_call(): pl.pallas_call(final_kernel, out_shape=jax.ShapeDtypeStruct(current.shape...  1.45 us
  transfers between devices with their start and end apart: 18, of which 11 were waited for; matrix products, arithmetic and copies ran while one was open for 3% of the time, Pallas kernels for 36%

profile of v7, /device:TPU:0, one launch (start us, length us, event | category | flops | bytes accessed | tf_op | source)
XLA Modules:
  0.0 64.6 jit_solution(5792473940573573221)
XLA Ops:
  0.0 1.7 %collective-permute-start = (f32[64,2048]{1,0:T(8,128)}, f32[64,2048]{1,0:T(8,128)S(1)}, u32[]{:S(2)}, u32[]{:S(2)}) collective-permute-start(f32[64,2048]{1,0:T(8,128)} %own.1), channel_id=1, source_target_pairs={{0,1},{1,0},{2,3},{3,2},{4,5},{5,4},{6,7},{7,6},{8,9},{9,8},{10,11... | collective-permute-start | bytes 1572872 | tf_op jit(solution)/shard_map/ppermute | solution.py:18
  1.7 0.0 copy-start.4
  1.7 0.0 copy-start.1
  1.7 0.0 copy-start.2
  1.7 0.0 copy-start.3
  1.7 10.4 %gram.1 = (f32[256,256]{1,0:T(8,128)S(1)}, f32[256,256]{1,0:T(8,128)S(1)}, f32[256,256]{1,0:T(8,128)S(1)}, f32[768,256]{1,0:T(8,128)S(1)}, f32[2,512,128]{2,1,0:T(8,128)S(1)}) custom-call(f32[4,256,2048]{2,1,0:T(8,128)} %corr_hbm.3, f32[4,2048,256]{2,1,0:T(8,128)} %proj_hbm.5, f32[1,4,2,256,256]{4,3,2,1,0:T(8,128)} %coupling.7), custom_call_target="tpu_custom_call" | custom-call | flops 4831838208 | bytes 12582912 | tf_op jit(solution)/shard_map/gram/pallas_call | solution.py:206
  12.1 1.7 %collective-permute-done.other = f32[64,2048]{1,0:T(8,128)S(1)} collective-permute-done((f32[64,2048]{1,0:T(8,128)}, f32[64,2048]{1,0:T(8,128)S(1)}, u32[]{:S(2)}, u32[]{:S(2)}) %collective-permute-start) | collective-permute-done | bytes 524320 | tf_op jit(solution)/shard_map/ppermute | solution.py:18
  13.8 0.1 collective-permute-start.2
  13.9 1.8 %collective-permute-start.1 = (f32[256,256]{1,0:T(8,128)S(1)}, f32[256,256]{1,0:T(8,128)S(1)}, u32[]{:S(2)}, u32[]{:S(2)}) collective-permute-start(f32[256,256]{1,0:T(8,128)S(1)} %get-tuple-element.50), channel_id=1, source_target_pairs={{0,1},{1,0},{2,3},{3,2},{4,5},{5,4},{6,7},{7,6},{8,9},{9,8},{10,11... | collective-permute-start | bytes 786440 | tf_op jit(solution)/shard_map/ppermute | solution.py:18
  15.7 0.0 collective-permute-done.2
  15.8 1.6 %collective-permute-start.3 = (f32[512,128]{1,0:T(8,128)S(1)}, f32[512,128]{1,0:T(8,128)S(1)}, u32[]{:S(2)}, u32[]{:S(2)}) collective-permute-start(f32[512,128]{1,0:T(8,128)S(1)} %bitcast_add_fusion), channel_id=1, source_target_pairs={{0,4},{4,0},{1,5},{5,1},{2,6},{6,2},{3,7},{7,3},{8,12},{12,8},{9,1... | collective-permute-start | bytes 786440 | tf_op jit(solution)/shard_map/ppermute | solution.py:18
  17.4 0.0 copy-done.4
  17.4 0.1 copy.9.index
  17.5 0.0 copy-done.1
  17.5 0.0 copy-done.2
  17.5 0.0 copy-done.3
  17.5 6.9 %near.1 = (f32[64,2048]{1,0:T(8,128)S(1)}, f32[128,256]{1,0:T(8,128)S(1)}) custom-call(s32[4096]{0:T(1024)S(1)} %copy-done.2, s32[16,4]{1,0:T(8,128)S(1)} %copy.9.index, s32[16]{0:T(128)S(1)} %copy-done.3, s32[1]{0:T(128)} %bitcast.side, f32[64,2048]{1,0:T(8,128)S(1)} %copy-done.1, f32[64,2048]{1,0:T(8,128)S(1)} %collective-permute-done.other, ...), custom_call_target="tpu_custom_call" | custom-call | flops 200000000 | bytes 8388608 | tf_op jit(solution)/shard_map/near/pallas_call | solution.py:113
  24.4 0.0 collective-permute-done.1
  24.4 0.0 collective-permute-done.3
  24.4 1.9 %collective-permute-start.4 = (f32[128,256]{1,0:T(8,128)S(1)}, f32[128,256]{1,0:T(8,128)S(1)}, u32[]{:S(2)}, u32[]{:S(2)}) collective-permute-start(f32[128,256]{1,0:T(8,128)S(1)} %get-tuple-element.47), channel_id=1, source_target_pairs={{0,1},{1,0},{2,3},{3,2},{4,5},{5,4},{6,7},{7,6},{8,9},{9,8},{10,11... | collective-permute-start | bytes 393224 | tf_op jit(solution)/shard_map/ppermute | solution.py:18
  26.3 0.0 copy-start
  26.3 3.2 %later.1 = f32[128,256]{1,0:T(8,128)S(1)} custom-call(f32[64,2048]{1,0:T(8,128)S(1)} %get-tuple-element.48.current, f32[4,2048,256]{2,1,0:T(8,128)} %proj_hbm.5), custom_call_target="tpu_custom_call" | custom-call | flops 402653184 | bytes 4194304 | tf_op jit(solution)/shard_map/later/pallas_call | solution.py:154
  29.4 0.1 collective-permute-done.4
  29.6 0.3 collective-permute-start.5
  29.9 1.2 %collective-permute-done.5.sib = f32[64,256]{1,0:T(8,128)S(1)} collective-permute-done((f32[64,256]{1,0:T(8,128)S(1)}, f32[64,256]{1,0:T(8,128)S(1)}, u32[]{:S(2)}, u32[]{:S(2)}) %collective-permute-start.5) | collective-permute-done | bytes 65568 | tf_op jit(solution)/shard_map/ppermute | solution.py:18
  31.1 0.0 copy-done
  31.1 0.4 shard_map.82
  31.5 0.2 collective-permute-start.6
  31.8 0.2 convolution_subtract_fusion.2.part2
  32.0 0.9 %collective-permute-done.6 = f32[64,256]{1,0:T(8,128)S(1)} collective-permute-done((f32[64,256]{1,0:T(8,128)S(1)}, f32[64,256]{1,0:T(8,128)S(1)}, u32[]{:S(2)}, u32[]{:S(2)}) %collective-permute-start.6) | collective-permute-done | bytes 65568 | tf_op jit(solution)/shard_map/ppermute | solution.py:18
  32.9 1.2 %collective-permute-start.7 = (f32[64,256]{1,0:T(8,128)S(1)}, f32[64,256]{1,0:T(8,128)S(1)}, u32[]{:S(2)}, u32[]{:S(2)}) collective-permute-start(f32[64,256]{1,0:T(8,128)S(1)} %add.27.own), channel_id=1, source_target_pairs={{0,4},{4,0},{1,5},{5,1},{2,6},{6,2},{3,7},{7,3},{8,12},{12,8},{9,1... | collective-permute-start | bytes 196616 | tf_op jit(solution)/shard_map/ppermute | solution.py:18
  34.1 2.2 %collective-permute-start.10 = (f32[512,128]{1,0:T(8,128)S(1)}, f32[512,128]{1,0:T(8,128)S(1)}, u32[]{:S(2)}, u32[]{:S(2)}) collective-permute-start(f32[512,128]{1,0:T(8,128)S(1)} %add.28), channel_id=1, source_target_pairs={{0,12},{4,8},{8,4},{12,0},{1,13},{5,9},{9,5},{13,1},{2,14},{6,10},... | collective-permute-start | bytes 786440 | tf_op jit(solution)/shard_map/ppermute | solution.py:18
  36.3 0.2 convolution_subtract_fusion.1.part3
  36.5 0.7 %collective-permute-done.7.sib = f32[64,256]{1,0:T(8,128)S(1)} collective-permute-done((f32[64,256]{1,0:T(8,128)S(1)}, f32[64,256]{1,0:T(8,128)S(1)}, u32[]{:S(2)}, u32[]{:S(2)}) %collective-permute-start.7) | collective-permute-done | bytes 65568 | tf_op jit(solution)/shard_map/ppermute | solution.py:18
  37.2 0.5 shard_map.83
  37.7 1.8 %collective-permute-start.8 = (f32[64,256]{1,0:T(8,128)S(1)}, f32[64,256]{1,0:T(8,128)S(1)}, u32[]{:S(2)}, u32[]{:S(2)}) collective-permute-start(f32[64,256]{1,0:T(8,128)S(1)} %get-tuple-element.60), channel_id=1, source_target_pairs={{0,1},{1,0},{2,3},{3,2},{4,5},{5,4},{6,7},{7,6},{8,9},{9,8},{10,11... | collective-permute-start | bytes 196616 | tf_op jit(solution)/shard_map/ppermute | solution.py:18
  39.5 2.6 %collective-permute-done.8 = f32[64,256]{1,0:T(8,128)S(1)} collective-permute-done((f32[64,256]{1,0:T(8,128)S(1)}, f32[64,256]{1,0:T(8,128)S(1)}, u32[]{:S(2)}, u32[]{:S(2)}) %collective-permute-start.8) | collective-permute-done | bytes 65568 | tf_op jit(solution)/shard_map/ppermute | solution.py:18
  42.1 0.1 collective-permute-start.9
  42.2 1.2 %collective-permute-done.10 = f32[512,128]{1,0:T(8,128)S(1)} collective-permute-done((f32[512,128]{1,0:T(8,128)S(1)}, f32[512,128]{1,0:T(8,128)S(1)}, u32[]{:S(2)}, u32[]{:S(2)}) %collective-permute-start.10) | collective-permute-done | bytes 262176 | tf_op jit(solution)/shard_map/ppermute | solution.py:18
  43.4 0.1 collective-permute-done.9
  43.5 0.2 collective-permute-start.14
  43.8 0.0 slice-start
  43.8 2.8 %collective-permute-start.13 = (f32[128,256]{1,0:T(8,128)S(1)}, f32[128,256]{1,0:T(8,128)S(1)}, u32[]{:S(2)}, u32[]{:S(2)}) collective-permute-start(f32[128,256]{1,0:T(8,128)S(1)} %fusion.5.both), channel_id=1, source_target_pairs={{0,8},{4,12},{8,0},{12,4},{1,9},{5,13},{9,1},{13,5},{2,10},{6,14},... | collective-permute-start | bytes 393224 | tf_op jit(solution)/shard_map/ppermute | solution.py:18
  46.6 1.0 %collective-permute-start.12 = (f32[128,256]{1,0:T(8,128)S(1)}, f32[128,256]{1,0:T(8,128)S(1)}, u32[]{:S(2)}, u32[]{:S(2)}) collective-permute-start(f32[128,256]{1,0:T(8,128)S(1)} %fusion.5.both), channel_id=1, source_target_pairs={{0,12},{4,8},{8,4},{12,0},{1,13},{5,9},{9,5},{13,1},{2,14},{6,10},... | collective-permute-start | bytes 393224 | tf_op jit(solution)/shard_map/ppermute | solution.py:18
  47.6 0.0 collective-permute-start.11
  47.6 0.0 collective-permute-done.14
  47.7 3.4 %collective-permute-done.13.across = f32[128,256]{1,0:T(8,128)S(1)} collective-permute-done((f32[128,256]{1,0:T(8,128)S(1)}, f32[128,256]{1,0:T(8,128)S(1)}, u32[]{:S(2)}, u32[]{:S(2)}) %collective-permute-start.13) | collective-permute-done | bytes 131104 | tf_op jit(solution)/shard_map/ppermute | solution.py:18
  51.1 2.7 %collective-permute-done.12.far = f32[128,256]{1,0:T(8,128)S(1)} collective-permute-done((f32[128,256]{1,0:T(8,128)S(1)}, f32[128,256]{1,0:T(8,128)S(1)}, u32[]{:S(2)}, u32[]{:S(2)}) %collective-permute-start.12) | collective-permute-done | bytes 131104 | tf_op jit(solution)/shard_map/ppermute | solution.py:18
  53.8 0.0 collective-permute-done.11.near
  53.8 0.4 shard_map.84
  54.2 3.4 %collective-permute-start.17 = (f32[64,256]{1,0:T(8,128)S(1)}, f32[64,256]{1,0:T(8,128)S(1)}, u32[]{:S(2)}, u32[]{:S(2)}) collective-permute-start(f32[64,256]{1,0:T(8,128)S(1)} %get-tuple-element.66.part), channel_id=1, source_target_pairs={{0,16},{1,17},{2,18},{3,19},{4,20},{5,21},{6,22},{7,23},{8,24},{9,... | collective-permute-start | bytes 196616 | tf_op jit(solution)/shard_map/ppermute | solution.py:18
  57.6 1.1 %collective-permute-start.16 = (f32[64,256]{1,0:T(8,128)S(1)}, f32[64,256]{1,0:T(8,128)S(1)}, u32[]{:S(2)}, u32[]{:S(2)}) collective-permute-start(f32[64,256]{1,0:T(8,128)S(1)} %get-tuple-element.66.part), channel_id=1, source_target_pairs={{0,17},{1,16},{2,19},{3,18},{4,21},{5,20},{6,23},{7,22},{8,25},{9,... | collective-permute-start | bytes 196616 | tf_op jit(solution)/shard_map/ppermute | solution.py:18
  58.7 0.0 collective-permute-start.15
  58.7 0.0 slice-done
  58.7 1.5 %convolution_subtract_fusion.current = f32[64,2048]{1,0:T(8,128)S(1)} fusion(f32[64,2048]{1,0:T(8,128)S(1)} %get-tuple-element.48.current, f32[512,2048]{1,0:T(8,128)S(1)} %bitcast.10, f32[64,256]{1,0:T(8,128)S(1)} %get-tuple-element.68, f32[64,256]{1,0:T(8,128)S(1)} %get-tuple-element.67), kind=kOutput, calls=%fused_computation | convolution fusion | flops 402817024 | bytes 5373952 | tf_op jit(solution)/shard_map/dot_general | solution.py:13
  60.2 2.5 %middle.1 = (f32[64,2048]{1,0:T(8,128)S(1)}, bf16[256,2048]{1,0:T(8,128)(2,1)S(1)}, bf16[256,2048]{1,0:T(8,128)(2,1)S(1)}) custom-call(f32[64,2048]{1,0:T(8,128)S(1)} %convolution_subtract_fusion.current, f32[64,256]{1,0:T(8,128)S(1)} %get-tuple-element.69.coeff, f32[4,256,2048]{2,1,0:T(8,128)} %corr_hbm.3), custom_call_target="tpu_custom_call" | custom-call | flops 400000000 | bytes 4194304 | tf_op jit(solution)/shard_map/middle/pallas_call | solution.py:308
  62.7 0.0 collective-permute-done.17.across
  62.7 0.3 collective-permute-done.16.far
  63.0 0.0 collective-permute-done.15.near
  63.0 1.4 %final.1 = f32[64,2048]{1,0:T(8,128)} custom-call(f32[64,256]{1,0:T(8,128)S(1)} %get-tuple-element.66.part, f32[64,256]{1,0:T(8,128)S(1)} %collective-permute-done.15.near, f32[64,256]{1,0:T(8,128)S(1)} %collective-permute-done.16.far, f32[64,256]{1,0:T(8,128)S(1)} %collective-permute-done.17.across, f32[1,4,2,256,256]{4,3,2,1,0:T(8,128)S(1)} %copy-done, ...), custom_call_target="tpu_custom_call" | custom-call | flops 400000000 | bytes 4194304 | tf_op jit(solution)/shard_map/final/pallas_call | solution.py:322
  (14 shorter events, 0.3 us)
Async XLA Ops:
  0.0 13.8 %collective-permute-start = (f32[64,2048]{1,0:T(8,128)}, f32[64,2048]{1,0:T(8,128)S(1)}, u32[]{:S(2)}, u32[]{:S(2)}) collective-permute-start(f32[64,2048]{1,0:T(8,128)} %own.1), channel_id=1, source_target_pairs={{0,1},{1,0},{2,3},{3,2},{4,5},{5,4},{6,7},{7,6},{8,9},{9,8},{10,11... | collective-permute-start | bytes 1572872 | tf_op jit(solution)/shard_map/ppermute | solution.py:18
  1.7 15.7 %copy-start.4 = (s32[16,4]{0,1:T(4,128)S(1)}, s32[16,4]{0,1:T(4,128)}, u32[]{:S(2)}) copy-start(s32[16,4]{0,1:T(4,128)} %param.11) | copy-start | bytes 772
  1.7 15.8 %copy-start.1 = (f32[64,2048]{1,0:T(8,128)S(1)}, f32[64,2048]{1,0:T(8,128)}, u32[]{:S(2)}) copy-start(f32[64,2048]{1,0:T(8,128)} %own.1) | copy-start | bytes 1572868
  1.7 15.8 %copy-start.2 = (s32[4096]{0:T(1024)S(1)}, s32[4096]{0:T(1024)}, u32[]{:S(2)}) copy-start(s32[4096]{0:T(1024)} %order.1) | copy-start | bytes 49156
  1.7 15.8 %copy-start.3 = (s32[16]{0:T(128)S(1)}, s32[16]{0:T(128)}, u32[]{:S(2)}) copy-start(s32[16]{0:T(128)} %count.1) | copy-start | bytes 196
  13.8 1.9 %collective-permute-start.2 = (f32[512,128]{1,0:T(8,128)S(1)}, f32[512,128]{1,0:T(8,128)S(1)}, u32[]{:S(2)}, u32[]{:S(2)}) collective-permute-start(f32[512,128]{1,0:T(8,128)S(1)} %select_bitcast_fusion), channel_id=1, source_target_pairs={{0,2},{2,0},{1,3},{3,1},{4,6},{6,4},{5,7},{7,5},{8,10},{10,8},{9,1... | collective-permute-start | bytes 786440 | tf_op jit(solution)/shard_map/ppermute | solution.py:18
  13.9 10.5 %collective-permute-start.1 = (f32[256,256]{1,0:T(8,128)S(1)}, f32[256,256]{1,0:T(8,128)S(1)}, u32[]{:S(2)}, u32[]{:S(2)}) collective-permute-start(f32[256,256]{1,0:T(8,128)S(1)} %get-tuple-element.50), channel_id=1, source_target_pairs={{0,1},{1,0},{2,3},{3,2},{4,5},{5,4},{6,7},{7,6},{8,9},{9,8},{10,11... | collective-permute-start | bytes 786440 | tf_op jit(solution)/shard_map/ppermute | solution.py:18
  15.8 8.6 %collective-permute-start.3 = (f32[512,128]{1,0:T(8,128)S(1)}, f32[512,128]{1,0:T(8,128)S(1)}, u32[]{:S(2)}, u32[]{:S(2)}) collective-permute-start(f32[512,128]{1,0:T(8,128)S(1)} %bitcast_add_fusion), channel_id=1, source_target_pairs={{0,4},{4,0},{1,5},{5,1},{2,6},{6,2},{3,7},{7,3},{8,12},{12,8},{9,1... | collective-permute-start | bytes 786440 | tf_op jit(solution)/shard_map/ppermute | solution.py:18
  24.4 5.1 %collective-permute-start.4 = (f32[128,256]{1,0:T(8,128)S(1)}, f32[128,256]{1,0:T(8,128)S(1)}, u32[]{:S(2)}, u32[]{:S(2)}) collective-permute-start(f32[128,256]{1,0:T(8,128)S(1)} %get-tuple-element.47), channel_id=1, source_target_pairs={{0,1},{1,0},{2,3},{3,2},{4,5},{5,4},{6,7},{7,6},{8,9},{9,8},{10,11... | collective-permute-start | bytes 393224 | tf_op jit(solution)/shard_map/ppermute | solution.py:18
  26.3 4.8 %copy-start = (f32[1,4,2,256,256]{4,3,2,1,0:T(8,128)S(1)}, f32[1,4,2,256,256]{4,3,2,1,0:T(8,128)}, u32[]{:S(2)}) copy-start(f32[1,4,2,256,256]{4,3,2,1,0:T(8,128)} %coupling.7) | copy-start | bytes 6291460
  29.6 1.5 %collective-permute-start.5 = (f32[64,256]{1,0:T(8,128)S(1)}, f32[64,256]{1,0:T(8,128)S(1)}, u32[]{:S(2)}, u32[]{:S(2)}) collective-permute-start(f32[64,256]{1,0:T(8,128)S(1)} %get-tuple-element.49.own), channel_id=1, source_target_pairs={{0,2},{2,0},{1,3},{3,1},{4,6},{6,4},{5,7},{7,5},{8,10},{10,8},{9,1... | collective-permute-start | bytes 196616 | tf_op jit(solution)/shard_map/ppermute | solution.py:18
  31.5 1.3 %collective-permute-start.6 = (f32[64,256]{1,0:T(8,128)S(1)}, f32[64,256]{1,0:T(8,128)S(1)}, u32[]{:S(2)}, u32[]{:S(2)}) collective-permute-start(f32[64,256]{1,0:T(8,128)S(1)} %get-tuple-element.52), channel_id=1, source_target_pairs={{0,2},{2,0},{1,3},{3,1},{4,6},{6,4},{5,7},{7,5},{8,10},{10,8},{9,1... | collective-permute-start | bytes 196616 | tf_op jit(solution)/shard_map/ppermute | solution.py:18
  32.9 4.3 %collective-permute-start.7 = (f32[64,256]{1,0:T(8,128)S(1)}, f32[64,256]{1,0:T(8,128)S(1)}, u32[]{:S(2)}, u32[]{:S(2)}) collective-permute-start(f32[64,256]{1,0:T(8,128)S(1)} %add.27.own), channel_id=1, source_target_pairs={{0,4},{4,0},{1,5},{5,1},{2,6},{6,2},{3,7},{7,3},{8,12},{12,8},{9,1... | collective-permute-start | bytes 196616 | tf_op jit(solution)/shard_map/ppermute | solution.py:18
  34.1 9.3 %collective-permute-start.10 = (f32[512,128]{1,0:T(8,128)S(1)}, f32[512,128]{1,0:T(8,128)S(1)}, u32[]{:S(2)}, u32[]{:S(2)}) collective-permute-start(f32[512,128]{1,0:T(8,128)S(1)} %add.28), channel_id=1, source_target_pairs={{0,12},{4,8},{8,4},{12,0},{1,13},{5,9},{9,5},{13,1},{2,14},{6,10},... | collective-permute-start | bytes 786440 | tf_op jit(solution)/shard_map/ppermute | solution.py:18
  37.7 4.3 %collective-permute-start.8 = (f32[64,256]{1,0:T(8,128)S(1)}, f32[64,256]{1,0:T(8,128)S(1)}, u32[]{:S(2)}, u32[]{:S(2)}) collective-permute-start(f32[64,256]{1,0:T(8,128)S(1)} %get-tuple-element.60), channel_id=1, source_target_pairs={{0,1},{1,0},{2,3},{3,2},{4,5},{5,4},{6,7},{7,6},{8,9},{9,8},{10,11... | collective-permute-start | bytes 196616 | tf_op jit(solution)/shard_map/ppermute | solution.py:18
  42.1 1.4 %collective-permute-start.9 = (f32[128,256]{1,0:T(8,128)S(1)}, f32[128,256]{1,0:T(8,128)S(1)}, u32[]{:S(2)}, u32[]{:S(2)}) collective-permute-start(f32[128,256]{1,0:T(8,128)S(1)} %pad_maximum_fusion.1), channel_id=1, source_target_pairs={{0,2},{2,0},{1,3},{3,1},{4,6},{6,4},{5,7},{7,5},{8,10},{10,8},{9,1... | collective-permute-start | bytes 393224 | tf_op jit(solution)/shard_map/ppermute | solution.py:18
  43.5 4.1 %collective-permute-start.14 = (f32[512,128]{1,0:T(8,128)S(1)}, f32[512,128]{1,0:T(8,128)S(1)}, u32[]{:S(2)}, u32[]{:S(2)}) collective-permute-start(f32[512,128]{1,0:T(8,128)S(1)} %maximum_add_fusion), channel_id=1, source_target_pairs={{0,2},{2,0},{1,3},{3,1},{4,6},{6,4},{5,7},{7,5},{8,10},{10,8},{9,1... | collective-permute-start | bytes 786440 | tf_op jit(solution)/shard_map/ppermute | solution.py:18
  43.8 14.9 %slice-start = ((f32[4,256,2048]{2,1,0:T(8,128)}), f32[2,256,2048]{2,1,0:T(8,128)S(1)}, s32[]{:S(2)}) async-start(f32[4,256,2048]{2,1,0:T(8,128)} %corr_hbm.3), calls=%async_computation | async-start | bytes 8388608 | tf_op jit(solution)/shard_map/slice | solution.py:382
  43.8 7.3 %collective-permute-start.13 = (f32[128,256]{1,0:T(8,128)S(1)}, f32[128,256]{1,0:T(8,128)S(1)}, u32[]{:S(2)}, u32[]{:S(2)}) collective-permute-start(f32[128,256]{1,0:T(8,128)S(1)} %fusion.5.both), channel_id=1, source_target_pairs={{0,8},{4,12},{8,0},{12,4},{1,9},{5,13},{9,1},{13,5},{2,10},{6,14},... | collective-permute-start | bytes 393224 | tf_op jit(solution)/shard_map/ppermute | solution.py:18
  46.6 7.3 %collective-permute-start.12 = (f32[128,256]{1,0:T(8,128)S(1)}, f32[128,256]{1,0:T(8,128)S(1)}, u32[]{:S(2)}, u32[]{:S(2)}) collective-permute-start(f32[128,256]{1,0:T(8,128)S(1)} %fusion.5.both), channel_id=1, source_target_pairs={{0,12},{4,8},{8,4},{12,0},{1,13},{5,9},{9,5},{13,1},{2,14},{6,10},... | collective-permute-start | bytes 393224 | tf_op jit(solution)/shard_map/ppermute | solution.py:18
  47.6 6.2 %collective-permute-start.11 = (f32[128,256]{1,0:T(8,128)S(1)}, f32[128,256]{1,0:T(8,128)S(1)}, u32[]{:S(2)}, u32[]{:S(2)}) collective-permute-start(f32[128,256]{1,0:T(8,128)S(1)} %fusion.5.both), channel_id=1, source_target_pairs={{0,4},{4,0},{8,12},{12,8},{1,5},{5,1},{9,13},{13,9},{2,6},{6,2},{1... | collective-permute-start | bytes 393224 | tf_op jit(solution)/shard_map/ppermute | solution.py:18
  54.2 8.5 %collective-permute-start.17 = (f32[64,256]{1,0:T(8,128)S(1)}, f32[64,256]{1,0:T(8,128)S(1)}, u32[]{:S(2)}, u32[]{:S(2)}) collective-permute-start(f32[64,256]{1,0:T(8,128)S(1)} %get-tuple-element.66.part), channel_id=1, source_target_pairs={{0,16},{1,17},{2,18},{3,19},{4,20},{5,21},{6,22},{7,23},{8,24},{9,... | collective-permute-start | bytes 196616 | tf_op jit(solution)/shard_map/ppermute | solution.py:18
  57.6 5.5 %collective-permute-start.16 = (f32[64,256]{1,0:T(8,128)S(1)}, f32[64,256]{1,0:T(8,128)S(1)}, u32[]{:S(2)}, u32[]{:S(2)}) collective-permute-start(f32[64,256]{1,0:T(8,128)S(1)} %get-tuple-element.66.part), channel_id=1, source_target_pairs={{0,17},{1,16},{2,19},{3,18},{4,21},{5,20},{6,23},{7,22},{8,25},{9,... | collective-permute-start | bytes 196616 | tf_op jit(solution)/shard_map/ppermute | solution.py:18
  58.7 4.4 %collective-permute-start.15 = (f32[64,256]{1,0:T(8,128)S(1)}, f32[64,256]{1,0:T(8,128)S(1)}, u32[]{:S(2)}, u32[]{:S(2)}) collective-permute-start(f32[64,256]{1,0:T(8,128)S(1)} %get-tuple-element.66.part), channel_id=1, source_target_pairs={{0,1},{1,0},{2,3},{3,2},{4,5},{5,4},{6,7},{7,6},{8,9},{9,8},{10,11... | collective-permute-start | bytes 196616 | tf_op jit(solution)/shard_map/ppermute | solution.py:18
